TPU v7x, 32 devices: a whole 2x2x4 slice. The times are simulated.
32 devices in a mesh: zrow: 4 (over z), zcol: 8 (over y, x, core).
Axes of the slice: x: 2, y: 2, z: 4, core: 2. Of those that a mesh axis runs over, the one named last changes fastest.
Arguments:
- state: float32 [64, 8, 32768], P(None, None, ('zrow', 'zcol')), may hold values from -6 to 6
- kernel: float32 [32768], P(('zrow', 'zcol')), may hold values from 0.5 to 5
- blocks: int32 [2048, 4], replicated, may hold values from 0 to 255
- foot_weight: float32 [2048, 4], replicated, may hold values from 0.2 to 1
- bin_response: float32 [2048, 8], replicated, may hold values from 0.1 to 1
- observed: float32 [2048, 64], replicated, may hold values from -6 to 6
- obs_var: float32 [2048], replicated, may hold values from 0.1 to 1
- batch_order: int32 [2048], replicated, may hold values from 0 to 2047, each once
Outputs:
- analysis: float32 [64, 8, 32768], P(None, None, ('zrow', 'zcol'))
- obs_analysis: float32 [2, 64, 1024], P(None, None, ('zrow', 'zcol'))
All inputs are finite; a program needn't handle non-finite values.
Results may differ from a plain program's by a relative error of at most 0.0003.
Values sent between devices are 32-bit elements; how exact they have to be, the bound alone decides.
No kernel may reach another device: no remote copies, remote signals or barrier semaphores. Data moves between devices by JAX's collectives and lax.ppermute only.
A program may use at most 128 MiB of HBM per device.

v0:
```python
import jax
import jax.numpy as jnp
from jax import lax
from jax.sharding import PartitionSpec as P

BLK = 128
P_SIZE = 1024
BATCHES = 2


def shards(state, kernel, blocks, foot_weight, bin_response, observed, obs_var, batch_order):
    members = state.shape[0]
    nbins = state.shape[1]
    cells = state.shape[2]
    nblocks = cells // BLK
    devices = lax.axis_size(("zrow", "zcol"))
    myself = lax.axis_index(("zrow", "zcol"))
    share = P_SIZE // devices
    high = lax.Precision.HIGHEST
    center = jnp.eye(members, dtype=jnp.float32) - 1.0 / members
    ident = jnp.eye(members, dtype=jnp.float32)

    def batch_ids(batch):
        return batch_order[batch * P_SIZE : (batch + 1) * P_SIZE]

    def observe(means, batch):
        chosen = batch_ids(batch)
        local_blocks = blocks[chosen] - myself * nblocks
        onehot = (
            local_blocks[:, :, None] == jnp.arange(nblocks, dtype=jnp.int32)[None, None, :]
        ).astype(jnp.float32)
        spread = jnp.sum(onehot * foot_weight[chosen][:, :, None], axis=1)
        weights = (bin_response[chosen][:, :, None] * spread[:, None, :]).reshape(
            P_SIZE, nbins * nblocks
        )
        return lax.dot_general(
            means.reshape(members, nbins * nblocks),
            weights,
            (((1,), (1,)), ((), ())),
            precision=high,
        )

    block_weighted = state.reshape(members, nbins, nblocks, BLK) * kernel.reshape(nblocks, BLK)
    means = jnp.sum(block_weighted, axis=3) / BLK
    priors = lax.psum_scatter(
        jnp.stack([observe(means, batch) for batch in range(BATCHES)]),
        ("zrow", "zcol"),
        scatter_dimension=2,
        tiled=True,
    )
    total = ident
    self_sums = []
    obs_sums = []
    for batch in range(BATCHES):
        mine = lax.dynamic_slice_in_dim(batch_ids(batch), myself * share, share, 0)
        weighted = priors[batch] / obs_var[mine][None, :]
        self_sums.append(jnp.dot(weighted, priors[batch].T, precision=high))
        obs_sums.append(jnp.dot(weighted, observed[mine], precision=high))
    self_all, obs_all = lax.psum((jnp.stack(self_sums), jnp.stack(obs_sums)), ("zrow", "zcol"))
    for batch in range(BATCHES):
        left = jnp.dot(center, total, precision=high)
        inner = jnp.dot(jnp.dot(left, self_all[batch], precision=high), left.T, precision=high)
        residue = obs_all[batch] - jnp.dot(self_all[batch], total.T, precision=high)
        cross = jnp.dot(left, residue, precision=high)
        factor = jnp.linalg.cholesky((members - 1) * ident + inner)
        gain = jax.scipy.linalg.cho_solve((factor, True), cross)
        total = jnp.dot(ident + jnp.dot(gain.T, center, precision=high), total, precision=high)
    field = jnp.dot(total, state.reshape(members, -1), precision=high).reshape(
        members, nbins, cells
    )
    finals = jnp.einsum("ij,tjp->tip", total, priors, precision=high)
    return (field, finals)


def solution(mesh):
    return jax.shard_map(
        shards,
        mesh=mesh,
        in_specs=(
            P(None, None, ("zrow", "zcol")),
            P(("zrow", "zcol")),
            P(),
            P(),
            P(),
            P(),
            P(),
            P(),
        ),
        out_specs=(P(None, None, ("zrow", "zcol")), P(None, None, ("zrow", "zcol"))),
        check_vma=False,
    )
```

profile of v0, /device:TPU:1, one launch (start us, length us, event | category | flops | bytes accessed | tf_op | source)
XLA Modules:
  0.0 346.5 jit_solution(2390267959956065888)
XLA Ops:
  7.2 0.7 fusion.50
  7.9 1.1 copy.94
  9.1 4.0 %gather_fusion.4 = s32[1024,4]{1,0:T(8,128)} fusion(s32[2048,4]{1,0:T(8,128)S(1)} %copy.94, s32[1024]{0:T(1024)S(1)} %get-tuple-element.24), kind=kCustom, calls=%fused_computation.4 | custom fusion | bytes 36864 | tf_op jit(solution)/shard_map/gather | solution.py:28
  13.1 4.0 %gather_fusion.1 = s32[1024,4]{1,0:T(8,128)} fusion(s32[2048,4]{1,0:T(8,128)S(1)} %copy.94, s32[1024]{0:T(1024)S(1)} %get-tuple-element.23), kind=kCustom, calls=%fused_computation.1 | custom fusion | bytes 36864 | tf_op jit(solution)/shard_map/gather | solution.py:28
  17.1 0.4 copy.96
  17.4 4.0 %gather_fusion.5 = f32[1024,4]{1,0:T(8,128)} fusion(f32[2048,4]{1,0:T(8,128)S(1)} %copy.96, s32[1024]{0:T(1024)S(1)} %get-tuple-element.24), kind=kCustom, calls=%fused_computation.5 | custom fusion | bytes 36864 | tf_op jit(solution)/shard_map/gather | solution.py:32
  21.5 4.0 %gather_fusion.2 = f32[1024,4]{1,0:T(8,128)} fusion(f32[2048,4]{1,0:T(8,128)S(1)} %copy.96, s32[1024]{0:T(1024)S(1)} %get-tuple-element.23), kind=kCustom, calls=%fused_computation.2 | custom fusion | bytes 36864 | tf_op jit(solution)/shard_map/gather | solution.py:32
  25.4 0.3 copy.92
  25.8 4.0 %gather_fusion.3 = f32[1024,8]{1,0:T(8,128)} fusion(f32[2048,8]{1,0:T(8,128)S(1)} %copy.92, s32[1024]{0:T(1024)S(1)} %get-tuple-element.24), kind=kCustom, calls=%fused_computation.3 | custom fusion | bytes 69632 | tf_op jit(solution)/shard_map/gather | solution.py:33
  29.8 4.0 %gather_fusion = f32[1024,8]{1,0:T(8,128)} fusion(f32[2048,8]{1,0:T(8,128)S(1)} %copy.92, s32[1024]{0:T(1024)S(1)} %get-tuple-element.23), kind=kCustom, calls=%fused_computation | custom fusion | bytes 69632 | tf_op jit(solution)/shard_map/gather | solution.py:33
  33.8 0.6 fusion.3
  34.5 1.2 copy.95
  36.0 1.2 copy.97
  37.4 1.2 copy.93
  38.6 1.2 copy.99
  39.9 0.4 convolution_bitcast_fusion
  40.4 0.4 convolution_bitcast_fusion.1
  40.8 1.3 copy.104
  42.5 0.7 gather_fusion.7
  43.2 0.7 gather_fusion.6
  43.9 1.4 copy.107
  45.2 0.6 gather_fusion.9
  45.8 0.6 gather_fusion.8
  46.6 126.8 %all-reduce.5.cloned.1.call-done = f32[2,64,1024]{1,0,2:T(2,128)} async-done(((f32[2,64,1024]{1,0,2:T(2,128)}), f32[2,64,1024]{1,0,2:T(2,128)}) %all-reduce.5.cloned.1.call-update) | async-done | bytes 524304
  173.4 1.0 broadcast_divide_fusion.1
  174.6 0.3 convolution_bitcast_fusion.5
  175.2 0.3 convolution_bitcast_fusion.4
  175.5 0.6 pad_maximum_fusion.1
  176.1 0.6 pad_maximum_fusion.2
  176.8 0.8 constant_dynamic-slice_fusion.2
  177.6 125.0 %all-reduce.7.cloned.1.call-done = (f32[2,64,64]{2,1,0:T(8,128)}, f32[2,64,64]{2,1,0:T(8,128)}) async-done(((f32[2,64,64]{2,1,0:T(8,128)}, f32[2,64,64]{2,1,0:T(8,128)}), (f32[2,64,64]{2,1,0:T(8,128)}, f32[2,64,64]{2,1,0:T(8,128)})) %all-reduce.7.cloned.1.call-update) | async-done | bytes 65552 | tf_op jit(solution)/shard_map/psum | solution.py:59
  302.6 0.9 convolution_subtract_fusion.1
  303.5 0.9 fusion.28
  304.9 5.8 %cholesky.44 = f32[64,64]{1,0:T(8,128)S(1)} custom-call(f32[64,64]{1,0:T(8,128)S(1)} %fusion.23), custom_call_target="Cholesky" | custom-call | tf_op jit(solution)/shard_map/jit(cholesky)/cholesky | solution.py:65
  310.8 0.6 compare_reduce_fusion.1
  311.4 0.7 fusion.12
  312.1 4.9 %custom-call.8 = f32[1,64,64]{1,2,0:T(8,128)S(1)} custom-call(f32[1,64,64]{2,1,0:T(8,128)S(1)} %fusion.12), custom_call_target="InvertDiagBlocksLowerTriangular" | custom-call | tf_op jit(solution)/shard_map/jit(_cho_solve)/triangular_solve | solution.py:66
  317.0 0.3 fusion.21
  317.8 1.0 convolution_subtract_fusion
  319.0 0.9 fusion.29
  320.4 5.8 %cholesky.55 = f32[64,64]{1,0:T(8,128)S(1)} custom-call(f32[64,64]{1,0:T(8,128)S(1)} %fusion.18), custom_call_target="Cholesky" | custom-call | tf_op jit(solution)/shard_map/jit(cholesky)/cholesky | solution.py:65
  326.3 0.6 compare_reduce_fusion
  326.9 0.7 fusion.13
  327.6 4.9 %custom-call.9 = f32[1,64,64]{1,2,0:T(8,128)S(1)} custom-call(f32[1,64,64]{2,1,0:T(8,128)S(1)} %fusion.13), custom_call_target="InvertDiagBlocksLowerTriangular" | custom-call | tf_op jit(solution)/shard_map/jit(_cho_solve)/triangular_solve | solution.py:66
  332.5 0.3 fusion.16
  333.3 0.8 convolution_bitcast_fusion.2
  334.1 3.0 fusion
  337.2 2.5 copy.115
  (48 shorter events, 4.0 us)
Async XLA Ops:
  7.2 35.3 %copy-start = (f32[2048]{0:T(1024)S(1)}, f32[2048]{0:T(1024)}, u32[]{:S(2)}) copy-start(f32[2048]{0:T(1024)} %param.17) | copy-start | bytes 24580
  7.2 166.2 %all-reduce.5.cloned.1.call-start = ((), (), s32[]{:S(2)}) async-start(), calls=%async_computation | async-start | bytes 2097152
  13.1 4.0 %copy-start.5 = (f32[2048,4]{0,1:T(4,128)S(1)}, f32[2048,4]{0,1:T(4,128)}, u32[]{:S(2)}) copy-start(f32[2048,4]{0,1:T(4,128)} %param.14) | copy-start | bytes 98308
  21.5 4.0 %copy-start.4 = (f32[2048,8]{0,1:T(8,128)S(1)}, f32[2048,8]{0,1:T(8,128)}, u32[]{:S(2)}) copy-start(f32[2048,8]{0,1:T(8,128)} %param.15) | copy-start | bytes 196612
  29.8 4.0 %copy-start.1 = (f32[64,8,1024]{2,1,0:T(8,128)S(1)}, f32[64,8,1024]{2,1,0:T(8,128)}, u32[]{:S(2)}) copy-start(f32[64,8,1024]{2,1,0:T(8,128)} %param.11) | copy-start | bytes 6291460
  29.8 4.0 %copy-start.6 = (f32[1024]{0:T(1024)S(1)}, f32[1024]{0:T(1024)}, u32[]{:S(2)}) copy-start(f32[1024]{0:T(1024)} %param.12) | copy-start | bytes 12292
  33.8 2.0 copy-start.2
  33.8 3.4 copy-start.3
  42.1 260.5 %all-reduce.7.cloned.1.call-start = ((), (), s32[]{:S(2)}) async-start(), calls=%async_computation.1 | async-start | bytes 262144 | tf_op jit(solution)/shard_map/psum | solution.py:59
Sparse Core Ops, SparseCore 0:
  42.2 131.1 all-reduce.4
  180.6 121.8 all-reduce.6
where the time goes:
time: 349 us; the launch traced here: 347 us
  waiting for transfers between devices  252 us (72%)
  local copies, waits for them, and re-layouts  39.9 us (11%)
  other arithmetic  27.9 us (8%)
  between operations  14.4 us (4%)
  matrix products  12.2 us (3%)
    unnamed x3, waiting for transfers between devices  127 us
    psum x1, waiting for transfers between devices, shards(): lax.psum((jnp.stack(self_sums), jnp.stack(obs_sums)), ('zrow', 'zcol'))  125 us
    another operation x6, other arithmetic, shards(): factor = jnp.linalg.cholesky((members - 1) * ident + inner)  13 us
    another operation x4, other arithmetic, shards(): gain = jax.scipy.linalg.cho_solve((factor, True), cross)  11.1 us
    gather x4, local copies, waits for them, and re-layouts, observe(): bin_response[chosen][:, :, None] * spread[:, None, :]  10.4 us
    gather x4, local copies, waits for them, and re-layouts, observe(): spread = jnp.sum(onehot * foot_weight[chosen][:, :, None], axis=1)  9.45 us
    gather x4, local copies, waits for them, and re-layouts, observe(): local_blocks = blocks[chosen] - myself * nblocks  9.42 us
  transfers between devices with their start and end apart: 2, of which 2 were waited for; matrix products, arithmetic and copies ran while one was open for 1% of the time, Pallas kernels for 0%

commit v1 on v0

v1 whole, which is shorter than its diff:
```python
import functools

import jax
import jax.numpy as jnp
from jax import lax
from jax.experimental import pallas as pl
from jax.experimental.pallas import tpu as pltpu
from jax.sharding import PartitionSpec as P

BLK = 128
P_SIZE = 1024
AXES = ("zrow", "zcol")
F32 = jnp.float32
BF16 = jnp.bfloat16
NT = (((1,), (1,)), ((), ()))
VMEM_SPEC = pl.BlockSpec(memory_space=pltpu.VMEM)
LIMIT = 56 * 1024 * 1024


def split(x):
    hi = x.astype(BF16)
    return hi, (x - hi.astype(F32)).astype(BF16)


def mm(a, b):
    return jnp.dot(a, b, precision=lax.Precision.HIGHEST, preferred_element_type=F32)


def means_kernel(x_ref, kernel_ref, out_ref):
    nb, cells = out_ref.shape[0], x_ref.shape[1]
    row = lax.broadcasted_iota(jnp.int32, (nb, cells), 0)
    col = lax.broadcasted_iota(jnp.int32, (nb, cells), 1)
    lo = row * BLK
    picked = jnp.where((col >= lo) & (col < lo + BLK), kernel_ref[...] * (1.0 / BLK), 0.0)
    out_ref[...] = lax.dot_general(
        picked, x_ref[...], NT, precision=lax.Precision.HIGHEST, preferred_element_type=F32
    )


def spread_kernel(bits, nb, me_ref, blocks_ref, weight_ref, out_ref):
    foot, sensors = blocks_ref.shape
    slots = out_ref.shape[1]
    step = 128
    for c in range(0, sensors, step):
        blk = blocks_ref[:, c : c + step]
        away = lax.shift_right_logical(blk, nb.bit_length() - 1) ^ me_ref[0]
        place = blk & (nb - 1)
        for i, bit in enumerate(bits):
            place += (lax.shift_right_logical(away, bit) & 1) * (nb << i)
        weight = weight_ref[:, c : c + step]
        for r in range(0, slots, 256):
            row = lax.broadcasted_iota(jnp.int32, (256, step), 0) + r
            total = jnp.zeros((256, step), F32)
            for f in range(foot):
                total += jnp.where(row == place[f : f + 1, :], weight[f : f + 1, :], 0.0)
            hi, low = split(total)
            out_ref[0, r : r + 256, c : c + step] = hi
            out_ref[1, r : r + 256, c : c + step] = low


def halves_kernel(members, bins, x_ref, hi_ref, lo_ref):
    for b in range(bins):
        hi, low = split(x_ref[:, b, :])
        hi_ref[b] = hi
        lo_ref[b] = low


def sublane_mean(x):
    return jnp.sum(x, axis=0, keepdims=True) * (1.0 / x.shape[0])


def lane_mean(x):
    return jnp.sum(x, axis=1, keepdims=True) * (1.0 / x.shape[1])


def solve(aug):
    n = aug.shape[0]
    width = aug.shape[1]
    rows = [aug[8 * i : 8 * i + 8, :] for i in range(n // 8)]
    sub = lax.broadcasted_iota(jnp.int32, (8, width), 0)

    def lanes(x, j):
        return jnp.broadcast_to(x[:, j : j + 1], (8, width))

    for k in range(n // 8):
        piv = rows[k]
        own = [lanes(piv, 8 * k + q) for q in range(8)]
        for q in range(8):
            here = sub == q
            mult = own[q]
            inv = 1.0 / mult[q : q + 1, :]
            scaled = piv[q : q + 1, :] * inv
            piv = jnp.where(here, scaled, piv - mult * scaled)
            for p in range(q + 1, 8):
                scaled = own[p][q : q + 1, :] * inv
                own[p] = jnp.where(here, scaled, own[p] - mult * scaled)
        for i in range(n // 8):
            if i != k:
                new = rows[i]
                for q in range(8):
                    new = new - lanes(rows[i], 8 * k + q) * piv[q : q + 1, :]
                rows[i] = new
        rows[k] = piv
    return jnp.concatenate(rows, axis=0)[:, n:]


def update_kernel(
    members, bins, gathered_ref, spread_ref, resp_ref, obs_ref, weight_ref, own_ref, xhi_ref, xlo_ref,
    field_ref, finals_ref, turned, left, anom, depart,
):
    slots = gathered_ref.shape[0]
    sensors = resp_ref.shape[1]
    rows = members * bins
    for r in range(0, slots, 128):
        turned[...] = gathered_ref[r : r + 128, :].T
        for b in range(bins):
            hi, low = split(turned[pl.ds(b, members, stride=bins), :])
            left[0, b * members : (b + 1) * members, r : r + 128] = hi
            left[1, b * members : (b + 1) * members, r : r + 128] = low
    step = 256
    for c in range(0, sensors, step):
        z = (
            jnp.dot(left[0], spread_ref[0, :, c : c + step], preferred_element_type=F32)
            + jnp.dot(left[0], spread_ref[1, :, c : c + step], preferred_element_type=F32)
            + jnp.dot(left[1], spread_ref[0, :, c : c + step], preferred_element_type=F32)
        )
        hx = z[0:members, :] * resp_ref[0:1, c : c + step]
        for b in range(1, bins):
            hx += z[b * members : (b + 1) * members, :] * resp_ref[b : b + 1, c : c + step]
        center = sublane_mean(hx)
        anom[0:members, c : c + step] = hx - center
        anom[members : 2 * members, c : c + step] = obs_ref[:, c : c + step] - center
        depart[:, c : c + step] = hx
    ahi, alo = split(anom[...])
    wide = jnp.concatenate(
        [anom[0:members, :] * weight_ref[t : t + 1, :] for t in range(2)], axis=0
    )
    whi, wlo = split(wide)
    sums = (
        lax.dot_general(whi, ahi, NT, preferred_element_type=F32)
        + lax.dot_general(whi, alo, NT, preferred_element_type=F32)
        + lax.dot_general(wlo, ahi, NT, preferred_element_type=F32)
    )
    r64 = lax.broadcasted_iota(jnp.int32, (members, members), 0)
    c64 = lax.broadcasted_iota(jnp.int32, (members, members), 1)
    eye = (r64 == c64).astype(F32)
    s0, e0 = sums[0:members, 0:members], sums[0:members, members:]
    s1, e1 = sums[members:, 0:members], sums[members:, members:]
    gain = solve(jnp.concatenate([s0 + (members - 1.0) * eye, e0 - s0], axis=1))
    first_t = eye + gain - sublane_mean(gain)
    first_ct = first_t - lane_mean(first_t)
    first = first_t.T
    first_c = first - sublane_mean(first)
    prod = mm(s1, jnp.concatenate([first_ct, first_t], axis=1))
    aug = mm(first_c, jnp.concatenate([prod[:, 0:members], e1 - prod[:, members:]], axis=1))
    gain = solve(
        jnp.concatenate([aug[:, 0:members] + (members - 1.0) * eye, aug[:, members:]], axis=1)
    )
    total = first + mm(gain.T, first_c)
    thi, tlo = split(total)
    for b in range(bins):
        out = (
            jnp.dot(thi, xhi_ref[b], preferred_element_type=F32)
            + jnp.dot(thi, xlo_ref[b], preferred_element_type=F32)
            + jnp.dot(tlo, xhi_ref[b], preferred_element_type=F32)
        )
        field_ref[:, b, :] = out
    nown = own_ref.shape[0]
    sensor = lax.broadcasted_iota(jnp.int32, (nown, sensors), 1)
    onehot = (sensor == own_ref[...]).astype(BF16)
    hhi, hlo = split(depart[...])
    hlo2 = (depart[...] - hhi.astype(F32) - hlo.astype(F32)).astype(BF16)
    picked = (
        lax.dot_general(onehot, hhi, NT, preferred_element_type=F32)
        + lax.dot_general(onehot, hlo, NT, preferred_element_type=F32)
        + lax.dot_general(onehot, hlo2, NT, preferred_element_type=F32)
    )
    finals_ref[...] = lax.dot_general(
        picked, total, NT, precision=lax.Precision.HIGHEST, preferred_element_type=F32
    )


def shards(state, kernel, blocks, foot_weight, bin_response, observed, obs_var, batch_order):
    members, bins, cells = state.shape
    nb = cells // BLK
    sensors = obs_var.shape[0]
    batches = sensors // P_SIZE
    nz, nc = lax.axis_size("zrow"), lax.axis_size("zcol")
    devices = nz * nc
    me = lax.axis_index(AXES)
    share = P_SIZE // devices
    zbits = [(nc << i).bit_length() - 1 for i in range(nz.bit_length() - 1)]
    cbits = [i for i in reversed(range(nc.bit_length() - 1))]
    bits = zbits + cbits
    rows = members * bins
    params = pltpu.CompilerParams(vmem_limit_bytes=LIMIT)

    flat = state.reshape(rows, cells)
    piece = pl.pallas_call(
        means_kernel,
        out_shape=jax.ShapeDtypeStruct((nb, rows), F32),
        in_specs=[VMEM_SPEC, VMEM_SPEC],
        out_specs=VMEM_SPEC,
        compiler_params=params,
        name="means",
    )(flat, kernel.reshape(1, cells))
    for bit in bits:
        other = lax.ppermute(piece, AXES, [(i, i ^ (1 << bit)) for i in range(devices)])
        piece = jnp.concatenate([piece, other], axis=0)

    slots = nb * devices
    spread = pl.pallas_call(
        functools.partial(spread_kernel, bits, nb),
        out_shape=jax.ShapeDtypeStruct((2, slots, sensors), BF16),
        in_specs=[pl.BlockSpec(memory_space=pltpu.SMEM), VMEM_SPEC, VMEM_SPEC],
        out_specs=VMEM_SPEC,
        compiler_params=params,
        name="spread",
        cost_estimate=pl.CostEstimate(flops=2000000, bytes_accessed=3000000, transcendentals=0),
    )(me.reshape(1), blocks.T, foot_weight.T)
    xhi, xlo = pl.pallas_call(
        functools.partial(halves_kernel, members, bins),
        out_shape=[jax.ShapeDtypeStruct((bins, members, cells), BF16)] * 2,
        in_specs=[VMEM_SPEC],
        out_specs=[VMEM_SPEC, VMEM_SPEC],
        compiler_params=params,
        name="halves",
        cost_estimate=pl.CostEstimate(flops=2000000, bytes_accessed=4000000, transcendentals=0),
    )(state)
    orders = batch_order.reshape(batches, P_SIZE)
    member_of = jnp.any(
        orders[:, :, None] == jnp.arange(sensors, dtype=jnp.int32)[None, None, :], axis=1
    )
    weight = jnp.where(member_of, 1.0 / obs_var[None, :], 0.0)
    own = lax.dynamic_slice_in_dim(orders, me * share, share, 1).reshape(batches * share, 1)

    field, finals = pl.pallas_call(
        functools.partial(update_kernel, members, bins),
        out_shape=[
            jax.ShapeDtypeStruct((members, bins, cells), F32),
            jax.ShapeDtypeStruct((batches * share, members), F32),
        ],
        in_specs=[VMEM_SPEC] * 8,
        out_specs=[VMEM_SPEC, VMEM_SPEC],
        scratch_shapes=[
            pltpu.VMEM((rows, 128), F32),
            pltpu.VMEM((2, rows, slots), BF16),
            pltpu.VMEM((2 * members, sensors), F32),
            pltpu.VMEM((members, sensors), F32),
        ],
        compiler_params=params,
        name="update",
    )(piece, spread, bin_response.T, observed.T, weight, own, xhi, xlo)
    return (
        field,
        finals.reshape(batches, share, members).transpose(0, 2, 1),
    )


def solution(mesh):
    return jax.shard_map(
        shards,
        mesh=mesh,
        in_specs=(
            P(None, None, AXES),
            P(AXES),
            P(),
            P(),
            P(),
            P(),
            P(),
            P(),
        ),
        out_specs=(P(None, None, AXES), P(None, None, AXES)),
        check_vma=False,
    )
```

time: 349 us -> 55 us (0.16)
  waiting for transfers between devices: 252 us -> 5.01 us
  local copies, waits for them, and re-layouts: 39.9 us -> 2.37 us
  Pallas kernels: 0 us -> 30.8 us
  other arithmetic: 27.9 us -> 4.78 us
  between operations: 14.4 us -> 0.71 us
  matrix products: 12.2 us -> 0 us
  starting transfers between devices: 0.26 us -> 10.6 us
    unnamed x3 -> x0, waiting for transfers between devices: 127 us -> none
    psum x1 -> x0, waiting for transfers between devices: 125 us -> none  [shards(): lax.psum((jnp.stack(self_sums), jnp.stack(obs_sums)), ('zrow', 'zcol'))]
    gather x16 -> x0, local copies, waits for them, and re-layouts: 31.8 us -> none  [the longest x4 10.4 us: observe(): bin_response[chosen][:, :, None] * spread[:, None, :]]
    pallas_call x0 -> x4, Pallas kernels: none -> 30.8 us  [the longest x1 13.7 us: shards(): pl.pallas_call(functools.partial(update_kernel, members, bins), out_shape...]
    another operation x13 -> x0, other arithmetic: 25.4 us -> none  [the longest x6 13 us: shards(): factor = jnp.linalg.cholesky((members - 1) * ident + inner)]
    dot_general x22 -> x0, matrix products: 11.4 us -> none  [the longest x1 3.04 us: shards(): jnp.dot(total, state.reshape(members, -1), precision=high)]
    ppermute x0 -> x5, starting transfers between devices: none -> 10.6 us  [shards(): lax.ppermute(piece, AXES, [(i, i ^ 1 << bit) for i in range(devices)])]
    ppermute x0 -> x5, waiting for transfers between devices: none -> 5.01 us  [shards(): lax.ppermute(piece, AXES, [(i, i ^ 1 << bit) for i in range(devices)])]
  transfers between devices with their start and end apart: 2 -> 5, of which waited for: 2 -> 3; matrix products, arithmetic and copies ran while one was open for 1% -> 10% of each run, Pallas kernels for 0% -> 24%
where the time goes in v1:
time: 55 us; the launch traced here: 54.3 us
  Pallas kernels  30.8 us (56%)
  starting transfers between devices  10.6 us (19%)
  waiting for transfers between devices  5.01 us (9%)
  other arithmetic  4.78 us (9%)
  local copies, waits for them, and re-layouts  2.37 us (4%)
  between operations  0.71 us (1%)
    pallas_call x1, Pallas kernels, shards(): pl.pallas_call(functools.partial(update_kernel, members, bins), out_shape...  13.7 us
    ppermute x5, starting transfers between devices, shards(): lax.ppermute(piece, AXES, [(i, i ^ 1 << bit) for i in range(devices)])  10.6 us
    pallas_call x1, Pallas kernels, shards(): pl.pallas_call(functools.partial(halves_kernel, members, bins), out_shape...  9.56 us
    ppermute x5, waiting for transfers between devices, shards(): lax.ppermute(piece, AXES, [(i, i ^ 1 << bit) for i in range(devices)])  5.01 us
    pallas_call x1, Pallas kernels, shards(): pl.pallas_call(means_kernel, out_shape=jax.ShapeDtypeStruct((nb, rows), F...  3.95 us
    pallas_call x1, Pallas kernels, shards(): pl.pallas_call(functools.partial(spread_kernel, bits, nb), out_shape=jax....  3.56 us
    reduce_or x1, other arithmetic, shards(): jnp.any(orders[:, :, None] == jnp.arange(sensors, dtype=jnp.int32)[None,...  3.43 us
    unnamed x12, local copies, waits for them, and re-layouts  1.54 us
  transfers between devices with their start and end apart: 5, of which 3 were waited for; matrix products, arithmetic and copies ran while one was open for 10% of the time, Pallas kernels for 24%

profile of v1, /device:TPU:1, one launch (start us, length us, event | category | flops | bytes accessed | tf_op | source)
XLA Modules:
  0.0 54.3 jit_solution(512963270173900487)
XLA Ops:
  0.6 0.0 copy-start.2
  0.6 0.0 copy-start.3
  0.7 4.0 %means.1 = f32[8,512]{1,0:T(8,128)} custom-call(f32[512,1024]{1,0:T(8,128)} %bitcast.10, f32[1,1024]{1,0:T(1,128)} %bitcast.15), custom_call_target="tpu_custom_call" | custom-call | tf_op jit(solution)/shard_map/means/pallas_call | solution.py:199
  4.6 2.1 %collective-permute-start = (f32[8,512]{1,0:T(8,128)}, f32[8,512]{1,0:T(8,128)S(1)}, u32[]{:S(2)}, u32[]{:S(2)}) collective-permute-start(f32[8,512]{1,0:T(8,128)} %means.1), channel_id=1, source_target_pairs={{0,8},{1,9},{2,10},{3,11},{4,12},{5,13},{6,14},{7,15},{8,0},{9,1},... | collective-permute-start | bytes 49160 | tf_op jit(solution)/shard_map/ppermute | solution.py:208
  6.7 0.0 copy-done.2
  6.7 3.4 %fusion = pred[2,2048]{1,0:T(4,128)(4,1)S(1)} fusion(s32[2,1024]{1,0:T(2,128)S(1)} %eq.15), kind=kLoop, calls=%fused_computation.1 | loop fusion | flops 8384512 | bytes 12288 | tf_op jit(solution)/shard_map/reduce_or | solution.py:231
  10.2 0.0 copy-done.3
  10.2 0.7 %constant_dynamic-update-slice_fusion.4 = (f32[128,512]{1,0:T(8,128)S(1)}, f32[256,512]{1,0:T(8,128)S(1)}) fusion(f32[8,512]{1,0:T(8,128)} %means.1), kind=kLoop, calls=%fused_computation.9 | loop fusion | bytes 49152
  10.9 0.0 collective-permute-done
  10.9 0.7 %pad_maximum_fusion.2 = f32[16,512]{1,0:T(8,128)S(1)} fusion(f32[8,512]{1,0:T(8,128)S(1)} %collective-permute-done, f32[8,512]{1,0:T(8,128)} %means.1), kind=kLoop, calls=%fused_computation.4 | loop fusion | flops 8192 | bytes 65536 | tf_op jit(solution)/shard_map/concatenate | solution.py:209
  11.7 2.3 %collective-permute-start.1 = (f32[16,512]{1,0:T(8,128)S(1)}, f32[16,512]{1,0:T(8,128)S(1)}, u32[]{:S(2)}, u32[]{:S(2)}) collective-permute-start(f32[16,512]{1,0:T(8,128)S(1)} %pad_maximum_fusion.2), channel_id=1, source_target_pairs={{0,16},{1,17},{2,18},{3,19},{4,20},{5,21},{6,22},{7,23},{8,24},{9,... | collective-permute-start | bytes 98312 | tf_op jit(solution)/shard_map/ppermute | solution.py:208
  14.0 0.1 constant_dynamic-slice_fusion
  14.0 0.7 %reshape.28.own_ref = s32[64,1]{1,0:T(8,128)} reshape(s32[2,32]{1,0:T(2,128)S(1)} %constant_dynamic-slice_fusion) | data formatting | bytes 512 | tf_op jit(solution)/shard_map/reshape | solution.py:235
  14.7 0.0 copy-start.1
  14.7 9.6 %halves.1 = (bf16[8,64,1024]{2,1,0:T(8,128)(2,1)}, bf16[8,64,1024]{2,1,0:T(8,128)(2,1)}) custom-call(f32[64,8,1024]{2,1,0:T(8,128)} %x_ref.1), custom_call_target="tpu_custom_call" | custom-call | flops 2000000 | bytes 4000000 | tf_op jit(solution)/shard_map/halves/pallas_call | solution.py:221
  24.3 3.6 %spread.1.spread_ref = bf16[2,256,2048]{2,1,0:T(8,128)(2,1)} custom-call(s32[1]{0:T(128)} %bitcast.2.me_ref, s32[4,2048]{1,0:T(4,128)} %bitcast.13, f32[4,2048]{1,0:T(4,128)} %bitcast.14), custom_call_target="tpu_custom_call" | custom-call | flops 2000000 | bytes 3000000 | tf_op jit(solution)/shard_map/spread/pallas_call | solution.py:212
  27.9 0.0 collective-permute-done.1
  27.9 0.0 copy-done.1
  27.9 1.3 %collective-permute-start.2 = (f32[32,512]{1,0:T(8,128)S(1)}, f32[32,512]{1,0:T(8,128)S(1)}, u32[]{:S(2)}, u32[]{:S(2)}) collective-permute-start(f32[32,512]{1,0:T(8,128)S(1)} %pad_maximum_fusion.1), channel_id=1, source_target_pairs={{0,4},{1,5},{2,6},{3,7},{4,0},{5,1},{6,2},{7,3},{8,12},{9,13},{10,... | collective-permute-start | bytes 196616 | tf_op jit(solution)/shard_map/ppermute | solution.py:208
  29.2 1.9 %collective-permute-done.2 = f32[32,512]{1,0:T(8,128)S(1)} collective-permute-done((f32[32,512]{1,0:T(8,128)S(1)}, f32[32,512]{1,0:T(8,128)S(1)}, u32[]{:S(2)}, u32[]{:S(2)}) %collective-permute-start.2) | collective-permute-done | bytes 65568 | tf_op jit(solution)/shard_map/ppermute | solution.py:208
  31.1 1.3 %collective-permute-start.3 = (f32[64,512]{1,0:T(8,128)S(1)}, f32[64,512]{1,0:T(8,128)S(1)}, u32[]{:S(2)}, u32[]{:S(2)}) collective-permute-start(f32[64,512]{1,0:T(8,128)S(1)} %pad_maximum_fusion), channel_id=1, source_target_pairs={{0,2},{1,3},{2,0},{3,1},{4,6},{5,7},{6,4},{7,5},{8,10},{9,11},{10,... | collective-permute-start | bytes 393224 | tf_op jit(solution)/shard_map/ppermute | solution.py:208
  32.4 2.6 %collective-permute-done.3 = f32[64,512]{1,0:T(8,128)S(1)} collective-permute-done((f32[64,512]{1,0:T(8,128)S(1)}, f32[64,512]{1,0:T(8,128)S(1)}, u32[]{:S(2)}, u32[]{:S(2)}) %collective-permute-start.3) | collective-permute-done | bytes 131104 | tf_op jit(solution)/shard_map/ppermute | solution.py:208
  35.0 3.6 %collective-permute-start.4 = (f32[128,512]{1,0:T(8,128)S(1)}, f32[128,512]{1,0:T(8,128)S(1)}, u32[]{:S(2)}, u32[]{:S(2)}) collective-permute-start(f32[128,512]{1,0:T(8,128)S(1)} %get-tuple-element.10), channel_id=1, source_target_pairs={{0,1},{1,0},{2,3},{3,2},{4,5},{5,4},{6,7},{7,6},{8,9},{9,8},{10,11... | collective-permute-start | bytes 786440 | tf_op jit(solution)/shard_map/ppermute | solution.py:208
  38.6 0.6 %broadcast_select_fusion.weight_ref = f32[2,2048]{1,0:T(2,128)} fusion(pred[2,2048]{1,0:T(4,128)(4,1)S(1)} %fusion, f32[2048]{0:T(1024)S(1)} %broadcast_divide_fusion), kind=kLoop, calls=%fused_computation.16 | loop fusion | flops 4096 | bytes 28672 | tf_op jit(solution)/shard_map/jit(_where)/select_n | solution.py:234
  39.2 0.5 %collective-permute-done.4 = f32[128,512]{1,0:T(8,128)S(1)} collective-permute-done((f32[128,512]{1,0:T(8,128)S(1)}, f32[128,512]{1,0:T(8,128)S(1)}, u32[]{:S(2)}, u32[]{:S(2)}) %collective-permute-start.4) | collective-permute-done | bytes 262176 | tf_op jit(solution)/shard_map/ppermute | solution.py:208
  39.8 0.0 copy-start
  39.8 0.8 %copy-done = f32[256,512]{1,0:T(8,128)} copy-done((f32[256,512]{1,0:T(8,128)}, f32[256,512]{1,0:T(8,128)S(1)}, u32[]{:S(2)}) %copy-start) | copy-done | bytes 524312
  40.6 13.7 %update.1 = (f32[64,8,1024]{2,1,0:T(8,128)}, f32[64,64]{1,0:T(8,128)}) custom-call(f32[256,512]{1,0:T(8,128)} %copy-done, bf16[2,256,2048]{2,1,0:T(8,128)(2,1)} %spread.1.spread_ref, f32[8,2048]{1,0:T(8,128)} %bitcast.12, f32[64,2048]{1,0:T(8,128)} %bitcast.11, f32[2,2048]{1,0:T(2,128)} %broadcast_select_fusion.weight_ref, s32[64,1]{1,0:T(8,128)} %reshape.28.own_ref, ...), custom_call_target="tpu_custom_call" | custom-call | tf_op jit(solution)/shard_map/update/pallas_call | solution.py:237
  (9 shorter events, 0.1 us)
Async XLA Ops:
  0.6 6.1 %copy-start.2 = (s32[2048]{0:T(1024)S(1)}, s32[2048]{0:T(1024)}, u32[]{:S(2)}) copy-start(s32[2048]{0:T(1024)} %param.15) | copy-start | bytes 24580
  0.6 9.5 %copy-start.3 = (f32[2048]{0:T(1024)S(1)}, f32[2048]{0:T(1024)}, u32[]{:S(2)}) copy-start(f32[2048]{0:T(1024)} %param.14) | copy-start | bytes 24580
  4.6 6.3 %collective-permute-start = (f32[8,512]{1,0:T(8,128)}, f32[8,512]{1,0:T(8,128)S(1)}, u32[]{:S(2)}, u32[]{:S(2)}) collective-permute-start(f32[8,512]{1,0:T(8,128)} %means.1), channel_id=1, source_target_pairs={{0,8},{1,9},{2,10},{3,11},{4,12},{5,13},{6,14},{7,15},{8,0},{9,1},... | collective-permute-start | bytes 49160 | tf_op jit(solution)/shard_map/ppermute | solution.py:208
  11.7 16.2 %collective-permute-start.1 = (f32[16,512]{1,0:T(8,128)S(1)}, f32[16,512]{1,0:T(8,128)S(1)}, u32[]{:S(2)}, u32[]{:S(2)}) collective-permute-start(f32[16,512]{1,0:T(8,128)S(1)} %pad_maximum_fusion.2), channel_id=1, source_target_pairs={{0,16},{1,17},{2,18},{3,19},{4,20},{5,21},{6,22},{7,23},{8,24},{9,... | collective-permute-start | bytes 98312 | tf_op jit(solution)/shard_map/ppermute | solution.py:208
  14.7 13.1 %copy-start.1 = (f32[8,512]{1,0:T(8,128)S(1)}, f32[8,512]{1,0:T(8,128)}, u32[]{:S(2)}) copy-start(f32[8,512]{1,0:T(8,128)} %means.1) | copy-start | bytes 49156
  27.9 3.2 %collective-permute-start.2 = (f32[32,512]{1,0:T(8,128)S(1)}, f32[32,512]{1,0:T(8,128)S(1)}, u32[]{:S(2)}, u32[]{:S(2)}) collective-permute-start(f32[32,512]{1,0:T(8,128)S(1)} %pad_maximum_fusion.1), channel_id=1, source_target_pairs={{0,4},{1,5},{2,6},{3,7},{4,0},{5,1},{6,2},{7,3},{8,12},{9,13},{10,... | collective-permute-start | bytes 196616 | tf_op jit(solution)/shard_map/ppermute | solution.py:208
  31.1 3.9 %collective-permute-start.3 = (f32[64,512]{1,0:T(8,128)S(1)}, f32[64,512]{1,0:T(8,128)S(1)}, u32[]{:S(2)}, u32[]{:S(2)}) collective-permute-start(f32[64,512]{1,0:T(8,128)S(1)} %pad_maximum_fusion), channel_id=1, source_target_pairs={{0,2},{1,3},{2,0},{3,1},{4,6},{5,7},{6,4},{7,5},{8,10},{9,11},{10,... | collective-permute-start | bytes 393224 | tf_op jit(solution)/shard_map/ppermute | solution.py:208
  35.0 4.8 %collective-permute-start.4 = (f32[128,512]{1,0:T(8,128)S(1)}, f32[128,512]{1,0:T(8,128)S(1)}, u32[]{:S(2)}, u32[]{:S(2)}) collective-permute-start(f32[128,512]{1,0:T(8,128)S(1)} %get-tuple-element.10), channel_id=1, source_target_pairs={{0,1},{1,0},{2,3},{3,2},{4,5},{5,4},{6,7},{7,6},{8,9},{9,8},{10,11... | collective-permute-start | bytes 786440 | tf_op jit(solution)/shard_map/ppermute | solution.py:208
  39.8 0.8 %copy-start = (f32[256,512]{1,0:T(8,128)}, f32[256,512]{1,0:T(8,128)S(1)}, u32[]{:S(2)}) copy-start(f32[256,512]{1,0:T(8,128)S(1)} %constant_dynamic-update-slice_fusion.5.gathered_ref) | copy-start | bytes 1572868

commit v2 on v1

v2 whole, which is shorter than its diff:
```python
import functools

import jax
import jax.numpy as jnp
from jax import lax
from jax.experimental import pallas as pl
from jax.experimental.pallas import tpu as pltpu
from jax.sharding import PartitionSpec as P

BLK = 128
P_SIZE = 1024
AXES = ("zrow", "zcol")
F32 = jnp.float32
BF16 = jnp.bfloat16
NT = (((1,), (1,)), ((), ()))
VMEM_SPEC = pl.BlockSpec(memory_space=pltpu.VMEM)
HBM_SPEC = pl.BlockSpec(memory_space=pltpu.HBM)
SMEM_SPEC = pl.BlockSpec(memory_space=pltpu.SMEM)
MIB = 1024 * 1024


def split(x):
    hi = x.astype(BF16)
    return hi, (x - hi.astype(F32)).astype(BF16)


def mm(a, b):
    return jnp.dot(a, b, precision=lax.Precision.HIGHEST, preferred_element_type=F32)


def sublane_mean(x):
    return jnp.sum(x, axis=0, keepdims=True) * (1.0 / x.shape[0])


def lane_mean(x):
    return jnp.sum(x, axis=1, keepdims=True) * (1.0 / x.shape[1])


def means_kernel(x_ref, kernel_ref, out_ref, held_ref, sems):
    members, bins, _ = x_ref.shape
    nb = out_ref.shape[0]
    copies = []
    for b in range(bins):
        copies.append(pltpu.make_async_copy(x_ref.at[:, b, :], held_ref.at[b], sems.at[b]))
        copies[-1].start()
    scale = kernel_ref[...] * (1.0 / BLK)
    lane = lax.broadcasted_iota(jnp.int32, (2 * members, 128), 1)
    for b in range(0, bins, 2):
        copies[b].wait()
        copies[b + 1].wait()
        total = jnp.zeros((2 * members, 128), F32)
        for j in range(nb):
            cut = slice(j * BLK, (j + 1) * BLK)
            x = jnp.concatenate([held_ref[b, :, cut], held_ref[b + 1, :, cut]], axis=0)
            summed = jnp.sum(x * scale[:, cut], axis=1, keepdims=True)
            total = jnp.where(lane == j, summed, total)
        out_ref[:, b * members : (b + 2) * members] = total.T[0:nb, :]


def spread_kernel(bits, nb, first, me_ref, blocks_ref, weight_ref, out_ref):
    foot, sensors = blocks_ref.shape
    half = out_ref.shape[0] // 3
    step = 128
    for c in range(0, sensors, step):
        blk = blocks_ref[:, c : c + step]
        away = lax.shift_right_logical(blk, nb.bit_length() - 1) ^ me_ref[0]
        place = blk & (nb - 1)
        for i, bit in enumerate(bits):
            place += (lax.shift_right_logical(away, bit) & 1) * (nb << i)
        weight = weight_ref[:, c : c + step]
        for r in range(0, half, 128):
            row = lax.broadcasted_iota(jnp.int32, (128, step), 0) + (r + first)
            total = jnp.where(row == place[0:1, :], weight[0:1, :], 0.0)
            for f in range(1, foot):
                total += jnp.where(row == place[f : f + 1, :], weight[f : f + 1, :], 0.0)
            hi, low = split(total)
            out_ref[r : r + 128, c : c + step] = hi
            out_ref[half + r : half + r + 128, c : c + step] = low
            out_ref[2 * half + r : 2 * half + r + 128, c : c + step] = hi


def halves_kernel(x_ref, out_ref, held_ref, sems):
    members, bins, _ = x_ref.shape
    copies = []
    for b in range(bins):
        copies.append(pltpu.make_async_copy(x_ref.at[:, b, :], held_ref.at[b], sems.at[b]))
        copies[-1].start()
    for b in range(bins):
        copies[b].wait()
        hi, low = split(held_ref[b])
        out_ref[b, 0:members, :] = hi
        out_ref[b, members : 2 * members, :] = low
        out_ref[b, 2 * members : 3 * members, :] = hi


def roles_kernel(orders_ref, own_ref, var_ref, weight_ref, pick_ref):
    batches, per = orders_ref.shape
    groups = var_ref.shape[0]
    inverse = 1.0 / var_ref[...]
    high = lax.broadcasted_iota(jnp.int32, (groups, per), 0)
    low = lax.broadcasted_iota(jnp.int32, (128, per), 0)
    for t in range(batches):
        order = orders_ref[t : t + 1, :]
        of_high = jnp.where(high == lax.shift_right_logical(order, 7), 1.0, 0.0).astype(BF16)
        of_low = jnp.where(low == (order & 127), 1.0, 0.0).astype(BF16)
        held = lax.dot_general(of_high, of_low, NT, preferred_element_type=F32) * inverse
        for g in range(groups):
            weight_ref[t : t + 1, g * 128 : (g + 1) * 128] = held[g : g + 1, :]
    sensors, nown = pick_ref.shape
    sensor = lax.broadcasted_iota(jnp.int32, (sensors, nown), 0)
    pick_ref[...] = jnp.where(sensor == own_ref[...], 1.0, 0.0).astype(BF16)


def turn(gathered_ref, left):
    half = gathered_ref.shape[0]
    for r in range(0, half, 128):
        hi, low = split(gathered_ref[r : r + 128, :].T)
        left[:, r : r + 128] = hi
        left[:, half + r : half + r + 128] = hi
        left[:, 2 * half + r : 2 * half + r + 128] = low


def observe(members, bins, left, spread_ref, resp_ref, cut):
    z = jnp.dot(left[...], spread_ref[:, cut], preferred_element_type=F32)
    hx = z[0:members, :] * resp_ref[0:1, cut]
    for b in range(1, bins):
        hx += z[b * members : (b + 1) * members, :] * resp_ref[b : b + 1, cut]
    return hx


def partial_kernel(members, bins, gathered_ref, spread_ref, resp_ref, hx_ref, left):
    turn(gathered_ref, left)
    step = 256
    for c in range(0, resp_ref.shape[1], step):
        cut = slice(c, c + step)
        hx_ref[:, cut] = observe(members, bins, left, spread_ref, resp_ref, cut)


def solve(aug):
    n = aug.shape[0]
    width = aug.shape[1]
    rows = [aug[8 * i : 8 * i + 8, :] for i in range(n // 8)]
    sub = lax.broadcasted_iota(jnp.int32, (8, width), 0)

    def lanes(x, j):
        return jnp.broadcast_to(x[:, j : j + 1], (8, width))

    for k in range(n // 8):
        piv = rows[k]
        own = [lanes(piv, 8 * k + q) for q in range(8)]
        for q in range(8):
            here = sub == q
            mult = own[q]
            inv = 1.0 / mult[q : q + 1, :]
            scaled = piv[q : q + 1, :] * inv
            piv = jnp.where(here, scaled, piv - mult * scaled)
            for p in range(q + 1, 8):
                scaled = own[p][q : q + 1, :] * inv
                own[p] = jnp.where(here, scaled, own[p] - mult * scaled)
        for i in range(n // 8):
            if i != k:
                new = rows[i]
                for q in range(8):
                    new = new - lanes(rows[i], 8 * k + q) * piv[q : q + 1, :]
                rows[i] = new
        rows[k] = piv
    return jnp.concatenate(rows, axis=0)[:, n:]


def update_kernel(
    members, bins, hx_ref, gathered_ref, spread_ref, resp_ref, obs_ref, weight_ref, pick_ref, x_ref,
    field_ref, finals_ref, left, out, sems,
):
    sensors = resp_ref.shape[1]
    turn(gathered_ref, left)
    step = 256
    sums = jnp.zeros((2 * members, 2 * members), F32)
    picked = jnp.zeros((2 * members, pick_ref.shape[1]), F32)
    for c in range(0, sensors, step):
        cut = slice(c, c + step)
        hx = hx_ref[:, cut] + observe(members, bins, left, spread_ref, resp_ref, cut)
        center = sublane_mean(hx)
        anom = hx - center
        right = jnp.concatenate([anom, obs_ref[:, cut] - center], axis=0)
        wide = jnp.concatenate([anom * weight_ref[t : t + 1, cut] for t in range(2)], axis=0)
        rhi, rlo = split(right)
        whi, wlo = split(wide)
        sums += lax.dot_general(
            jnp.concatenate([whi, whi, wlo], axis=1),
            jnp.concatenate([rhi, rlo, rhi], axis=1),
            NT,
            preferred_element_type=F32,
        )
        hhi, hlo = split(hx)
        picked += jnp.dot(
            jnp.concatenate([hhi, hlo], axis=0), pick_ref[cut, :], preferred_element_type=F32
        )
    picked = picked[0:members] + picked[members:]
    r64 = lax.broadcasted_iota(jnp.int32, (members, members), 0)
    c64 = lax.broadcasted_iota(jnp.int32, (members, members), 1)
    eye = (r64 == c64).astype(F32)
    s0, e0 = sums[0:members, 0:members], sums[0:members, members:]
    s1, e1 = sums[members:, 0:members], sums[members:, members:]
    gain = solve(jnp.concatenate([s0 + (members - 1.0) * eye, e0 - s0], axis=1))
    first_t = eye + gain - sublane_mean(gain)
    first_ct = first_t - lane_mean(first_t)
    first = first_t.T
    first_c = first - sublane_mean(first)
    prod = mm(s1, jnp.concatenate([first_ct, first_t], axis=1))
    aug = mm(first_c, jnp.concatenate([prod[:, 0:members], e1 - prod[:, members:]], axis=1))
    gain = solve(
        jnp.concatenate([aug[:, 0:members] + (members - 1.0) * eye, aug[:, members:]], axis=1)
    )
    total = first + mm(gain.T, first_c)
    thi, tlo = split(total)
    both = jnp.concatenate([thi, thi, tlo], axis=1)
    copies = []
    for b in range(bins):
        out[b] = jnp.dot(both, x_ref[b], preferred_element_type=F32)
        copies.append(pltpu.make_async_copy(out.at[b], field_ref.at[:, b, :], sems.at[b]))
        copies[-1].start()
    finals_ref[...] = mm(total, picked).T
    for copy in copies:
        copy.wait()


def shards(state, kernel, blocks, foot_weight, bin_response, observed, obs_var, batch_order):
    members, bins, cells = state.shape
    nb = cells // BLK
    sensors = obs_var.shape[0]
    batches = sensors // P_SIZE
    nz, nc = lax.axis_size("zrow"), lax.axis_size("zcol")
    devices = nz * nc
    me = lax.axis_index(AXES)
    share = P_SIZE // devices
    zbits = [(nc << i).bit_length() - 1 for i in range(nz.bit_length() - 1)]
    cbits = [i for i in reversed(range(nc.bit_length() - 1))]
    bits = zbits + cbits
    rows = members * bins
    half = nb * devices // 2
    wide = 6 * half * sensors
    small = pltpu.CompilerParams(vmem_limit_bytes=8 * MIB + wide)
    large = pltpu.CompilerParams(vmem_limit_bytes=12 * MIB + 2 * wide)

    def cost(us):
        return pl.CostEstimate(flops=0, bytes_accessed=int(us * 3000000), transcendentals=0)

    def spread_of(first, who, places, weights):
        return pl.pallas_call(
            functools.partial(spread_kernel, bits, nb, first),
            out_shape=jax.ShapeDtypeStruct((3 * half, sensors), BF16),
            in_specs=[SMEM_SPEC, VMEM_SPEC, VMEM_SPEC],
            out_specs=VMEM_SPEC,
            compiler_params=small,
            name="spread",
            cost_estimate=cost(1.0),
        )(who, places, weights)

    def exchange(value, bit):
        return lax.ppermute(value, AXES, [(i, i ^ (1 << bit)) for i in range(devices)])

    far_state = pltpu.with_memory_space_constraint(state, pltpu.HBM)
    staging = [pltpu.VMEM((bins, members, cells), F32), pltpu.SemaphoreType.DMA((bins,))]
    piece = pl.pallas_call(
        means_kernel,
        out_shape=jax.ShapeDtypeStruct((nb, rows), F32),
        in_specs=[HBM_SPEC, VMEM_SPEC],
        out_specs=VMEM_SPEC,
        scratch_shapes=staging,
        compiler_params=small,
        name="means",
    )(far_state, kernel.reshape(1, cells))

    who, places, weights = me.reshape(1), blocks.T, foot_weight.T
    orders = batch_order.reshape(batches, P_SIZE)
    own = lax.dynamic_slice_in_dim(orders, me * share, share, 1).reshape(1, batches * share)
    inverse = obs_var.reshape(sensors // 128, 128)

    def roles_of(orders, own, inverse):
        return pl.pallas_call(
            roles_kernel,
            out_shape=[
                jax.ShapeDtypeStruct((batches, sensors), F32),
                jax.ShapeDtypeStruct((sensors, batches * share), BF16),
            ],
            in_specs=[VMEM_SPEC] * 3,
            out_specs=[VMEM_SPEC] * 2,
            compiler_params=small,
            name="roles",
            cost_estimate=cost(0.6),
        )(orders, own, inverse)

    def halves_of(far_state):
        return pl.pallas_call(
            halves_kernel,
            out_shape=jax.ShapeDtypeStruct((bins, 3 * members, cells), BF16),
            in_specs=[HBM_SPEC],
            out_specs=VMEM_SPEC,
            scratch_shapes=staging,
            compiler_params=small,
            name="halves",
            cost_estimate=cost(1.5),
        )(pltpu.with_memory_space_constraint(far_state, pltpu.HBM))

    beside = [
        (functools.partial(spread_of, 0), (who, places, weights)),
        (functools.partial(spread_of, half), (who, places, weights)),
        (roles_of, (orders, own, inverse)),
        (halves_of, (state,)),
    ]
    made = []
    for i, bit in enumerate(bits[:-1]):
        if i < len(beside):
            work, needs = beside[i]
            piece, needs = lax.optimization_barrier((piece, needs))
            other = exchange(piece, bit)
            result = work(*needs)
            other, result = lax.optimization_barrier((other, result))
            made.append(result)
        else:
            other = exchange(piece, bit)
        piece = jnp.concatenate([piece, other], axis=0)
    spread_near, spread_far, (weight, pick), parts = made
    other = exchange(piece, bits[-1])

    left = pltpu.VMEM((rows, 3 * half), BF16)
    resp = bin_response.T
    hx = pl.pallas_call(
        functools.partial(partial_kernel, members, bins),
        out_shape=jax.ShapeDtypeStruct((members, sensors), F32),
        in_specs=[VMEM_SPEC] * 3,
        out_specs=VMEM_SPEC,
        scratch_shapes=[left],
        compiler_params=large,
        name="partial",
        cost_estimate=cost(1.2),
    )(piece, spread_near, resp)

    field, finals = pl.pallas_call(
        functools.partial(update_kernel, members, bins),
        out_shape=[
            jax.ShapeDtypeStruct((members, bins, cells), F32),
            jax.ShapeDtypeStruct((batches * share, members), F32),
        ],
        in_specs=[VMEM_SPEC] * 8,
        out_specs=[HBM_SPEC, VMEM_SPEC],
        scratch_shapes=[
            left,
            pltpu.VMEM((bins, members, cells), F32),
            pltpu.SemaphoreType.DMA((bins,)),
        ],
        compiler_params=large,
        name="update",
    )(hx, other, spread_far, resp, observed.T, weight, pick, parts)
    return (field, finals.reshape(batches, share, members).transpose(0, 2, 1))


def solution(mesh):
    return jax.shard_map(
        shards,
        mesh=mesh,
        in_specs=(
            P(None, None, AXES),
            P(AXES),
            P(),
            P(),
            P(),
            P(),
            P(),
            P(),
        ),
        out_specs=(P(None, None, AXES), P(None, None, AXES)),
        check_vma=False,
    )
```

time: 55 us -> 36.3 us (0.66)
  Pallas kernels: 30.8 us -> 18.9 us
  other arithmetic: 4.78 us -> 0.02 us
  waiting for transfers between devices: 5.01 us -> 2.98 us
  starting transfers between devices: 10.6 us -> 12.3 us
  local copies, waits for them, and re-layouts: 2.37 us -> 0.9 us
    pallas_call x2 -> x5, Pallas kernels: 13.1 us -> 4.89 us  [the longest x1 1.77 us: halves_of(): pl.pallas_call(halves_kernel, out_shape=jax.ShapeDtypeStruct((bins, 3 * m...]
    reduce_or x1 -> x0, other arithmetic: 3.43 us -> none  [shards(): jnp.any(orders[:, :, None] == jnp.arange(sensors, dtype=jnp.int32)[None,...]
    ppermute x5, waiting for transfers between devices: 5.01 us -> 2.98 us  [exchange(): lax.ppermute(value, AXES, [(i, i ^ 1 << bit) for i in range(devices)])]
    pallas_call x1, Pallas kernels: 13.7 us -> 11.8 us  [shards(): pl.pallas_call(functools.partial(update_kernel, members, bins), out_shape...]
    pallas_call x1, Pallas kernels: 3.95 us -> 2.16 us  [shards(): pl.pallas_call(means_kernel, out_shape=jax.ShapeDtypeStruct((nb, rows), F...]
    ppermute x5, starting transfers between devices: 10.6 us -> 12.3 us  [exchange(): lax.ppermute(value, AXES, [(i, i ^ 1 << bit) for i in range(devices)])]
    unnamed x12 -> x15, local copies, waits for them, and re-layouts: 1.54 us -> 0.73 us
    concatenate x3, other arithmetic: 0.74 us -> 0.02 us  [shards(): piece = jnp.concatenate([piece, other], axis=0)]
  transfers between devices with their start and end apart: 5 -> 5, of which waited for: 3 -> 4; matrix products, arithmetic and copies ran while one was open for 10% -> 0% of each run, Pallas kernels for 24% -> 14%
where the time goes in v2:
time: 36.3 us; the launch traced here: 35.9 us
  Pallas kernels  18.9 us (52%)
  starting transfers between devices  12.3 us (34%)
  waiting for transfers between devices  2.98 us (8%)
  local copies, waits for them, and re-layouts  0.9 us (2%)
  between operations  0.79 us (2%)
    ppermute x5, starting transfers between devices, exchange(): lax.ppermute(value, AXES, [(i, i ^ 1 << bit) for i in range(devices)])  12.3 us
    pallas_call x1, Pallas kernels, shards(): pl.pallas_call(functools.partial(update_kernel, members, bins), out_shape...  11.8 us
    ppermute x5, waiting for transfers between devices, exchange(): lax.ppermute(value, AXES, [(i, i ^ 1 << bit) for i in range(devices)])  2.98 us
    pallas_call x1, Pallas kernels, shards(): pl.pallas_call(means_kernel, out_shape=jax.ShapeDtypeStruct((nb, rows), F...  2.16 us
    pallas_call x1, Pallas kernels, halves_of(): pl.pallas_call(halves_kernel, out_shape=jax.ShapeDtypeStruct((bins, 3 * m...  1.77 us
    pallas_call x1, Pallas kernels, shards(): pl.pallas_call(functools.partial(partial_kernel, members, bins), out_shap...  1.31 us
    pallas_call x2, Pallas kernels, spread_of(): pl.pallas_call(functools.partial(spread_kernel, bits, nb, first), out_sha...  1.3 us
    unnamed x15, local copies, waits for them, and re-layouts  0.73 us
  transfers between devices with their start and end apart: 5, of which 4 were waited for; matrix products, arithmetic and copies ran while one was open for 0% of the time, Pallas kernels for 14%

profile of v2, /device:TPU:1, one launch (start us, length us, event | category | flops | bytes accessed | tf_op | source)
XLA Modules:
  0.0 35.9 jit_solution(14329909115157391640)
XLA Ops:
  0.6 0.0 copy-start.3
  0.6 0.0 copy-start.2
  0.7 0.0 copy-start.5
  0.7 0.7 %copy-done.5 = f32[1024]{0:T(1024)S(1)} copy-done((f32[1024]{0:T(1024)S(1)}, f32[1024]{0:T(1024)}, u32[]{:S(2)}) %copy-start.5) | copy-done | bytes 4120
  1.4 0.0 copy-start.6
  1.4 2.2 %means.1 = f32[8,512]{1,0:T(8,128)S(1)} custom-call(f32[64,8,1024]{2,1,0:T(8,128)} %x_ref.2, f32[1,1024]{1,0:T(1,128)S(1)} %bitcast.18), custom_call_target="tpu_custom_call" | custom-call | tf_op jit(solution)/shard_map/means/pallas_call | solution.py:264
  3.5 0.0 copy-start.4
  3.5 2.2 %collective-permute-start = (f32[8,512]{1,0:T(8,128)S(1)}, f32[8,512]{1,0:T(8,128)S(1)}, u32[]{:S(2)}, u32[]{:S(2)}) collective-permute-start(f32[8,512]{1,0:T(8,128)S(1)} %means.1), channel_id=1, source_target_pairs={{0,8},{1,9},{2,10},{3,11},{4,12},{5,13},{6,14},{7,15},{8,0},{9,1},... | collective-permute-start | bytes 49160 | tf_op jit(solution)/shard_map/ppermute | solution.py:260
  5.7 0.0 copy-done.6
  5.7 0.0 copy-done.3
  5.7 0.0 copy-done.2
  5.8 0.6 %spread.2.spread_ref = bf16[384,2048]{1,0:T(8,128)(2,1)S(1)} custom-call(s32[1]{0:T(128)} %bitcast.1.me_ref, s32[4,2048]{1,0:T(4,128)S(1)} %bitcast.13, f32[4,2048]{1,0:T(4,128)S(1)} %bitcast.15), custom_call_target="tpu_custom_call" | custom-call | bytes 3000000 | tf_op jit(solution)/shard_map/spread/pallas_call | solution.py:249
  6.4 0.4 %collective-permute-done = f32[8,512]{1,0:T(8,128)S(1)} collective-permute-done((f32[8,512]{1,0:T(8,128)S(1)}, f32[8,512]{1,0:T(8,128)S(1)}, u32[]{:S(2)}, u32[]{:S(2)}) %collective-permute-start) | collective-permute-done | bytes 16416 | tf_op jit(solution)/shard_map/ppermute | solution.py:260
  6.9 2.5 %collective-permute-start.1 = (f32[16,512]{1,0:T(8,128)S(1)}, f32[16,512]{1,0:T(8,128)S(1)}, u32[]{:S(2)}, u32[]{:S(2)}) collective-permute-start(f32[16,512]{1,0:T(8,128)S(1)} %pad_maximum_fusion.2), channel_id=1, source_target_pairs={{0,16},{1,17},{2,18},{3,19},{4,20},{5,21},{6,22},{7,23},{8,24},{9,... | collective-permute-start | bytes 98312 | tf_op jit(solution)/shard_map/ppermute | solution.py:260
  9.3 0.1 constant_dynamic-slice_fusion
  9.4 0.1 reshape.25.own_ref
  9.5 0.7 %spread.3.spread_ref = bf16[384,2048]{1,0:T(8,128)(2,1)S(1)} custom-call(s32[1]{0:T(128)} %bitcast.1.me_ref, s32[4,2048]{1,0:T(4,128)S(1)} %bitcast.14, f32[4,2048]{1,0:T(4,128)S(1)} %bitcast.16), custom_call_target="tpu_custom_call" | custom-call | bytes 3000000 | tf_op jit(solution)/shard_map/spread/pallas_call | solution.py:249
  10.1 0.5 %collective-permute-done.1 = f32[16,512]{1,0:T(8,128)S(1)} collective-permute-done((f32[16,512]{1,0:T(8,128)S(1)}, f32[16,512]{1,0:T(8,128)S(1)}, u32[]{:S(2)}, u32[]{:S(2)}) %collective-permute-start.1) | collective-permute-done | bytes 32800 | tf_op jit(solution)/shard_map/ppermute | solution.py:260
  10.6 1.3 %collective-permute-start.2 = (f32[32,512]{1,0:T(8,128)S(1)}, f32[32,512]{1,0:T(8,128)S(1)}, u32[]{:S(2)}, u32[]{:S(2)}) collective-permute-start(f32[32,512]{1,0:T(8,128)S(1)} %pad_maximum_fusion.1), channel_id=1, source_target_pairs={{0,4},{1,5},{2,6},{3,7},{4,0},{5,1},{6,2},{7,3},{8,12},{9,13},{10,... | collective-permute-start | bytes 196616 | tf_op jit(solution)/shard_map/ppermute | solution.py:260
  11.9 0.0 copy-done.4
  11.9 0.5 %roles.1 = (f32[2,2048]{1,0:T(2,128)S(1)}, bf16[2048,64]{1,0:T(8,128)(2,1)S(1)}) custom-call(s32[2,1024]{1,0:T(2,128)S(1)} %reshape.24.orders_ref, s32[1,64]{1,0:T(1,128)S(1)} %reshape.25.own_ref, f32[16,128]{1,0:T(8,128)S(1)} %bitcast.17), custom_call_target="tpu_custom_call" | custom-call | bytes 1800000 | tf_op jit(solution)/shard_map/roles/pallas_call | solution.py:280
  12.5 1.3 %collective-permute-done.2 = f32[32,512]{1,0:T(8,128)S(1)} collective-permute-done((f32[32,512]{1,0:T(8,128)S(1)}, f32[32,512]{1,0:T(8,128)S(1)}, u32[]{:S(2)}, u32[]{:S(2)}) %collective-permute-start.2) | collective-permute-done | bytes 65568 | tf_op jit(solution)/shard_map/ppermute | solution.py:260
  13.8 0.0 copy-start.1
  13.8 1.3 %collective-permute-start.3 = (f32[64,512]{1,0:T(8,128)S(1)}, f32[64,512]{1,0:T(8,128)S(1)}, u32[]{:S(2)}, u32[]{:S(2)}) collective-permute-start(f32[64,512]{1,0:T(8,128)S(1)} %pad_maximum_fusion), channel_id=1, source_target_pairs={{0,2},{1,3},{2,0},{3,1},{4,6},{5,7},{6,4},{7,5},{8,10},{9,11},{10,... | collective-permute-start | bytes 393224 | tf_op jit(solution)/shard_map/ppermute | solution.py:260
  15.1 1.8 %halves.1.x_ref = bf16[8,192,1024]{2,1,0:T(8,128)(2,1)S(1)} custom-call(f32[64,8,1024]{2,1,0:T(8,128)} %x_ref.2), custom_call_target="tpu_custom_call" | custom-call | bytes 4500000 | tf_op jit(solution)/shard_map/halves/pallas_call | solution.py:294
  16.9 0.0 copy-start
  16.9 0.7 %collective-permute-done.3 = f32[64,512]{1,0:T(8,128)S(1)} collective-permute-done((f32[64,512]{1,0:T(8,128)S(1)}, f32[64,512]{1,0:T(8,128)S(1)}, u32[]{:S(2)}, u32[]{:S(2)}) %collective-permute-start.3) | collective-permute-done | bytes 131104 | tf_op jit(solution)/shard_map/ppermute | solution.py:260
  17.7 5.1 %collective-permute-start.4 = (f32[128,512]{1,0:T(8,128)S(1)}, f32[128,512]{1,0:T(8,128)S(1)}, u32[]{:S(2)}, u32[]{:S(2)}) collective-permute-start(f32[128,512]{1,0:T(8,128)S(1)} %constant_dynamic-update-slice_fusion.gathered_ref), channel_id=1, source_target_pairs={{0,1},{1,0},{2,3},{3,2},{4,5},{5,4},{6,7},{7,6},{8,9},{9,8},{10,11... | collective-permute-start | bytes 786440 | tf_op jit(solution)/shard_map/ppermute | solution.py:260
  22.7 0.0 copy-done.1
  22.7 1.3 %partial.1.hx_ref = f32[64,2048]{1,0:T(8,128)S(1)} custom-call(f32[128,512]{1,0:T(8,128)S(1)} %constant_dynamic-update-slice_fusion.gathered_ref, bf16[384,2048]{1,0:T(8,128)(2,1)S(1)} %spread.2.spread_ref, f32[8,2048]{1,0:T(8,128)S(1)} %bitcast.11), custom_call_target="tpu_custom_call" | custom-call | bytes 3600000 | tf_op jit(solution)/shard_map/partial/pallas_call | solution.py:328
  24.1 0.0 collective-permute-done.4.gathered_ref
  24.1 0.0 copy-done
  24.1 11.8 %update.1 = (f32[64,8,1024]{2,1,0:T(8,128)}, f32[64,64]{1,0:T(8,128)}) custom-call(f32[64,2048]{1,0:T(8,128)S(1)} %partial.1.hx_ref, f32[128,512]{1,0:T(8,128)S(1)} %collective-permute-done.4.gathered_ref, bf16[384,2048]{1,0:T(8,128)(2,1)S(1)} %spread.3.spread_ref, f32[8,2048]{1,0:T(8,128)S(1)} %bitcast.12, f32[64,2048]{1,0:T(8,128)S(1)} %bitcast.10, ...), custom_call_target="tpu_custom_call" | custom-call | tf_op jit(solution)/shard_map/update/pallas_call | solution.py:339
  (6 shorter events, 0.0 us)
Async XLA Ops:
  0.6 5.1 %copy-start.3 = (f32[2048,4]{0,1:T(4,128)S(1)}, f32[2048,4]{0,1:T(4,128)}, u32[]{:S(2)}) copy-start(f32[2048,4]{0,1:T(4,128)} %param.11) | copy-start | bytes 98308
  0.6 5.1 %copy-start.2 = (s32[2048,4]{0,1:T(4,128)S(1)}, s32[2048,4]{0,1:T(4,128)}, u32[]{:S(2)}) copy-start(s32[2048,4]{0,1:T(4,128)} %param.10) | copy-start | bytes 98308
  0.7 0.7 %copy-start.5 = (f32[1024]{0:T(1024)S(1)}, f32[1024]{0:T(1024)}, u32[]{:S(2)}) copy-start(f32[1024]{0:T(1024)} %param.9) | copy-start | bytes 12292
  1.4 4.4 %copy-start.6 = (s32[2048]{0:T(1024)S(1)}, s32[2048]{0:T(1024)}, u32[]{:S(2)}) copy-start(s32[2048]{0:T(1024)} %param.15) | copy-start | bytes 24580
  3.5 8.4 %copy-start.4 = (f32[2048]{0:T(1024)S(1)}, f32[2048]{0:T(1024)}, u32[]{:S(2)}) copy-start(f32[2048]{0:T(1024)} %param.14) | copy-start | bytes 24580
  3.5 3.3 %collective-permute-start = (f32[8,512]{1,0:T(8,128)S(1)}, f32[8,512]{1,0:T(8,128)S(1)}, u32[]{:S(2)}, u32[]{:S(2)}) collective-permute-start(f32[8,512]{1,0:T(8,128)S(1)} %means.1), channel_id=1, source_target_pairs={{0,8},{1,9},{2,10},{3,11},{4,12},{5,13},{6,14},{7,15},{8,0},{9,1},... | collective-permute-start | bytes 49160 | tf_op jit(solution)/shard_map/ppermute | solution.py:260
  6.9 3.8 %collective-permute-start.1 = (f32[16,512]{1,0:T(8,128)S(1)}, f32[16,512]{1,0:T(8,128)S(1)}, u32[]{:S(2)}, u32[]{:S(2)}) collective-permute-start(f32[16,512]{1,0:T(8,128)S(1)} %pad_maximum_fusion.2), channel_id=1, source_target_pairs={{0,16},{1,17},{2,18},{3,19},{4,20},{5,21},{6,22},{7,23},{8,24},{9,... | collective-permute-start | bytes 98312 | tf_op jit(solution)/shard_map/ppermute | solution.py:260
  10.6 3.1 %collective-permute-start.2 = (f32[32,512]{1,0:T(8,128)S(1)}, f32[32,512]{1,0:T(8,128)S(1)}, u32[]{:S(2)}, u32[]{:S(2)}) collective-permute-start(f32[32,512]{1,0:T(8,128)S(1)} %pad_maximum_fusion.1), channel_id=1, source_target_pairs={{0,4},{1,5},{2,6},{3,7},{4,0},{5,1},{6,2},{7,3},{8,12},{9,13},{10,... | collective-permute-start | bytes 196616 | tf_op jit(solution)/shard_map/ppermute | solution.py:260
  13.8 9.0 %copy-start.1 = (f32[2048,8]{0,1:T(8,128)S(1)}, f32[2048,8]{0,1:T(8,128)}, u32[]{:S(2)}) copy-start(f32[2048,8]{0,1:T(8,128)} %param.12) | copy-start | bytes 196612
  13.8 3.9 %collective-permute-start.3 = (f32[64,512]{1,0:T(8,128)S(1)}, f32[64,512]{1,0:T(8,128)S(1)}, u32[]{:S(2)}, u32[]{:S(2)}) collective-permute-start(f32[64,512]{1,0:T(8,128)S(1)} %pad_maximum_fusion), channel_id=1, source_target_pairs={{0,2},{1,3},{2,0},{3,1},{4,6},{5,7},{6,4},{7,5},{8,10},{9,11},{10,... | collective-permute-start | bytes 393224 | tf_op jit(solution)/shard_map/ppermute | solution.py:260
  16.9 7.2 %copy-start = (f32[2048,64]{0,1:T(8,128)S(1)}, f32[2048,64]{0,1:T(8,128)}, u32[]{:S(2)}) copy-start(f32[2048,64]{0,1:T(8,128)} %param.13) | copy-start | bytes 1572868
  17.7 6.4 %collective-permute-start.4 = (f32[128,512]{1,0:T(8,128)S(1)}, f32[128,512]{1,0:T(8,128)S(1)}, u32[]{:S(2)}, u32[]{:S(2)}) collective-permute-start(f32[128,512]{1,0:T(8,128)S(1)} %constant_dynamic-update-slice_fusion.gathered_ref), channel_id=1, source_target_pairs={{0,1},{1,0},{2,3},{3,2},{4,5},{5,4},{6,7},{7,6},{8,9},{9,8},{10,11... | collective-permute-start | bytes 786440 | tf_op jit(solution)/shard_map/ppermute | solution.py:260

commit v3 on v2

--- a/solution.py
+++ b/solution.py
@@ -36,14 +36,17 @@
     return jnp.sum(x, axis=1, keepdims=True) * (1.0 / x.shape[1])
 
 
-def means_kernel(x_ref, kernel_ref, out_ref, held_ref, sems):
+def means_kernel(x_ref, kernel_ref, out_ref, held_ref, sems, weight_ref, sem):
     members, bins, _ = x_ref.shape
     nb = out_ref.shape[0]
+    kernel_copy = pltpu.make_async_copy(kernel_ref, weight_ref, sem)
+    kernel_copy.start()
     copies = []
     for b in range(bins):
         copies.append(pltpu.make_async_copy(x_ref.at[:, b, :], held_ref.at[b], sems.at[b]))
         copies[-1].start()
-    scale = kernel_ref[...] * (1.0 / BLK)
+    kernel_copy.wait()
+    scale = weight_ref[...] * (1.0 / BLK)
     lane = lax.broadcasted_iota(jnp.int32, (2 * members, 128), 1)
     for b in range(0, bins, 2):
         copies[b].wait()
@@ -235,7 +238,12 @@
     share = P_SIZE // devices
     zbits = [(nc << i).bit_length() - 1 for i in range(nz.bit_length() - 1)]
     cbits = [i for i in reversed(range(nc.bit_length() - 1))]
-    bits = zbits + cbits
+    rounds = [[bit] for bit in reversed(zbits)]
+    plane = [bit for bit in cbits if bit > 0]
+    while plane:
+        rounds.append(sorted(plane[-2:]))
+        plane = plane[:-2]
+    bits = [bit for group in rounds for bit in group] + [0]
     rows = members * bins
     half = nb * devices // 2
     wide = 6 * half * sensors
@@ -256,20 +264,20 @@
             cost_estimate=cost(1.0),
         )(who, places, weights)
 
-    def exchange(value, bit):
-        return lax.ppermute(value, AXES, [(i, i ^ (1 << bit)) for i in range(devices)])
+    def exchange(value, mask):
+        return lax.ppermute(value, AXES, [(i, i ^ mask) for i in range(devices)])
 
     far_state = pltpu.with_memory_space_constraint(state, pltpu.HBM)
     staging = [pltpu.VMEM((bins, members, cells), F32), pltpu.SemaphoreType.DMA((bins,))]
     piece = pl.pallas_call(
         means_kernel,
         out_shape=jax.ShapeDtypeStruct((nb, rows), F32),
-        in_specs=[HBM_SPEC, VMEM_SPEC],
+        in_specs=[HBM_SPEC, HBM_SPEC],
         out_specs=VMEM_SPEC,
-        scratch_shapes=staging,
+        scratch_shapes=staging + [pltpu.VMEM((1, cells), F32), pltpu.SemaphoreType.DMA],
         compiler_params=small,
         name="means",
-    )(far_state, kernel.reshape(1, cells))
+    )(far_state, pltpu.with_memory_space_constraint(kernel.reshape(1, cells), pltpu.HBM))
 
     who, places, weights = me.reshape(1), blocks.T, foot_weight.T
     orders = batch_order.reshape(batches, P_SIZE)
@@ -303,25 +311,25 @@
         )(pltpu.with_memory_space_constraint(far_state, pltpu.HBM))
 
     beside = [
-        (functools.partial(spread_of, 0), (who, places, weights)),
-        (functools.partial(spread_of, half), (who, places, weights)),
-        (roles_of, (orders, own, inverse)),
-        (halves_of, (state,)),
+        [(functools.partial(spread_of, 0), (who, places, weights))],
+        [(functools.partial(spread_of, half), (who, places, weights))],
+        [(roles_of, (orders, own, inverse)), (halves_of, (state,))],
     ]
     made = []
-    for i, bit in enumerate(bits[:-1]):
-        if i < len(beside):
-            work, needs = beside[i]
-            piece, needs = lax.optimization_barrier((piece, needs))
-            other = exchange(piece, bit)
-            result = work(*needs)
-            other, result = lax.optimization_barrier((other, result))
-            made.append(result)
-        else:
-            other = exchange(piece, bit)
-        piece = jnp.concatenate([piece, other], axis=0)
+    for i, group in enumerate(rounds):
+        work = beside[i] if i < len(beside) else []
+        needs = [args for _, args in work]
+        piece, needs = lax.optimization_barrier((piece, needs))
+        masks = [1 << bit for bit in group]
+        if len(masks) == 2:
+            masks.append(masks[0] | masks[1])
+        others = [exchange(piece, mask) for mask in masks]
+        results = [run(*args) for (run, _), args in zip(work, needs)]
+        others, results = lax.optimization_barrier((others, results))
+        made += results
+        piece = jnp.concatenate([piece] + others, axis=0)
     spread_near, spread_far, (weight, pick), parts = made
-    other = exchange(piece, bits[-1])
+    other = exchange(piece, 1)
 
     left = pltpu.VMEM((rows, 3 * half), BF16)
     resp = bin_response.T

time: 36.3 us -> 33.9 us (0.934)
  waiting for transfers between devices: 2.98 us -> 1.62 us
  local copies, waits for them, and re-layouts: 0.9 us -> 0.22 us
    ppermute x5 -> x6, waiting for transfers between devices: 2.98 us -> 1.62 us  [exchange(): return lax.ppermute(value, AXES, [(i, i ^ mask) for i in range(devices)])]
    unnamed x15, local copies, waits for them, and re-layouts: 0.73 us -> 0.05 us
    ppermute x5 -> x6, starting transfers between devices: 12.3 us -> 12.1 us  [exchange(): return lax.ppermute(value, AXES, [(i, i ^ mask) for i in range(devices)])]
  transfers between devices with their start and end apart: 5 -> 6, of which waited for: 4 -> 4; matrix products, arithmetic and copies ran while one was open for 0% -> 1% of each run, Pallas kernels for 14% -> 15%
where the time goes in v3:
time: 33.9 us; the launch traced here: 33.6 us
  Pallas kernels  18.9 us (56%)
  starting transfers between devices  12.1 us (36%)
  waiting for transfers between devices  1.62 us (5%)
  between operations  0.8 us (2%)
    ppermute x6, starting transfers between devices, exchange(): return lax.ppermute(value, AXES, [(i, i ^ mask) for i in range(devices)])  12.1 us
    pallas_call x1, Pallas kernels, shards(): pl.pallas_call(functools.partial(update_kernel, members, bins), out_shape...  11.8 us
    pallas_call x1, Pallas kernels, shards(): pl.pallas_call(means_kernel, out_shape=jax.ShapeDtypeStruct((nb, rows), F...  2.18 us
    pallas_call x1, Pallas kernels, halves_of(): pl.pallas_call(halves_kernel, out_shape=jax.ShapeDtypeStruct((bins, 3 * m...  1.77 us
    ppermute x6, waiting for transfers between devices, exchange(): return lax.ppermute(value, AXES, [(i, i ^ mask) for i in range(devices)])  1.62 us
    pallas_call x1, Pallas kernels, shards(): pl.pallas_call(functools.partial(partial_kernel, members, bins), out_shap...  1.32 us
    pallas_call x2, Pallas kernels, spread_of(): pl.pallas_call(functools.partial(spread_kernel, bits, nb, first), out_sha...  1.3 us
  transfers between devices with their start and end apart: 6, of which 4 were waited for; matrix products, arithmetic and copies ran while one was open for 1% of the time, Pallas kernels for 15%

profile of v3, /device:TPU:1, one launch (start us, length us, event | category | flops | bytes accessed | tf_op | source)
XLA Modules:
  0.0 33.6 jit_solution(12485764925911520396)
XLA Ops:
  0.6 0.0 copy-start.3
  0.6 0.0 copy-start.2
  0.7 0.0 copy-start.5
  0.7 2.2 %means.1 = f32[8,512]{1,0:T(8,128)S(1)} custom-call(f32[64,8,1024]{2,1,0:T(8,128)} %x_ref.2, f32[1,1024]{1,0:T(1,128)} %bitcast.18), custom_call_target="tpu_custom_call" | custom-call | tf_op jit(solution)/shard_map/means/pallas_call | solution.py:272
  2.9 3.2 %collective-permute-start = (f32[8,512]{1,0:T(8,128)S(1)}, f32[8,512]{1,0:T(8,128)S(1)}, u32[]{:S(2)}, u32[]{:S(2)}) collective-permute-start(f32[8,512]{1,0:T(8,128)S(1)} %means.1), channel_id=1, source_target_pairs={{0,16},{1,17},{2,18},{3,19},{4,20},{5,21},{6,22},{7,23},{8,24},{9,... | collective-permute-start | bytes 49160 | tf_op jit(solution)/shard_map/ppermute | solution.py:268
  6.1 0.0 copy-done.5
  6.1 0.0 copy-done.3
  6.1 0.0 copy-done.2
  6.1 0.6 %spread.2.spread_ref = bf16[384,2048]{1,0:T(8,128)(2,1)S(1)} custom-call(s32[1]{0:T(128)} %bitcast.1.me_ref, s32[4,2048]{1,0:T(4,128)S(1)} %bitcast.13, f32[4,2048]{1,0:T(4,128)S(1)} %bitcast.15), custom_call_target="tpu_custom_call" | custom-call | bytes 3000000 | tf_op jit(solution)/shard_map/spread/pallas_call | solution.py:257
  6.7 0.4 %collective-permute-done = f32[8,512]{1,0:T(8,128)S(1)} collective-permute-done((f32[8,512]{1,0:T(8,128)S(1)}, f32[8,512]{1,0:T(8,128)S(1)}, u32[]{:S(2)}, u32[]{:S(2)}) %collective-permute-start) | collective-permute-done | bytes 16416 | tf_op jit(solution)/shard_map/ppermute | solution.py:268
  7.2 1.3 %collective-permute-start.1 = (f32[16,512]{1,0:T(8,128)S(1)}, f32[16,512]{1,0:T(8,128)S(1)}, u32[]{:S(2)}, u32[]{:S(2)}) collective-permute-start(f32[16,512]{1,0:T(8,128)S(1)} %pad_maximum_fusion.1), channel_id=1, source_target_pairs={{0,8},{1,9},{2,10},{3,11},{4,12},{5,13},{6,14},{7,15},{8,0},{9,1},... | collective-permute-start | bytes 98312 | tf_op jit(solution)/shard_map/ppermute | solution.py:268
  8.5 0.1 constant_dynamic-slice_fusion
  8.6 0.1 reshape.25.own_ref
  8.7 0.7 %spread.3.spread_ref = bf16[384,2048]{1,0:T(8,128)(2,1)S(1)} custom-call(s32[1]{0:T(128)} %bitcast.1.me_ref, s32[4,2048]{1,0:T(4,128)S(1)} %bitcast.14, f32[4,2048]{1,0:T(4,128)S(1)} %bitcast.16), custom_call_target="tpu_custom_call" | custom-call | bytes 3000000 | tf_op jit(solution)/shard_map/spread/pallas_call | solution.py:257
  9.4 0.6 %collective-permute-done.1 = f32[16,512]{1,0:T(8,128)S(1)} collective-permute-done((f32[16,512]{1,0:T(8,128)S(1)}, f32[16,512]{1,0:T(8,128)S(1)}, u32[]{:S(2)}, u32[]{:S(2)}) %collective-permute-start.1) | collective-permute-done | bytes 32800 | tf_op jit(solution)/shard_map/ppermute | solution.py:268
  10.0 0.0 copy-start.4
  10.0 0.0 copy-start.1
  10.0 2.3 %collective-permute-start.4 = (f32[32,512]{1,0:T(8,128)S(1)}, f32[32,512]{1,0:T(8,128)S(1)}, u32[]{:S(2)}, u32[]{:S(2)}) collective-permute-start(f32[32,512]{1,0:T(8,128)S(1)} %pad_maximum_fusion), channel_id=1, source_target_pairs={{0,6},{1,7},{2,4},{3,5},{4,2},{5,3},{6,0},{7,1},{8,14},{9,15},{10,... | collective-permute-start | bytes 196616 | tf_op jit(solution)/shard_map/ppermute | solution.py:268
  12.3 0.2 collective-permute-start.3
  12.5 0.2 collective-permute-start.2
  12.7 1.8 %halves.1.x_ref = bf16[8,192,1024]{2,1,0:T(8,128)(2,1)S(1)} custom-call(f32[64,8,1024]{2,1,0:T(8,128)} %x_ref.2), custom_call_target="tpu_custom_call" | custom-call | bytes 4500000 | tf_op jit(solution)/shard_map/halves/pallas_call | solution.py:302
  14.5 0.0 copy-done.4
  14.5 0.0 copy-start
  14.5 0.5 %roles.1 = (f32[2,2048]{1,0:T(2,128)S(1)}, bf16[2048,64]{1,0:T(8,128)(2,1)S(1)}) custom-call(s32[2,1024]{1,0:T(2,128)S(1)} %reshape.24.orders_ref, s32[1,64]{1,0:T(1,128)S(1)} %reshape.25.own_ref, f32[16,128]{1,0:T(8,128)S(1)} %bitcast.17), custom_call_target="tpu_custom_call" | custom-call | bytes 1800000 | tf_op jit(solution)/shard_map/roles/pallas_call | solution.py:288
  15.0 0.0 collective-permute-done.4
  15.0 0.3 %collective-permute-done.3 = f32[32,512]{1,0:T(8,128)S(1)} collective-permute-done((f32[32,512]{1,0:T(8,128)S(1)}, f32[32,512]{1,0:T(8,128)S(1)}, u32[]{:S(2)}, u32[]{:S(2)}) %collective-permute-start.3) | collective-permute-done | bytes 65568 | tf_op jit(solution)/shard_map/ppermute | solution.py:268
  15.4 0.2 collective-permute-done.2
  15.6 4.8 %collective-permute-start.5 = (f32[128,512]{1,0:T(8,128)S(1)}, f32[128,512]{1,0:T(8,128)S(1)}, u32[]{:S(2)}, u32[]{:S(2)}) collective-permute-start(f32[128,512]{1,0:T(8,128)S(1)} %constant_dynamic-update-slice_fusion.gathered_ref), channel_id=1, source_target_pairs={{0,1},{1,0},{2,3},{3,2},{4,5},{5,4},{6,7},{7,6},{8,9},{9,8},{10,11... | collective-permute-start | bytes 786440 | tf_op jit(solution)/shard_map/ppermute | solution.py:268
  20.4 0.0 copy-done.1
  20.4 1.3 %partial.1.hx_ref = f32[64,2048]{1,0:T(8,128)S(1)} custom-call(f32[128,512]{1,0:T(8,128)S(1)} %constant_dynamic-update-slice_fusion.gathered_ref, bf16[384,2048]{1,0:T(8,128)(2,1)S(1)} %spread.2.spread_ref, f32[8,2048]{1,0:T(8,128)S(1)} %bitcast.11), custom_call_target="tpu_custom_call" | custom-call | bytes 3600000 | tf_op jit(solution)/shard_map/partial/pallas_call | solution.py:336
  21.8 0.0 collective-permute-done.5.gathered_ref
  21.8 0.0 copy-done
  21.8 11.8 %update.1 = (f32[64,8,1024]{2,1,0:T(8,128)}, f32[64,64]{1,0:T(8,128)}) custom-call(f32[64,2048]{1,0:T(8,128)S(1)} %partial.1.hx_ref, f32[128,512]{1,0:T(8,128)S(1)} %collective-permute-done.5.gathered_ref, bf16[384,2048]{1,0:T(8,128)(2,1)S(1)} %spread.3.spread_ref, f32[8,2048]{1,0:T(8,128)S(1)} %bitcast.12, f32[64,2048]{1,0:T(8,128)S(1)} %bitcast.10, ...), custom_call_target="tpu_custom_call" | custom-call | tf_op jit(solution)/shard_map/update/pallas_call | solution.py:347
  (7 shorter events, 0.0 us)
Async XLA Ops:
  0.6 5.4 %copy-start.3 = (f32[2048,4]{0,1:T(4,128)S(1)}, f32[2048,4]{0,1:T(4,128)}, u32[]{:S(2)}) copy-start(f32[2048,4]{0,1:T(4,128)} %param.11) | copy-start | bytes 98308
  0.6 5.4 %copy-start.2 = (s32[2048,4]{0,1:T(4,128)S(1)}, s32[2048,4]{0,1:T(4,128)}, u32[]{:S(2)}) copy-start(s32[2048,4]{0,1:T(4,128)} %param.10) | copy-start | bytes 98308
  0.7 5.4 %copy-start.5 = (s32[2048]{0:T(1024)S(1)}, s32[2048]{0:T(1024)}, u32[]{:S(2)}) copy-start(s32[2048]{0:T(1024)} %param.15) | copy-start | bytes 24580
  2.9 4.3 %collective-permute-start = (f32[8,512]{1,0:T(8,128)S(1)}, f32[8,512]{1,0:T(8,128)S(1)}, u32[]{:S(2)}, u32[]{:S(2)}) collective-permute-start(f32[8,512]{1,0:T(8,128)S(1)} %means.1), channel_id=1, source_target_pairs={{0,16},{1,17},{2,18},{3,19},{4,20},{5,21},{6,22},{7,23},{8,24},{9,... | collective-permute-start | bytes 49160 | tf_op jit(solution)/shard_map/ppermute | solution.py:268
  7.2 2.8 %collective-permute-start.1 = (f32[16,512]{1,0:T(8,128)S(1)}, f32[16,512]{1,0:T(8,128)S(1)}, u32[]{:S(2)}, u32[]{:S(2)}) collective-permute-start(f32[16,512]{1,0:T(8,128)S(1)} %pad_maximum_fusion.1), channel_id=1, source_target_pairs={{0,8},{1,9},{2,10},{3,11},{4,12},{5,13},{6,14},{7,15},{8,0},{9,1},... | collective-permute-start | bytes 98312 | tf_op jit(solution)/shard_map/ppermute | solution.py:268
  10.0 4.5 %copy-start.4 = (f32[2048]{0:T(1024)S(1)}, f32[2048]{0:T(1024)}, u32[]{:S(2)}) copy-start(f32[2048]{0:T(1024)} %param.14) | copy-start | bytes 24580
  10.0 10.5 %copy-start.1 = (f32[2048,8]{0,1:T(8,128)S(1)}, f32[2048,8]{0,1:T(8,128)}, u32[]{:S(2)}) copy-start(f32[2048,8]{0,1:T(8,128)} %param.12) | copy-start | bytes 196612
  10.0 5.1 %collective-permute-start.4 = (f32[32,512]{1,0:T(8,128)S(1)}, f32[32,512]{1,0:T(8,128)S(1)}, u32[]{:S(2)}, u32[]{:S(2)}) collective-permute-start(f32[32,512]{1,0:T(8,128)S(1)} %pad_maximum_fusion), channel_id=1, source_target_pairs={{0,6},{1,7},{2,4},{3,5},{4,2},{5,3},{6,0},{7,1},{8,14},{9,15},{10,... | collective-permute-start | bytes 196616 | tf_op jit(solution)/shard_map/ppermute | solution.py:268
  12.3 3.1 %collective-permute-start.3 = (f32[32,512]{1,0:T(8,128)S(1)}, f32[32,512]{1,0:T(8,128)S(1)}, u32[]{:S(2)}, u32[]{:S(2)}) collective-permute-start(f32[32,512]{1,0:T(8,128)S(1)} %pad_maximum_fusion), channel_id=1, source_target_pairs={{0,4},{1,5},{2,6},{3,7},{4,0},{5,1},{6,2},{7,3},{8,12},{9,13},{10,... | collective-permute-start | bytes 196616 | tf_op jit(solution)/shard_map/ppermute | solution.py:268
  12.5 3.1 %collective-permute-start.2 = (f32[32,512]{1,0:T(8,128)S(1)}, f32[32,512]{1,0:T(8,128)S(1)}, u32[]{:S(2)}, u32[]{:S(2)}) collective-permute-start(f32[32,512]{1,0:T(8,128)S(1)} %pad_maximum_fusion), channel_id=1, source_target_pairs={{0,2},{1,3},{2,0},{3,1},{4,6},{5,7},{6,4},{7,5},{8,10},{9,11},{10,... | collective-permute-start | bytes 196616 | tf_op jit(solution)/shard_map/ppermute | solution.py:268
  14.5 7.3 %copy-start = (f32[2048,64]{0,1:T(8,128)S(1)}, f32[2048,64]{0,1:T(8,128)}, u32[]{:S(2)}) copy-start(f32[2048,64]{0,1:T(8,128)} %param.13) | copy-start | bytes 1572868
  15.6 6.1 %collective-permute-start.5 = (f32[128,512]{1,0:T(8,128)S(1)}, f32[128,512]{1,0:T(8,128)S(1)}, u32[]{:S(2)}, u32[]{:S(2)}) collective-permute-start(f32[128,512]{1,0:T(8,128)S(1)} %constant_dynamic-update-slice_fusion.gathered_ref), channel_id=1, source_target_pairs={{0,1},{1,0},{2,3},{3,2},{4,5},{5,4},{6,7},{7,6},{8,9},{9,8},{10,11... | collective-permute-start | bytes 786440 | tf_op jit(solution)/shard_map/ppermute | solution.py:268

commit v4 on v3

--- a/solution.py
+++ b/solution.py
@@ -96,9 +96,10 @@
         out_ref[b, 2 * members : 3 * members, :] = hi
 
 
-def roles_kernel(orders_ref, own_ref, var_ref, weight_ref, pick_ref):
+def roles_kernel(orders_ref, own_ref, var_ref, blocks_ref, foot_ref, resp_ref, weight_ref, *table_refs):
     batches, per = orders_ref.shape
     groups = var_ref.shape[0]
+    sensors = blocks_ref.shape[1]
     inverse = 1.0 / var_ref[...]
     high = lax.broadcasted_iota(jnp.int32, (groups, per), 0)
     low = lax.broadcasted_iota(jnp.int32, (128, per), 0)
@@ -109,9 +110,34 @@
         held = lax.dot_general(of_high, of_low, NT, preferred_element_type=F32) * inverse
         for g in range(groups):
             weight_ref[t : t + 1, g * 128 : (g + 1) * 128] = held[g : g + 1, :]
-    sensors, nown = pick_ref.shape
-    sensor = lax.broadcasted_iota(jnp.int32, (sensors, nown), 0)
-    pick_ref[...] = jnp.where(sensor == own_ref[...], 1.0, 0.0).astype(BF16)
+    sensor = lax.broadcasted_iota(jnp.int32, (sensors, 128), 0)
+    pick = jnp.where(sensor == own_ref[...], 1.0, 0.0).astype(BF16)
+    tables = jnp.concatenate(
+        [blocks_ref[...].astype(F32), foot_ref[...], resp_ref[...]], axis=0
+    )
+    first = tables.astype(BF16)
+    rest = tables - first.astype(F32)
+    second = rest.astype(BF16)
+    third = (rest - second.astype(F32)).astype(BF16)
+    stacked = jnp.dot(
+        jnp.concatenate([first, second, third], axis=0), pick, preferred_element_type=F32
+    )
+    n = tables.shape[0]
+    own = stacked[0:n] + stacked[n : 2 * n] + stacked[2 * n : 3 * n]
+    at = 0
+    for ref, table in zip(table_refs, (blocks_ref, foot_ref, resp_ref)):
+        rows = table.shape[0]
+        ref[:, 0:sensors] = table[...]
+        ref[:, sensors : sensors + 128] = own[at : at + rows].astype(ref.dtype)
+        at += rows
+
+
+def obs_kernel(obs_ref, out_ref):
+    step = 128
+    for c in range(0, obs_ref.shape[1], step):
+        hi, low = split(obs_ref[:, c : c + step].T)
+        out_ref[0, c : c + step, :] = hi
+        out_ref[1, c : c + step, :] = low
 
 
 def turn(gathered_ref, left):
@@ -133,9 +159,9 @@
 
 def partial_kernel(members, bins, gathered_ref, spread_ref, resp_ref, hx_ref, left):
     turn(gathered_ref, left)
-    step = 256
-    for c in range(0, resp_ref.shape[1], step):
-        cut = slice(c, c + step)
+    width = resp_ref.shape[1]
+    for c in range(0, width, 512):
+        cut = slice(c, min(c + 512, width))
         hx_ref[:, cut] = observe(members, bins, left, spread_ref, resp_ref, cut)
 
 
@@ -171,39 +197,40 @@
 
 
 def update_kernel(
-    members, bins, hx_ref, gathered_ref, spread_ref, resp_ref, obs_ref, weight_ref, pick_ref, x_ref,
-    field_ref, finals_ref, left, out, sems,
+    members, bins, hx_ref, gathered_ref, spread_ref, resp_ref, obs_ref, weight_ref, x_ref,
+    field_ref, finals_ref, left, anom, out, sems,
 ):
-    sensors = resp_ref.shape[1]
+    sensors = weight_ref.shape[1]
     turn(gathered_ref, left)
-    step = 256
-    sums = jnp.zeros((2 * members, 2 * members), F32)
-    picked = jnp.zeros((2 * members, pick_ref.shape[1]), F32)
+    step = 512
     for c in range(0, sensors, step):
         cut = slice(c, c + step)
         hx = hx_ref[:, cut] + observe(members, bins, left, spread_ref, resp_ref, cut)
         center = sublane_mean(hx)
-        anom = hx - center
-        right = jnp.concatenate([anom, obs_ref[:, cut] - center], axis=0)
-        wide = jnp.concatenate([anom * weight_ref[t : t + 1, cut] for t in range(2)], axis=0)
-        rhi, rlo = split(right)
-        whi, wlo = split(wide)
-        sums += lax.dot_general(
-            jnp.concatenate([whi, whi, wlo], axis=1),
-            jnp.concatenate([rhi, rlo, rhi], axis=1),
-            NT,
-            preferred_element_type=F32,
-        )
-        hhi, hlo = split(hx)
-        picked += jnp.dot(
-            jnp.concatenate([hhi, hlo], axis=0), pick_ref[cut, :], preferred_element_type=F32
-        )
-    picked = picked[0:members] + picked[members:]
+        anom[0:members, cut] = hx - center
+        anom[members:, cut] = jnp.broadcast_to(center, (anom.shape[0] - members, step))
+    cut = slice(sensors, sensors + 128)
+    picked = hx_ref[:, cut] + observe(members, bins, left, spread_ref, resp_ref, cut)
+    rhi, rlo = split(anom[...])
+    whi, wlo = split(
+        jnp.concatenate([anom[0:members, :] * weight_ref[t : t + 1, :] for t in range(2)], axis=0)
+    )
+    sums = (
+        lax.dot_general(whi, rhi, NT, preferred_element_type=F32)
+        + lax.dot_general(wlo, rhi, NT, preferred_element_type=F32)
+        + lax.dot_general(whi, rlo, NT, preferred_element_type=F32)
+    )
+    pulls = (
+        jnp.dot(whi, obs_ref[0], preferred_element_type=F32)
+        + jnp.dot(wlo, obs_ref[0], preferred_element_type=F32)
+        + jnp.dot(whi, obs_ref[1], preferred_element_type=F32)
+        - sums[:, members : members + 1]
+    )
     r64 = lax.broadcasted_iota(jnp.int32, (members, members), 0)
     c64 = lax.broadcasted_iota(jnp.int32, (members, members), 1)
     eye = (r64 == c64).astype(F32)
-    s0, e0 = sums[0:members, 0:members], sums[0:members, members:]
-    s1, e1 = sums[members:, 0:members], sums[members:, members:]
+    s0, e0 = sums[0:members, 0:members], pulls[0:members]
+    s1, e1 = sums[members:, 0:members], pulls[members:]
     gain = solve(jnp.concatenate([s0 + (members - 1.0) * eye, e0 - s0], axis=1))
     first_t = eye + gain - sublane_mean(gain)
     first_ct = first_t - lane_mean(first_t)
@@ -216,13 +243,13 @@
     )
     total = first + mm(gain.T, first_c)
     thi, tlo = split(total)
-    both = jnp.concatenate([thi, thi, tlo], axis=1)
+    lhs = jnp.concatenate([thi, thi, tlo], axis=1)
     copies = []
     for b in range(bins):
-        out[b] = jnp.dot(both, x_ref[b], preferred_element_type=F32)
+        out[b] = jnp.dot(lhs, x_ref[b], preferred_element_type=F32)
         copies.append(pltpu.make_async_copy(out.at[b], field_ref.at[:, b, :], sems.at[b]))
         copies[-1].start()
-    finals_ref[...] = mm(total, picked).T
+    finals_ref[...] = mm(total, picked).T[0 : finals_ref.shape[0], :]
     for copy in copies:
         copy.wait()
 
@@ -247,6 +274,7 @@
     rows = members * bins
     half = nb * devices // 2
     wide = 6 * half * sensors
+    width = sensors + 128
     small = pltpu.CompilerParams(vmem_limit_bytes=8 * MIB + wide)
     large = pltpu.CompilerParams(vmem_limit_bytes=12 * MIB + 2 * wide)
 
@@ -256,7 +284,7 @@
     def spread_of(first, who, places, weights):
         return pl.pallas_call(
             functools.partial(spread_kernel, bits, nb, first),
-            out_shape=jax.ShapeDtypeStruct((3 * half, sensors), BF16),
+            out_shape=jax.ShapeDtypeStruct((3 * half, width), BF16),
             in_specs=[SMEM_SPEC, VMEM_SPEC, VMEM_SPEC],
             out_specs=VMEM_SPEC,
             compiler_params=small,
@@ -281,22 +309,34 @@
 
     who, places, weights = me.reshape(1), blocks.T, foot_weight.T
     orders = batch_order.reshape(batches, P_SIZE)
-    own = lax.dynamic_slice_in_dim(orders, me * share, share, 1).reshape(1, batches * share)
     inverse = obs_var.reshape(sensors // 128, 128)
 
-    def roles_of(orders, own, inverse):
+    def roles_of(*args):
         return pl.pallas_call(
             roles_kernel,
             out_shape=[
                 jax.ShapeDtypeStruct((batches, sensors), F32),
-                jax.ShapeDtypeStruct((sensors, batches * share), BF16),
+                jax.ShapeDtypeStruct((blocks.shape[1], width), jnp.int32),
+                jax.ShapeDtypeStruct((blocks.shape[1], width), F32),
+                jax.ShapeDtypeStruct((bins, width), F32),
             ],
-            in_specs=[VMEM_SPEC] * 3,
-            out_specs=[VMEM_SPEC] * 2,
+            in_specs=[VMEM_SPEC] * 6,
+            out_specs=[VMEM_SPEC] * 4,
             compiler_params=small,
             name="roles",
             cost_estimate=cost(0.6),
-        )(orders, own, inverse)
+        )(*args)
+
+    def obs_of(observed):
+        return pl.pallas_call(
+            obs_kernel,
+            out_shape=jax.ShapeDtypeStruct((2, sensors, members), BF16),
+            in_specs=[VMEM_SPEC],
+            out_specs=VMEM_SPEC,
+            compiler_params=small,
+            name="observed",
+            cost_estimate=cost(0.4),
+        )(observed)
 
     def halves_of(far_state):
         return pl.pallas_call(
@@ -310,39 +350,53 @@
             cost_estimate=cost(1.5),
         )(pltpu.with_memory_space_constraint(far_state, pltpu.HBM))
 
-    beside = [
-        [(functools.partial(spread_of, 0), (who, places, weights))],
-        [(functools.partial(spread_of, half), (who, places, weights))],
-        [(roles_of, (orders, own, inverse)), (halves_of, (state,))],
-    ]
-    made = []
+    made = {}
+
+    def first_work():
+        own = lax.dynamic_slice_in_dim(orders, me * share, share, 1).reshape(1, batches * share)
+        own = jnp.pad(own, ((0, 0), (0, 128 - batches * share)), constant_values=-1)
+        made["roles"] = roles_of(orders, own, inverse, places, weights, bin_response.T)
+        made["near"] = spread_of(0, who, *made["roles"][1:3])
+
+    def second_work():
+        made["far"] = spread_of(half, who, *made["roles"][1:3])
+
+    def third_work():
+        made["parts"] = halves_of(state)
+        made["obs"] = obs_of(observed.T)
+
+    beside = [first_work, second_work, third_work]
     for i, group in enumerate(rounds):
-        work = beside[i] if i < len(beside) else []
-        needs = [args for _, args in work]
-        piece, needs = lax.optimization_barrier((piece, needs))
         masks = [1 << bit for bit in group]
         if len(masks) == 2:
             masks.append(masks[0] | masks[1])
+        if i == 0:
+            piece, orders, places, weights = lax.optimization_barrier(
+                (piece, orders, places, weights)
+            )
+        elif i == 1:
+            piece, who = lax.optimization_barrier((piece, who))
+        elif i == 2:
+            piece, state, observed = lax.optimization_barrier((piece, state, observed))
         others = [exchange(piece, mask) for mask in masks]
-        results = [run(*args) for (run, _), args in zip(work, needs)]
-        others, results = lax.optimization_barrier((others, results))
-        made += results
+        if i < len(beside):
+            beside[i]()
+        others, made = lax.optimization_barrier((others, made))
         piece = jnp.concatenate([piece] + others, axis=0)
-    spread_near, spread_far, (weight, pick), parts = made
+    weight, _, _, resp = made["roles"]
     other = exchange(piece, 1)
 
     left = pltpu.VMEM((rows, 3 * half), BF16)
-    resp = bin_response.T
     hx = pl.pallas_call(
         functools.partial(partial_kernel, members, bins),
-        out_shape=jax.ShapeDtypeStruct((members, sensors), F32),
+        out_shape=jax.ShapeDtypeStruct((members, width), F32),
         in_specs=[VMEM_SPEC] * 3,
         out_specs=VMEM_SPEC,
         scratch_shapes=[left],
         compiler_params=large,
         name="partial",
         cost_estimate=cost(1.2),
-    )(piece, spread_near, resp)
+    )(piece, made["near"], resp)
 
     field, finals = pl.pallas_call(
         functools.partial(update_kernel, members, bins),
@@ -350,16 +404,17 @@
             jax.ShapeDtypeStruct((members, bins, cells), F32),
             jax.ShapeDtypeStruct((batches * share, members), F32),
         ],
-        in_specs=[VMEM_SPEC] * 8,
+        in_specs=[VMEM_SPEC] * 7,
         out_specs=[HBM_SPEC, VMEM_SPEC],
         scratch_shapes=[
             left,
+            pltpu.VMEM((members + 16, sensors), F32),
             pltpu.VMEM((bins, members, cells), F32),
             pltpu.SemaphoreType.DMA((bins,)),
         ],
         compiler_params=large,
         name="update",
-    )(hx, other, spread_far, resp, observed.T, weight, pick, parts)
+    )(hx, other, made["far"], resp, made["obs"], weight, made["parts"])
     return (field, finals.reshape(batches, share, members).transpose(0, 2, 1))
 
 

time: 33.9 us -> 33.6 us (level)
  local copies, waits for them, and re-layouts: 0.22 us -> 0.95 us
  Pallas kernels: 18.9 us -> 18.2 us
    pallas_call x1, Pallas kernels: 11.8 us -> 10.8 us  [shards(): pl.pallas_call(functools.partial(update_kernel, members, bins), out_shape...]
    reshape x1, local copies, waits for them, and re-layouts: 0.01 us -> 0.74 us  [shards(): orders = batch_order.reshape(batches, P_SIZE)]
    pallas_call x0 -> x1, Pallas kernels: none -> 0.34 us  [obs_of(): pl.pallas_call(obs_kernel, out_shape=jax.ShapeDtypeStruct((2, sensors, me...]
  transfers between devices with their start and end apart: 6 -> 6, of which waited for: 4 -> 3; matrix products, arithmetic and copies ran while one was open for 1% -> 1% of each run, Pallas kernels for 15% -> 16%
where the time goes in v4:
time: 33.6 us; the launch traced here: 33.3 us
  Pallas kernels  18.2 us (54%)
  starting transfers between devices  11.8 us (35%)
  waiting for transfers between devices  1.52 us (5%)
  local copies, waits for them, and re-layouts  0.95 us (3%)
  between operations  0.79 us (2%)
    ppermute x6, starting transfers between devices, exchange(): return lax.ppermute(value, AXES, [(i, i ^ mask) for i in range(devices)])  11.8 us
    pallas_call x1, Pallas kernels, shards(): pl.pallas_call(functools.partial(update_kernel, members, bins), out_shape...  10.8 us
    pallas_call x1, Pallas kernels, shards(): pl.pallas_call(means_kernel, out_shape=jax.ShapeDtypeStruct((nb, rows), F...  2.17 us
    pallas_call x1, Pallas kernels, halves_of(): pl.pallas_call(halves_kernel, out_shape=jax.ShapeDtypeStruct((bins, 3 * m...  1.78 us
    ppermute x6, waiting for transfers between devices, exchange(): return lax.ppermute(value, AXES, [(i, i ^ mask) for i in range(devices)])  1.52 us
    pallas_call x1, Pallas kernels, shards(): pl.pallas_call(functools.partial(partial_kernel, members, bins), out_shap...  1.46 us
    pallas_call x2, Pallas kernels, spread_of(): pl.pallas_call(functools.partial(spread_kernel, bits, nb, first), out_sha...  1.29 us
    reshape x1, local copies, waits for them, and re-layouts, shards(): orders = batch_order.reshape(batches, P_SIZE)  0.74 us
  transfers between devices with their start and end apart: 6, of which 3 were waited for; matrix products, arithmetic and copies ran while one was open for 1% of the time, Pallas kernels for 16%

profile of v4, /device:TPU:1, one launch (start us, length us, event | category | flops | bytes accessed | tf_op | source)
XLA Modules:
  0.0 33.3 jit_solution(1232367290766251610)
XLA Ops:
  0.6 0.0 copy-start.3
  0.6 0.0 copy-start.2
  0.7 0.0 copy-start.4
  0.7 0.0 copy-start.1
  0.7 0.7 %reshape.23.orders_ref = s32[2,1024]{1,0:T(2,128)S(1)} reshape(s32[2048]{0:T(1024)} %param.15) | data formatting | bytes 16384 | tf_op jit(solution)/shard_map/reshape | solution.py:311
  1.4 2.2 %means.1 = f32[8,512]{1,0:T(8,128)S(1)} custom-call(f32[64,8,1024]{2,1,0:T(8,128)} %x_ref.2, f32[1,1024]{1,0:T(1,128)} %bitcast.15), custom_call_target="tpu_custom_call" | custom-call | tf_op jit(solution)/shard_map/means/pallas_call | solution.py:300
  3.6 0.0 copy-start
  3.6 3.2 %collective-permute-start = (f32[8,512]{1,0:T(8,128)S(1)}, f32[8,512]{1,0:T(8,128)S(1)}, u32[]{:S(2)}, u32[]{:S(2)}) collective-permute-start(f32[8,512]{1,0:T(8,128)S(1)} %means.1), channel_id=1, source_target_pairs={{0,16},{1,17},{2,18},{3,19},{4,20},{5,21},{6,22},{7,23},{8,24},{9,... | collective-permute-start | bytes 49160 | tf_op jit(solution)/shard_map/ppermute | solution.py:296
  6.8 0.1 constant_dynamic-slice_fusion
  6.9 0.1 reshape.25
  7.0 0.0 copy-done.3
  7.0 0.0 copy-done.2
  7.0 0.0 copy-done.4
  7.0 0.0 copy-done.1
  7.0 0.4 %roles.1 = (f32[2,2048]{1,0:T(2,128)S(1)}, s32[4,2176]{1,0:T(4,128)S(1)}, f32[4,2176]{1,0:T(4,128)S(1)}, f32[8,2176]{1,0:T(8,128)S(1)}) custom-call(s32[2,1024]{1,0:T(2,128)S(1)} %reshape.23.orders_ref, s32[1,128]{1,0:T(1,128)S(1)} %pad.4.own_ref, f32[16,128]{1,0:T(8,128)S(1)} %bitcast.14, s32[4,2048]{1,0:T(4,128)S(1)} %bitcast.12, f32[4,2048]{1,0:T(4,128)S(1)} %bitcast.13, ...), custom_call_target="tpu_custom_call" | custom-call | bytes 1800000 | tf_op jit(solution)/shard_map/roles/pallas_call | solution.py:315
  7.4 0.6 %spread.2.spread_ref = bf16[384,2176]{1,0:T(8,128)(2,1)S(1)} custom-call(s32[1]{0:T(128)} %bitcast.3.me_ref, s32[4,2176]{1,0:T(4,128)S(1)} %get-tuple-element.48.blocks_ref, f32[4,2176]{1,0:T(4,128)S(1)} %get-tuple-element.49.weight_ref), custom_call_target="tpu_custom_call" | custom-call | bytes 3000000 | tf_op jit(solution)/shard_map/spread/pallas_call | solution.py:285
  8.1 0.0 collective-permute-done
  8.1 1.4 %collective-permute-start.1 = (f32[16,512]{1,0:T(8,128)S(1)}, f32[16,512]{1,0:T(8,128)S(1)}, u32[]{:S(2)}, u32[]{:S(2)}) collective-permute-start(f32[16,512]{1,0:T(8,128)S(1)} %pad_maximum_fusion.1), channel_id=1, source_target_pairs={{0,8},{1,9},{2,10},{3,11},{4,12},{5,13},{6,14},{7,15},{8,0},{9,1},... | collective-permute-start | bytes 98312 | tf_op jit(solution)/shard_map/ppermute | solution.py:296
  9.5 0.6 %spread.3.spread_ref = bf16[384,2176]{1,0:T(8,128)(2,1)S(1)} custom-call(s32[1]{0:T(128)} %bitcast.3.me_ref, s32[4,2176]{1,0:T(4,128)S(1)} %get-tuple-element.48.blocks_ref, f32[4,2176]{1,0:T(4,128)S(1)} %get-tuple-element.49.weight_ref), custom_call_target="tpu_custom_call" | custom-call | bytes 3000000 | tf_op jit(solution)/shard_map/spread/pallas_call | solution.py:285
  10.1 0.8 %collective-permute-done.1 = f32[16,512]{1,0:T(8,128)S(1)} collective-permute-done((f32[16,512]{1,0:T(8,128)S(1)}, f32[16,512]{1,0:T(8,128)S(1)}, u32[]{:S(2)}, u32[]{:S(2)}) %collective-permute-start.1) | collective-permute-done | bytes 32800 | tf_op jit(solution)/shard_map/ppermute | solution.py:296
  11.0 2.2 %collective-permute-start.4 = (f32[32,512]{1,0:T(8,128)S(1)}, f32[32,512]{1,0:T(8,128)S(1)}, u32[]{:S(2)}, u32[]{:S(2)}) collective-permute-start(f32[32,512]{1,0:T(8,128)S(1)} %pad_maximum_fusion), channel_id=1, source_target_pairs={{0,6},{1,7},{2,4},{3,5},{4,2},{5,3},{6,0},{7,1},{8,14},{9,15},{10,... | collective-permute-start | bytes 196616 | tf_op jit(solution)/shard_map/ppermute | solution.py:296
  13.1 0.2 collective-permute-start.3
  13.3 0.3 collective-permute-start.2
  13.6 0.0 copy-done
  13.6 0.3 %observed.1.obs_ref = bf16[2,2048,64]{2,1,0:T(8,128)(2,1)S(1)} custom-call(f32[64,2048]{1,0:T(8,128)S(1)} %bitcast.10), custom_call_target="tpu_custom_call" | custom-call | bytes 1200000 | tf_op jit(solution)/shard_map/observed/pallas_call | solution.py:331
  14.0 1.8 %halves.1.x_ref = bf16[8,192,1024]{2,1,0:T(8,128)(2,1)S(1)} custom-call(f32[64,8,1024]{2,1,0:T(8,128)} %x_ref.2), custom_call_target="tpu_custom_call" | custom-call | bytes 4500000 | tf_op jit(solution)/shard_map/halves/pallas_call | solution.py:342
  15.8 0.0 collective-permute-done.4
  15.8 0.5 %collective-permute-done.3 = f32[32,512]{1,0:T(8,128)S(1)} collective-permute-done((f32[32,512]{1,0:T(8,128)S(1)}, f32[32,512]{1,0:T(8,128)S(1)}, u32[]{:S(2)}, u32[]{:S(2)}) %collective-permute-start.3) | collective-permute-done | bytes 65568 | tf_op jit(solution)/shard_map/ppermute | solution.py:296
  16.2 0.2 collective-permute-done.2
  16.5 4.6 %collective-permute-start.5 = (f32[128,512]{1,0:T(8,128)S(1)}, f32[128,512]{1,0:T(8,128)S(1)}, u32[]{:S(2)}, u32[]{:S(2)}) collective-permute-start(f32[128,512]{1,0:T(8,128)S(1)} %constant_dynamic-update-slice_fusion.gathered_ref), channel_id=1, source_target_pairs={{0,1},{1,0},{2,3},{3,2},{4,5},{5,4},{6,7},{7,6},{8,9},{9,8},{10,11... | collective-permute-start | bytes 786440 | tf_op jit(solution)/shard_map/ppermute | solution.py:296
  21.1 1.5 %partial.1.hx_ref = f32[64,2176]{1,0:T(8,128)S(1)} custom-call(f32[128,512]{1,0:T(8,128)S(1)} %constant_dynamic-update-slice_fusion.gathered_ref, bf16[384,2176]{1,0:T(8,128)(2,1)S(1)} %spread.2.spread_ref, f32[8,2176]{1,0:T(8,128)S(1)} %get-tuple-element.65.resp_ref), custom_call_target="tpu_custom_call" | custom-call | bytes 3600000 | tf_op jit(solution)/shard_map/partial/pallas_call | solution.py:390
  22.6 0.0 collective-permute-done.5.gathered_ref
  22.6 10.8 %update.1 = (f32[64,8,1024]{2,1,0:T(8,128)}, f32[64,64]{1,0:T(8,128)}) custom-call(f32[64,2176]{1,0:T(8,128)S(1)} %partial.1.hx_ref, f32[128,512]{1,0:T(8,128)S(1)} %collective-permute-done.5.gathered_ref, bf16[384,2176]{1,0:T(8,128)(2,1)S(1)} %spread.3.spread_ref, f32[8,2176]{1,0:T(8,128)S(1)} %get-tuple-element.65.resp_ref, ...), custom_call_target="tpu_custom_call" | custom-call | tf_op jit(solution)/shard_map/update/pallas_call | solution.py:401
  (7 shorter events, 0.0 us)
Async XLA Ops:
  0.6 6.3 %copy-start.3 = (f32[2048,4]{0,1:T(4,128)S(1)}, f32[2048,4]{0,1:T(4,128)}, u32[]{:S(2)}) copy-start(f32[2048,4]{0,1:T(4,128)} %param.11) | copy-start | bytes 98308
  0.6 6.3 %copy-start.2 = (s32[2048,4]{0,1:T(4,128)S(1)}, s32[2048,4]{0,1:T(4,128)}, u32[]{:S(2)}) copy-start(s32[2048,4]{0,1:T(4,128)} %param.10) | copy-start | bytes 98308
  0.7 6.3 %copy-start.4 = (f32[2048]{0:T(1024)S(1)}, f32[2048]{0:T(1024)}, u32[]{:S(2)}) copy-start(f32[2048]{0:T(1024)} %param.14) | copy-start | bytes 24580
  0.7 6.3 %copy-start.1 = (f32[2048,8]{0,1:T(8,128)S(1)}, f32[2048,8]{0,1:T(8,128)}, u32[]{:S(2)}) copy-start(f32[2048,8]{0,1:T(8,128)} %param.12) | copy-start | bytes 196612
  3.6 10.0 %copy-start = (f32[2048,64]{0,1:T(8,128)S(1)}, f32[2048,64]{0,1:T(8,128)}, u32[]{:S(2)}) copy-start(f32[2048,64]{0,1:T(8,128)} %param.13) | copy-start | bytes 1572868
  3.6 4.5 %collective-permute-start = (f32[8,512]{1,0:T(8,128)S(1)}, f32[8,512]{1,0:T(8,128)S(1)}, u32[]{:S(2)}, u32[]{:S(2)}) collective-permute-start(f32[8,512]{1,0:T(8,128)S(1)} %means.1), channel_id=1, source_target_pairs={{0,16},{1,17},{2,18},{3,19},{4,20},{5,21},{6,22},{7,23},{8,24},{9,... | collective-permute-start | bytes 49160 | tf_op jit(solution)/shard_map/ppermute | solution.py:296
  8.1 2.8 %collective-permute-start.1 = (f32[16,512]{1,0:T(8,128)S(1)}, f32[16,512]{1,0:T(8,128)S(1)}, u32[]{:S(2)}, u32[]{:S(2)}) collective-permute-start(f32[16,512]{1,0:T(8,128)S(1)} %pad_maximum_fusion.1), channel_id=1, source_target_pairs={{0,8},{1,9},{2,10},{3,11},{4,12},{5,13},{6,14},{7,15},{8,0},{9,1},... | collective-permute-start | bytes 98312 | tf_op jit(solution)/shard_map/ppermute | solution.py:296
  11.0 4.8 %collective-permute-start.4 = (f32[32,512]{1,0:T(8,128)S(1)}, f32[32,512]{1,0:T(8,128)S(1)}, u32[]{:S(2)}, u32[]{:S(2)}) collective-permute-start(f32[32,512]{1,0:T(8,128)S(1)} %pad_maximum_fusion), channel_id=1, source_target_pairs={{0,6},{1,7},{2,4},{3,5},{4,2},{5,3},{6,0},{7,1},{8,14},{9,15},{10,... | collective-permute-start | bytes 196616 | tf_op jit(solution)/shard_map/ppermute | solution.py:296
  13.1 3.1 %collective-permute-start.3 = (f32[32,512]{1,0:T(8,128)S(1)}, f32[32,512]{1,0:T(8,128)S(1)}, u32[]{:S(2)}, u32[]{:S(2)}) collective-permute-start(f32[32,512]{1,0:T(8,128)S(1)} %pad_maximum_fusion), channel_id=1, source_target_pairs={{0,4},{1,5},{2,6},{3,7},{4,0},{5,1},{6,2},{7,3},{8,12},{9,13},{10,... | collective-permute-start | bytes 196616 | tf_op jit(solution)/shard_map/ppermute | solution.py:296
  13.3 3.1 %collective-permute-start.2 = (f32[32,512]{1,0:T(8,128)S(1)}, f32[32,512]{1,0:T(8,128)S(1)}, u32[]{:S(2)}, u32[]{:S(2)}) collective-permute-start(f32[32,512]{1,0:T(8,128)S(1)} %pad_maximum_fusion), channel_id=1, source_target_pairs={{0,2},{1,3},{2,0},{3,1},{4,6},{5,7},{6,4},{7,5},{8,10},{9,11},{10,... | collective-permute-start | bytes 196616 | tf_op jit(solution)/shard_map/ppermute | solution.py:296
  16.5 6.1 %collective-permute-start.5 = (f32[128,512]{1,0:T(8,128)S(1)}, f32[128,512]{1,0:T(8,128)S(1)}, u32[]{:S(2)}, u32[]{:S(2)}) collective-permute-start(f32[128,512]{1,0:T(8,128)S(1)} %constant_dynamic-update-slice_fusion.gathered_ref), channel_id=1, source_target_pairs={{0,1},{1,0},{2,3},{3,2},{4,5},{5,4},{6,7},{7,6},{8,9},{9,8},{10,11... | collective-permute-start | bytes 786440 | tf_op jit(solution)/shard_map/ppermute | solution.py:296

commit v5 on v4

--- a/solution.py
+++ b/solution.py
@@ -96,22 +96,34 @@
         out_ref[b, 2 * members : 3 * members, :] = hi
 
 
-def roles_kernel(orders_ref, own_ref, var_ref, blocks_ref, foot_ref, resp_ref, weight_ref, *table_refs):
-    batches, per = orders_ref.shape
+def roles_kernel(share, me_ref, orders_ref, var_ref, blocks_ref, foot_ref, resp_ref, weight_ref, *table_refs):
+    batches = weight_ref.shape[0]
     groups = var_ref.shape[0]
+    each = groups // batches
+    per = each * 128
     sensors = blocks_ref.shape[1]
+    start = me_ref[0] * share
+    lane = lax.broadcasted_iota(jnp.int32, (8, 128), 1)
+    own = jnp.full((8, 128), -1, jnp.int32)
     inverse = 1.0 / var_ref[...]
     high = lax.broadcasted_iota(jnp.int32, (groups, per), 0)
     low = lax.broadcasted_iota(jnp.int32, (128, per), 0)
     for t in range(batches):
-        order = orders_ref[t : t + 1, :]
+        order = jnp.concatenate(
+            [orders_ref[g : g + 1, :] for g in range(t * each, (t + 1) * each)], axis=1
+        )
+        mine = orders_ref[pl.ds(t * each + lax.shift_right_logical(start, 7), 1), :]
+        mine = pltpu.roll(
+            jnp.broadcast_to(mine, (8, 128)), (t * share - (start & 127)) & 127, axis=1
+        )
+        own = jnp.where((lane >= t * share) & (lane < (t + 1) * share), mine, own)
         of_high = jnp.where(high == lax.shift_right_logical(order, 7), 1.0, 0.0).astype(BF16)
         of_low = jnp.where(low == (order & 127), 1.0, 0.0).astype(BF16)
         held = lax.dot_general(of_high, of_low, NT, preferred_element_type=F32) * inverse
         for g in range(groups):
             weight_ref[t : t + 1, g * 128 : (g + 1) * 128] = held[g : g + 1, :]
     sensor = lax.broadcasted_iota(jnp.int32, (sensors, 128), 0)
-    pick = jnp.where(sensor == own_ref[...], 1.0, 0.0).astype(BF16)
+    pick = jnp.where(sensor == own[0:1, :], 1.0, 0.0).astype(BF16)
     tables = jnp.concatenate(
         [blocks_ref[...].astype(F32), foot_ref[...], resp_ref[...]], axis=0
     )
@@ -123,19 +135,21 @@
         jnp.concatenate([first, second, third], axis=0), pick, preferred_element_type=F32
     )
     n = tables.shape[0]
-    own = stacked[0:n] + stacked[n : 2 * n] + stacked[2 * n : 3 * n]
+    chosen = stacked[0:n] + stacked[n : 2 * n] + stacked[2 * n : 3 * n]
     at = 0
     for ref, table in zip(table_refs, (blocks_ref, foot_ref, resp_ref)):
         rows = table.shape[0]
         ref[:, 0:sensors] = table[...]
-        ref[:, sensors : sensors + 128] = own[at : at + rows].astype(ref.dtype)
+        ref[:, sensors : sensors + 128] = chosen[at : at + rows].astype(ref.dtype)
         at += rows
 
 
 def obs_kernel(obs_ref, out_ref):
+    members = obs_ref.shape[0]
     step = 128
     for c in range(0, obs_ref.shape[1], step):
-        hi, low = split(obs_ref[:, c : c + step].T)
+        turned = obs_ref[:, c : c + step].T
+        hi, low = split(jnp.concatenate([jnp.zeros_like(turned), turned], axis=1))
         out_ref[0, c : c + step, :] = hi
         out_ref[1, c : c + step, :] = low
 
@@ -166,34 +180,34 @@
 
 
 def solve(aug):
-    n = aug.shape[0]
-    width = aug.shape[1]
-    rows = [aug[8 * i : 8 * i + 8, :] for i in range(n // 8)]
-    sub = lax.broadcasted_iota(jnp.int32, (8, width), 0)
+    n, width = aug.shape
+    p = 16
+    blocks = n // p
+    rows = [aug[p * i : p * i + p, :] for i in range(blocks)]
+    sub = lax.broadcasted_iota(jnp.int32, (p, width), 0)
 
     def lanes(x, j):
-        return jnp.broadcast_to(x[:, j : j + 1], (8, width))
-
-    for k in range(n // 8):
+        return jnp.broadcast_to(x[:, j : j + 1], (p, width))
+
+    for k in range(blocks):
         piv = rows[k]
-        own = [lanes(piv, 8 * k + q) for q in range(8)]
-        for q in range(8):
+        own = [lanes(piv, p * k + q) for q in range(p)]
+        for q in range(p):
             here = sub == q
             mult = own[q]
             inv = 1.0 / mult[q : q + 1, :]
             scaled = piv[q : q + 1, :] * inv
             piv = jnp.where(here, scaled, piv - mult * scaled)
-            for p in range(q + 1, 8):
-                scaled = own[p][q : q + 1, :] * inv
-                own[p] = jnp.where(here, scaled, own[p] - mult * scaled)
-        for i in range(n // 8):
-            if i != k:
-                new = rows[i]
-                for q in range(8):
-                    new = new - lanes(rows[i], 8 * k + q) * piv[q : q + 1, :]
-                rows[i] = new
+            for r in range(q + 1, p):
+                scaled = own[r][q : q + 1, :] * inv
+                own[r] = jnp.where(here, scaled, own[r] - mult * scaled)
+        for i in list(range(k + 1, blocks)) + list(range(k)):
+            new = rows[i]
+            for q in range(p):
+                new = new - lanes(rows[i], p * k + q) * piv[q : q + 1, :]
+            rows[i] = new
         rows[k] = piv
-    return jnp.concatenate(rows, axis=0)[:, n:]
+    return jnp.concatenate(rows, axis=0)
 
 
 def update_kernel(
@@ -224,32 +238,41 @@
         jnp.dot(whi, obs_ref[0], preferred_element_type=F32)
         + jnp.dot(wlo, obs_ref[0], preferred_element_type=F32)
         + jnp.dot(whi, obs_ref[1], preferred_element_type=F32)
-        - sums[:, members : members + 1]
-    )
-    r64 = lax.broadcasted_iota(jnp.int32, (members, members), 0)
-    c64 = lax.broadcasted_iota(jnp.int32, (members, members), 1)
-    eye = (r64 == c64).astype(F32)
-    s0, e0 = sums[0:members, 0:members], pulls[0:members]
-    s1, e1 = sums[members:, 0:members], pulls[members:]
-    gain = solve(jnp.concatenate([s0 + (members - 1.0) * eye, e0 - s0], axis=1))
-    first_t = eye + gain - sublane_mean(gain)
-    first_ct = first_t - lane_mean(first_t)
-    first = first_t.T
+    )
+    lane = lax.broadcasted_iota(jnp.int32, (2 * members, 2 * members), 1)
+    wide_sums = jnp.concatenate(
+        [sums, jnp.zeros((2 * members, 2 * members - sums.shape[1]), F32)], axis=1
+    )
+    base = jnp.where(lane < members, wide_sums, pulls - sums[:, members : members + 1])
+    lane = lane[0:members]
+    right = lane >= members
+    row = lax.broadcasted_iota(jnp.int32, lane.shape, 0)
+    prior = jnp.where((lane == row) | (lane == row + members), members - 1.0, 0.0)
+    even = jnp.where(right, 1.0 / members, 0.0)
+
+    def mixer_t(solved):
+        held = jnp.where(right, solved, 0.0)
+        return held - sublane_mean(held) + even
+
+    first_t = mixer_t(solve(base[0:members] + prior))
+    tilt = jnp.sum(first_t, axis=1, keepdims=True) * (1.0 / members)
+    first = first_t.T[members:, :]
     first_c = first - sublane_mean(first)
-    prod = mm(s1, jnp.concatenate([first_ct, first_t], axis=1))
-    aug = mm(first_c, jnp.concatenate([prod[:, 0:members], e1 - prod[:, members:]], axis=1))
-    gain = solve(
-        jnp.concatenate([aug[:, 0:members] + (members - 1.0) * eye, aug[:, members:]], axis=1)
-    )
-    total = first + mm(gain.T, first_c)
+    moved = mm(first_c, base[members:])
+    swapped = pltpu.roll(first_t, members, axis=1) - tilt
+    crossed = mm(moved[:, 0:members], jnp.where(right, tilt, swapped))
+    second_t = mixer_t(
+        solve(prior + jnp.where(right, moved - crossed, crossed))
+    )
+    total = mm(second_t.T[members:, :], jnp.concatenate([first, first], axis=1))
     thi, tlo = split(total)
-    lhs = jnp.concatenate([thi, thi, tlo], axis=1)
+    lhs = jnp.concatenate([thi, tlo[:, 0:members]], axis=1)
     copies = []
     for b in range(bins):
         out[b] = jnp.dot(lhs, x_ref[b], preferred_element_type=F32)
         copies.append(pltpu.make_async_copy(out.at[b], field_ref.at[:, b, :], sems.at[b]))
         copies[-1].start()
-    finals_ref[...] = mm(total, picked).T[0 : finals_ref.shape[0], :]
+    finals_ref[...] = mm(total[:, 0:members], picked).T[0 : finals_ref.shape[0], :]
     for copy in copies:
         copy.wait()
 
@@ -308,19 +331,19 @@
     )(far_state, pltpu.with_memory_space_constraint(kernel.reshape(1, cells), pltpu.HBM))
 
     who, places, weights = me.reshape(1), blocks.T, foot_weight.T
-    orders = batch_order.reshape(batches, P_SIZE)
+    orders = batch_order.reshape(sensors // 128, 128)
     inverse = obs_var.reshape(sensors // 128, 128)
 
     def roles_of(*args):
         return pl.pallas_call(
-            roles_kernel,
+            functools.partial(roles_kernel, share),
             out_shape=[
                 jax.ShapeDtypeStruct((batches, sensors), F32),
                 jax.ShapeDtypeStruct((blocks.shape[1], width), jnp.int32),
                 jax.ShapeDtypeStruct((blocks.shape[1], width), F32),
                 jax.ShapeDtypeStruct((bins, width), F32),
             ],
-            in_specs=[VMEM_SPEC] * 6,
+            in_specs=[SMEM_SPEC] + [VMEM_SPEC] * 5,
             out_specs=[VMEM_SPEC] * 4,
             compiler_params=small,
             name="roles",
@@ -330,7 +353,7 @@
     def obs_of(observed):
         return pl.pallas_call(
             obs_kernel,
-            out_shape=jax.ShapeDtypeStruct((2, sensors, members), BF16),
+            out_shape=jax.ShapeDtypeStruct((2, sensors, 2 * members), BF16),
             in_specs=[VMEM_SPEC],
             out_specs=VMEM_SPEC,
             compiler_params=small,
@@ -353,9 +376,7 @@
     made = {}
 
     def first_work():
-        own = lax.dynamic_slice_in_dim(orders, me * share, share, 1).reshape(1, batches * share)
-        own = jnp.pad(own, ((0, 0), (0, 128 - batches * share)), constant_values=-1)
-        made["roles"] = roles_of(orders, own, inverse, places, weights, bin_response.T)
+        made["roles"] = roles_of(who, orders, inverse, places, weights, bin_response.T)
         made["near"] = spread_of(0, who, *made["roles"][1:3])
 
     def second_work():

time: 33.6 us -> 30.8 us (0.917)
  Pallas kernels: 18.2 us -> 16.5 us
  local copies, waits for them, and re-layouts: 0.95 us -> 0.05 us
    pallas_call x1, Pallas kernels: 10.8 us -> 8.7 us  [shards(): pl.pallas_call(functools.partial(update_kernel, members, bins), out_shape...]
    reshape x2 -> x0, local copies, waits for them, and re-layouts: 0.82 us -> none  [the longest x1 0.74 us: shards(): orders = batch_order.reshape(batches, P_SIZE)]
  transfers between devices with their start and end apart: 6 -> 6, of which waited for: 3 -> 3; matrix products, arithmetic and copies ran while one was open for 1% -> 0% of each run, Pallas kernels for 16% -> 18%
where the time goes in v5:
time: 30.8 us; the launch traced here: 30.6 us
  Pallas kernels  16.5 us (54%)
  starting transfers between devices  12 us (39%)
  waiting for transfers between devices  1.27 us (4%)
  between operations  0.78 us (3%)
    ppermute x6, starting transfers between devices, exchange(): return lax.ppermute(value, AXES, [(i, i ^ mask) for i in range(devices)])  12 us
    pallas_call x1, Pallas kernels, shards(): pl.pallas_call(functools.partial(update_kernel, members, bins), out_shape...  8.7 us
    pallas_call x1, Pallas kernels, shards(): pl.pallas_call(means_kernel, out_shape=jax.ShapeDtypeStruct((nb, rows), F...  2.21 us
    pallas_call x1, Pallas kernels, halves_of(): pl.pallas_call(halves_kernel, out_shape=jax.ShapeDtypeStruct((bins, 3 * m...  1.78 us
    pallas_call x1, Pallas kernels, shards(): pl.pallas_call(functools.partial(partial_kernel, members, bins), out_shap...  1.46 us
    pallas_call x2, Pallas kernels, spread_of(): pl.pallas_call(functools.partial(spread_kernel, bits, nb, first), out_sha...  1.29 us
    ppermute x6, waiting for transfers between devices, exchange(): return lax.ppermute(value, AXES, [(i, i ^ mask) for i in range(devices)])  1.27 us
    pallas_call x1, Pallas kernels, obs_of(): pl.pallas_call(obs_kernel, out_shape=jax.ShapeDtypeStruct((2, sensors, 2...  0.63 us
  transfers between devices with their start and end apart: 6, of which 3 were waited for; matrix products, arithmetic and copies ran while one was open for 0% of the time, Pallas kernels for 18%

profile of v5, /device:TPU:1, one launch (start us, length us, event | category | flops | bytes accessed | tf_op | source)
XLA Modules:
  0.0 30.6 jit_solution(287296944557539869)
XLA Ops:
  0.6 0.0 copy-start.4
  0.6 0.0 copy-start.3
  0.7 0.0 copy-start.2
  0.7 0.0 copy-start.5
  0.7 0.0 copy-start.1
  0.7 2.2 %means.1 = f32[8,512]{1,0:T(8,128)S(1)} custom-call(f32[64,8,1024]{2,1,0:T(8,128)} %x_ref.2, f32[1,1024]{1,0:T(1,128)} %bitcast.17), custom_call_target="tpu_custom_call" | custom-call | tf_op jit(solution)/shard_map/means/pallas_call | solution.py:323
  2.9 0.0 copy-start
  2.9 3.2 %collective-permute-start = (f32[8,512]{1,0:T(8,128)S(1)}, f32[8,512]{1,0:T(8,128)S(1)}, u32[]{:S(2)}, u32[]{:S(2)}) collective-permute-start(f32[8,512]{1,0:T(8,128)S(1)} %means.1), channel_id=1, source_target_pairs={{0,16},{1,17},{2,18},{3,19},{4,20},{5,21},{6,22},{7,23},{8,24},{9,... | collective-permute-start | bytes 49160 | tf_op jit(solution)/shard_map/ppermute | solution.py:319
  6.1 0.0 copy-done.4
  6.1 0.0 copy-done.3
  6.1 0.0 copy-done.2
  6.1 0.0 copy-done.5
  6.1 0.0 copy-done.1
  6.1 0.4 %roles.1 = (f32[2,2048]{1,0:T(2,128)S(1)}, s32[4,2176]{1,0:T(4,128)S(1)}, f32[4,2176]{1,0:T(4,128)S(1)}, f32[8,2176]{1,0:T(8,128)S(1)}) custom-call(s32[1]{0:T(128)} %bitcast.4.me_ref, s32[16,128]{1,0:T(8,128)S(1)} %bitcast.15, f32[16,128]{1,0:T(8,128)S(1)} %bitcast.16, s32[4,2048]{1,0:T(4,128)S(1)} %bitcast.13, f32[4,2048]{1,0:T(4,128)S(1)} %bitcast.14, ...), custom_call_target="tpu_custom_call" | custom-call | bytes 1800000 | tf_op jit(solution)/shard_map/roles/pallas_call | solution.py:338
  6.6 0.6 %spread.2.spread_ref = bf16[384,2176]{1,0:T(8,128)(2,1)S(1)} custom-call(s32[1]{0:T(128)} %bitcast.4.me_ref, s32[4,2176]{1,0:T(4,128)S(1)} %get-tuple-element.48.blocks_ref, f32[4,2176]{1,0:T(4,128)S(1)} %get-tuple-element.49.weight_ref), custom_call_target="tpu_custom_call" | custom-call | bytes 3000000 | tf_op jit(solution)/shard_map/spread/pallas_call | solution.py:308
  7.2 0.0 collective-permute-done
  7.3 1.3 %collective-permute-start.1 = (f32[16,512]{1,0:T(8,128)S(1)}, f32[16,512]{1,0:T(8,128)S(1)}, u32[]{:S(2)}, u32[]{:S(2)}) collective-permute-start(f32[16,512]{1,0:T(8,128)S(1)} %pad_maximum_fusion.1), channel_id=1, source_target_pairs={{0,8},{1,9},{2,10},{3,11},{4,12},{5,13},{6,14},{7,15},{8,0},{9,1},... | collective-permute-start | bytes 98312 | tf_op jit(solution)/shard_map/ppermute | solution.py:319
  8.6 0.6 %spread.3.spread_ref = bf16[384,2176]{1,0:T(8,128)(2,1)S(1)} custom-call(s32[1]{0:T(128)} %bitcast.4.me_ref, s32[4,2176]{1,0:T(4,128)S(1)} %get-tuple-element.48.blocks_ref, f32[4,2176]{1,0:T(4,128)S(1)} %get-tuple-element.49.weight_ref), custom_call_target="tpu_custom_call" | custom-call | bytes 3000000 | tf_op jit(solution)/shard_map/spread/pallas_call | solution.py:308
  9.3 0.8 %collective-permute-done.1 = f32[16,512]{1,0:T(8,128)S(1)} collective-permute-done((f32[16,512]{1,0:T(8,128)S(1)}, f32[16,512]{1,0:T(8,128)S(1)}, u32[]{:S(2)}, u32[]{:S(2)}) %collective-permute-start.1) | collective-permute-done | bytes 32800 | tf_op jit(solution)/shard_map/ppermute | solution.py:319
  10.1 2.2 %collective-permute-start.4 = (f32[32,512]{1,0:T(8,128)S(1)}, f32[32,512]{1,0:T(8,128)S(1)}, u32[]{:S(2)}, u32[]{:S(2)}) collective-permute-start(f32[32,512]{1,0:T(8,128)S(1)} %pad_maximum_fusion), channel_id=1, source_target_pairs={{0,6},{1,7},{2,4},{3,5},{4,2},{5,3},{6,0},{7,1},{8,14},{9,15},{10,... | collective-permute-start | bytes 196616 | tf_op jit(solution)/shard_map/ppermute | solution.py:319
  12.2 0.2 collective-permute-start.3
  12.5 0.3 collective-permute-start.2
  12.7 0.0 copy-done
  12.7 0.6 %observed.1.obs_ref = bf16[2,2048,128]{2,1,0:T(8,128)(2,1)S(1)} custom-call(f32[64,2048]{1,0:T(8,128)S(1)} %bitcast.11), custom_call_target="tpu_custom_call" | custom-call | bytes 1200000 | tf_op jit(solution)/shard_map/observed/pallas_call | solution.py:354
  13.4 1.8 %halves.1.x_ref = bf16[8,192,1024]{2,1,0:T(8,128)(2,1)S(1)} custom-call(f32[64,8,1024]{2,1,0:T(8,128)} %x_ref.2), custom_call_target="tpu_custom_call" | custom-call | bytes 4500000 | tf_op jit(solution)/shard_map/halves/pallas_call | solution.py:365
  15.2 0.0 collective-permute-done.4
  15.2 0.2 collective-permute-done.3
  15.4 0.2 collective-permute-done.2
  15.6 4.8 %collective-permute-start.5 = (f32[128,512]{1,0:T(8,128)S(1)}, f32[128,512]{1,0:T(8,128)S(1)}, u32[]{:S(2)}, u32[]{:S(2)}) collective-permute-start(f32[128,512]{1,0:T(8,128)S(1)} %constant_dynamic-update-slice_fusion.gathered_ref), channel_id=1, source_target_pairs={{0,1},{1,0},{2,3},{3,2},{4,5},{5,4},{6,7},{7,6},{8,9},{9,8},{10,11... | collective-permute-start | bytes 786440 | tf_op jit(solution)/shard_map/ppermute | solution.py:319
  20.4 1.5 %partial.1.hx_ref = f32[64,2176]{1,0:T(8,128)S(1)} custom-call(f32[128,512]{1,0:T(8,128)S(1)} %constant_dynamic-update-slice_fusion.gathered_ref, bf16[384,2176]{1,0:T(8,128)(2,1)S(1)} %spread.2.spread_ref, f32[8,2176]{1,0:T(8,128)S(1)} %get-tuple-element.65.resp_ref), custom_call_target="tpu_custom_call" | custom-call | bytes 3600000 | tf_op jit(solution)/shard_map/partial/pallas_call | solution.py:411
  21.9 0.0 collective-permute-done.5.gathered_ref
  21.9 8.7 %update.1 = (f32[64,8,1024]{2,1,0:T(8,128)}, f32[64,64]{1,0:T(8,128)}) custom-call(f32[64,2176]{1,0:T(8,128)S(1)} %partial.1.hx_ref, f32[128,512]{1,0:T(8,128)S(1)} %collective-permute-done.5.gathered_ref, bf16[384,2176]{1,0:T(8,128)(2,1)S(1)} %spread.3.spread_ref, f32[8,2176]{1,0:T(8,128)S(1)} %get-tuple-element.65.resp_ref, ...), custom_call_target="tpu_custom_call" | custom-call | tf_op jit(solution)/shard_map/update/pallas_call | solution.py:422
  (6 shorter events, 0.0 us)
Async XLA Ops:
  0.6 5.5 %copy-start.4 = (s32[2048]{0:T(1024)S(1)}, s32[2048]{0:T(1024)}, u32[]{:S(2)}) copy-start(s32[2048]{0:T(1024)} %param.15) | copy-start | bytes 24580
  0.6 5.5 %copy-start.3 = (f32[2048,4]{0,1:T(4,128)S(1)}, f32[2048,4]{0,1:T(4,128)}, u32[]{:S(2)}) copy-start(f32[2048,4]{0,1:T(4,128)} %param.11) | copy-start | bytes 98308
  0.7 5.5 %copy-start.2 = (s32[2048,4]{0,1:T(4,128)S(1)}, s32[2048,4]{0,1:T(4,128)}, u32[]{:S(2)}) copy-start(s32[2048,4]{0,1:T(4,128)} %param.10) | copy-start | bytes 98308
  0.7 5.5 %copy-start.5 = (f32[2048]{0:T(1024)S(1)}, f32[2048]{0:T(1024)}, u32[]{:S(2)}) copy-start(f32[2048]{0:T(1024)} %param.14) | copy-start | bytes 24580
  0.7 5.5 %copy-start.1 = (f32[2048,8]{0,1:T(8,128)S(1)}, f32[2048,8]{0,1:T(8,128)}, u32[]{:S(2)}) copy-start(f32[2048,8]{0,1:T(8,128)} %param.12) | copy-start | bytes 196612
  2.9 9.8 %copy-start = (f32[2048,64]{0,1:T(8,128)S(1)}, f32[2048,64]{0,1:T(8,128)}, u32[]{:S(2)}) copy-start(f32[2048,64]{0,1:T(8,128)} %param.13) | copy-start | bytes 1572868
  2.9 4.3 %collective-permute-start = (f32[8,512]{1,0:T(8,128)S(1)}, f32[8,512]{1,0:T(8,128)S(1)}, u32[]{:S(2)}, u32[]{:S(2)}) collective-permute-start(f32[8,512]{1,0:T(8,128)S(1)} %means.1), channel_id=1, source_target_pairs={{0,16},{1,17},{2,18},{3,19},{4,20},{5,21},{6,22},{7,23},{8,24},{9,... | collective-permute-start | bytes 49160 | tf_op jit(solution)/shard_map/ppermute | solution.py:319
  7.3 2.8 %collective-permute-start.1 = (f32[16,512]{1,0:T(8,128)S(1)}, f32[16,512]{1,0:T(8,128)S(1)}, u32[]{:S(2)}, u32[]{:S(2)}) collective-permute-start(f32[16,512]{1,0:T(8,128)S(1)} %pad_maximum_fusion.1), channel_id=1, source_target_pairs={{0,8},{1,9},{2,10},{3,11},{4,12},{5,13},{6,14},{7,15},{8,0},{9,1},... | collective-permute-start | bytes 98312 | tf_op jit(solution)/shard_map/ppermute | solution.py:319
  10.1 5.1 %collective-permute-start.4 = (f32[32,512]{1,0:T(8,128)S(1)}, f32[32,512]{1,0:T(8,128)S(1)}, u32[]{:S(2)}, u32[]{:S(2)}) collective-permute-start(f32[32,512]{1,0:T(8,128)S(1)} %pad_maximum_fusion), channel_id=1, source_target_pairs={{0,6},{1,7},{2,4},{3,5},{4,2},{5,3},{6,0},{7,1},{8,14},{9,15},{10,... | collective-permute-start | bytes 196616 | tf_op jit(solution)/shard_map/ppermute | solution.py:319
  12.2 3.1 %collective-permute-start.3 = (f32[32,512]{1,0:T(8,128)S(1)}, f32[32,512]{1,0:T(8,128)S(1)}, u32[]{:S(2)}, u32[]{:S(2)}) collective-permute-start(f32[32,512]{1,0:T(8,128)S(1)} %pad_maximum_fusion), channel_id=1, source_target_pairs={{0,4},{1,5},{2,6},{3,7},{4,0},{5,1},{6,2},{7,3},{8,12},{9,13},{10,... | collective-permute-start | bytes 196616 | tf_op jit(solution)/shard_map/ppermute | solution.py:319
  12.5 3.1 %collective-permute-start.2 = (f32[32,512]{1,0:T(8,128)S(1)}, f32[32,512]{1,0:T(8,128)S(1)}, u32[]{:S(2)}, u32[]{:S(2)}) collective-permute-start(f32[32,512]{1,0:T(8,128)S(1)} %pad_maximum_fusion), channel_id=1, source_target_pairs={{0,2},{1,3},{2,0},{3,1},{4,6},{5,7},{6,4},{7,5},{8,10},{9,11},{10,... | collective-permute-start | bytes 196616 | tf_op jit(solution)/shard_map/ppermute | solution.py:319
  15.6 6.3 %collective-permute-start.5 = (f32[128,512]{1,0:T(8,128)S(1)}, f32[128,512]{1,0:T(8,128)S(1)}, u32[]{:S(2)}, u32[]{:S(2)}) collective-permute-start(f32[128,512]{1,0:T(8,128)S(1)} %constant_dynamic-update-slice_fusion.gathered_ref), channel_id=1, source_target_pairs={{0,1},{1,0},{2,3},{3,2},{4,5},{5,4},{6,7},{7,6},{8,9},{9,8},{10,11... | collective-permute-start | bytes 786440 | tf_op jit(solution)/shard_map/ppermute | solution.py:319

commit v6 on v5

--- a/solution.py
+++ b/solution.py
@@ -268,10 +268,13 @@
     thi, tlo = split(total)
     lhs = jnp.concatenate([thi, tlo[:, 0:members]], axis=1)
     copies = []
-    for b in range(bins):
-        out[b] = jnp.dot(lhs, x_ref[b], preferred_element_type=F32)
-        copies.append(pltpu.make_async_copy(out.at[b], field_ref.at[:, b, :], sems.at[b]))
-        copies[-1].start()
+    for first_bin in range(0, bins, bins // 2):
+        group = range(first_bin, first_bin + bins // 2)
+        for b in group:
+            out[b] = jnp.dot(lhs, x_ref[b], preferred_element_type=F32)
+        for b in group:
+            copies.append(pltpu.make_async_copy(out.at[b], field_ref.at[:, b, :], sems.at[b]))
+            copies[-1].start()
     finals_ref[...] = mm(total[:, 0:members], picked).T[0 : finals_ref.shape[0], :]
     for copy in copies:
         copy.wait()

time: 30.8 us -> 30.3 us (0.984)
  Pallas kernels: 16.5 us -> 16 us
    pallas_call x1, Pallas kernels: 8.7 us -> 8.25 us  [shards(): pl.pallas_call(functools.partial(update_kernel, members, bins), out_shape...]
  transfers between devices with their start and end apart: 6 -> 6, of which waited for: 3 -> 3; matrix products, arithmetic and copies ran while one was open for 0% -> 0% of each run, Pallas kernels for 18% -> 19%
where the time goes in v6:
time: 30.3 us; the launch traced here: 30.1 us
  Pallas kernels  16 us (53%)
  starting transfers between devices  12 us (40%)
  waiting for transfers between devices  1.27 us (4%)
  between operations  0.78 us (3%)
    ppermute x6, starting transfers between devices, exchange(): return lax.ppermute(value, AXES, [(i, i ^ mask) for i in range(devices)])  12 us
    pallas_call x1, Pallas kernels, shards(): pl.pallas_call(functools.partial(update_kernel, members, bins), out_shape...  8.25 us
    pallas_call x1, Pallas kernels, shards(): pl.pallas_call(means_kernel, out_shape=jax.ShapeDtypeStruct((nb, rows), F...  2.21 us
    pallas_call x1, Pallas kernels, halves_of(): pl.pallas_call(halves_kernel, out_shape=jax.ShapeDtypeStruct((bins, 3 * m...  1.78 us
    pallas_call x1, Pallas kernels, shards(): pl.pallas_call(functools.partial(partial_kernel, members, bins), out_shap...  1.46 us
    pallas_call x2, Pallas kernels, spread_of(): pl.pallas_call(functools.partial(spread_kernel, bits, nb, first), out_sha...  1.29 us
    ppermute x6, waiting for transfers between devices, exchange(): return lax.ppermute(value, AXES, [(i, i ^ mask) for i in range(devices)])  1.27 us
    pallas_call x1, Pallas kernels, obs_of(): pl.pallas_call(obs_kernel, out_shape=jax.ShapeDtypeStruct((2, sensors, 2...  0.63 us
  transfers between devices with their start and end apart: 6, of which 3 were waited for; matrix products, arithmetic and copies ran while one was open for 0% of the time, Pallas kernels for 19%

profile of v6, /device:TPU:1, one launch (start us, length us, event | category | flops | bytes accessed | tf_op | source)
XLA Modules:
  0.0 30.1 jit_solution(5355848911763249157)
XLA Ops:
  0.6 0.0 copy-start.4
  0.6 0.0 copy-start.3
  0.7 0.0 copy-start.2
  0.7 0.0 copy-start.5
  0.7 0.0 copy-start.1
  0.7 2.2 %means.1 = f32[8,512]{1,0:T(8,128)S(1)} custom-call(f32[64,8,1024]{2,1,0:T(8,128)} %x_ref.2, f32[1,1024]{1,0:T(1,128)} %bitcast.17), custom_call_target="tpu_custom_call" | custom-call | tf_op jit(solution)/shard_map/means/pallas_call | solution.py:326
  2.9 0.0 copy-start
  2.9 3.2 %collective-permute-start = (f32[8,512]{1,0:T(8,128)S(1)}, f32[8,512]{1,0:T(8,128)S(1)}, u32[]{:S(2)}, u32[]{:S(2)}) collective-permute-start(f32[8,512]{1,0:T(8,128)S(1)} %means.1), channel_id=1, source_target_pairs={{0,16},{1,17},{2,18},{3,19},{4,20},{5,21},{6,22},{7,23},{8,24},{9,... | collective-permute-start | bytes 49160 | tf_op jit(solution)/shard_map/ppermute | solution.py:322
  6.1 0.0 copy-done.4
  6.1 0.0 copy-done.3
  6.1 0.0 copy-done.2
  6.1 0.0 copy-done.5
  6.1 0.0 copy-done.1
  6.1 0.4 %roles.1 = (f32[2,2048]{1,0:T(2,128)S(1)}, s32[4,2176]{1,0:T(4,128)S(1)}, f32[4,2176]{1,0:T(4,128)S(1)}, f32[8,2176]{1,0:T(8,128)S(1)}) custom-call(s32[1]{0:T(128)} %bitcast.4.me_ref, s32[16,128]{1,0:T(8,128)S(1)} %bitcast.15, f32[16,128]{1,0:T(8,128)S(1)} %bitcast.16, s32[4,2048]{1,0:T(4,128)S(1)} %bitcast.13, f32[4,2048]{1,0:T(4,128)S(1)} %bitcast.14, ...), custom_call_target="tpu_custom_call" | custom-call | bytes 1800000 | tf_op jit(solution)/shard_map/roles/pallas_call | solution.py:341
  6.6 0.6 %spread.2.spread_ref = bf16[384,2176]{1,0:T(8,128)(2,1)S(1)} custom-call(s32[1]{0:T(128)} %bitcast.4.me_ref, s32[4,2176]{1,0:T(4,128)S(1)} %get-tuple-element.48.blocks_ref, f32[4,2176]{1,0:T(4,128)S(1)} %get-tuple-element.49.weight_ref), custom_call_target="tpu_custom_call" | custom-call | bytes 3000000 | tf_op jit(solution)/shard_map/spread/pallas_call | solution.py:311
  7.2 0.0 collective-permute-done
  7.3 1.3 %collective-permute-start.1 = (f32[16,512]{1,0:T(8,128)S(1)}, f32[16,512]{1,0:T(8,128)S(1)}, u32[]{:S(2)}, u32[]{:S(2)}) collective-permute-start(f32[16,512]{1,0:T(8,128)S(1)} %pad_maximum_fusion.1), channel_id=1, source_target_pairs={{0,8},{1,9},{2,10},{3,11},{4,12},{5,13},{6,14},{7,15},{8,0},{9,1},... | collective-permute-start | bytes 98312 | tf_op jit(solution)/shard_map/ppermute | solution.py:322
  8.6 0.6 %spread.3.spread_ref = bf16[384,2176]{1,0:T(8,128)(2,1)S(1)} custom-call(s32[1]{0:T(128)} %bitcast.4.me_ref, s32[4,2176]{1,0:T(4,128)S(1)} %get-tuple-element.48.blocks_ref, f32[4,2176]{1,0:T(4,128)S(1)} %get-tuple-element.49.weight_ref), custom_call_target="tpu_custom_call" | custom-call | bytes 3000000 | tf_op jit(solution)/shard_map/spread/pallas_call | solution.py:311
  9.3 0.8 %collective-permute-done.1 = f32[16,512]{1,0:T(8,128)S(1)} collective-permute-done((f32[16,512]{1,0:T(8,128)S(1)}, f32[16,512]{1,0:T(8,128)S(1)}, u32[]{:S(2)}, u32[]{:S(2)}) %collective-permute-start.1) | collective-permute-done | bytes 32800 | tf_op jit(solution)/shard_map/ppermute | solution.py:322
  10.1 2.2 %collective-permute-start.4 = (f32[32,512]{1,0:T(8,128)S(1)}, f32[32,512]{1,0:T(8,128)S(1)}, u32[]{:S(2)}, u32[]{:S(2)}) collective-permute-start(f32[32,512]{1,0:T(8,128)S(1)} %pad_maximum_fusion), channel_id=1, source_target_pairs={{0,6},{1,7},{2,4},{3,5},{4,2},{5,3},{6,0},{7,1},{8,14},{9,15},{10,... | collective-permute-start | bytes 196616 | tf_op jit(solution)/shard_map/ppermute | solution.py:322
  12.2 0.2 collective-permute-start.3
  12.5 0.3 collective-permute-start.2
  12.7 0.0 copy-done
  12.7 0.6 %observed.1.obs_ref = bf16[2,2048,128]{2,1,0:T(8,128)(2,1)S(1)} custom-call(f32[64,2048]{1,0:T(8,128)S(1)} %bitcast.11), custom_call_target="tpu_custom_call" | custom-call | bytes 1200000 | tf_op jit(solution)/shard_map/observed/pallas_call | solution.py:357
  13.4 1.8 %halves.1.x_ref = bf16[8,192,1024]{2,1,0:T(8,128)(2,1)S(1)} custom-call(f32[64,8,1024]{2,1,0:T(8,128)} %x_ref.2), custom_call_target="tpu_custom_call" | custom-call | bytes 4500000 | tf_op jit(solution)/shard_map/halves/pallas_call | solution.py:368
  15.2 0.0 collective-permute-done.4
  15.2 0.2 collective-permute-done.3
  15.4 0.2 collective-permute-done.2
  15.6 4.8 %collective-permute-start.5 = (f32[128,512]{1,0:T(8,128)S(1)}, f32[128,512]{1,0:T(8,128)S(1)}, u32[]{:S(2)}, u32[]{:S(2)}) collective-permute-start(f32[128,512]{1,0:T(8,128)S(1)} %constant_dynamic-update-slice_fusion.gathered_ref), channel_id=1, source_target_pairs={{0,1},{1,0},{2,3},{3,2},{4,5},{5,4},{6,7},{7,6},{8,9},{9,8},{10,11... | collective-permute-start | bytes 786440 | tf_op jit(solution)/shard_map/ppermute | solution.py:322
  20.4 1.5 %partial.1.hx_ref = f32[64,2176]{1,0:T(8,128)S(1)} custom-call(f32[128,512]{1,0:T(8,128)S(1)} %constant_dynamic-update-slice_fusion.gathered_ref, bf16[384,2176]{1,0:T(8,128)(2,1)S(1)} %spread.2.spread_ref, f32[8,2176]{1,0:T(8,128)S(1)} %get-tuple-element.65.resp_ref), custom_call_target="tpu_custom_call" | custom-call | bytes 3600000 | tf_op jit(solution)/shard_map/partial/pallas_call | solution.py:414
  21.9 0.0 collective-permute-done.5.gathered_ref
  21.9 8.2 %update.1 = (f32[64,8,1024]{2,1,0:T(8,128)}, f32[64,64]{1,0:T(8,128)}) custom-call(f32[64,2176]{1,0:T(8,128)S(1)} %partial.1.hx_ref, f32[128,512]{1,0:T(8,128)S(1)} %collective-permute-done.5.gathered_ref, bf16[384,2176]{1,0:T(8,128)(2,1)S(1)} %spread.3.spread_ref, f32[8,2176]{1,0:T(8,128)S(1)} %get-tuple-element.65.resp_ref, ...), custom_call_target="tpu_custom_call" | custom-call | tf_op jit(solution)/shard_map/update/pallas_call | solution.py:425
  (6 shorter events, 0.0 us)
Async XLA Ops:
  0.6 5.5 %copy-start.4 = (s32[2048]{0:T(1024)S(1)}, s32[2048]{0:T(1024)}, u32[]{:S(2)}) copy-start(s32[2048]{0:T(1024)} %param.15) | copy-start | bytes 24580
  0.6 5.5 %copy-start.3 = (f32[2048,4]{0,1:T(4,128)S(1)}, f32[2048,4]{0,1:T(4,128)}, u32[]{:S(2)}) copy-start(f32[2048,4]{0,1:T(4,128)} %param.11) | copy-start | bytes 98308
  0.7 5.5 %copy-start.2 = (s32[2048,4]{0,1:T(4,128)S(1)}, s32[2048,4]{0,1:T(4,128)}, u32[]{:S(2)}) copy-start(s32[2048,4]{0,1:T(4,128)} %param.10) | copy-start | bytes 98308
  0.7 5.5 %copy-start.5 = (f32[2048]{0:T(1024)S(1)}, f32[2048]{0:T(1024)}, u32[]{:S(2)}) copy-start(f32[2048]{0:T(1024)} %param.14) | copy-start | bytes 24580
  0.7 5.5 %copy-start.1 = (f32[2048,8]{0,1:T(8,128)S(1)}, f32[2048,8]{0,1:T(8,128)}, u32[]{:S(2)}) copy-start(f32[2048,8]{0,1:T(8,128)} %param.12) | copy-start | bytes 196612
  2.9 9.8 %copy-start = (f32[2048,64]{0,1:T(8,128)S(1)}, f32[2048,64]{0,1:T(8,128)}, u32[]{:S(2)}) copy-start(f32[2048,64]{0,1:T(8,128)} %param.13) | copy-start | bytes 1572868
  2.9 4.3 %collective-permute-start = (f32[8,512]{1,0:T(8,128)S(1)}, f32[8,512]{1,0:T(8,128)S(1)}, u32[]{:S(2)}, u32[]{:S(2)}) collective-permute-start(f32[8,512]{1,0:T(8,128)S(1)} %means.1), channel_id=1, source_target_pairs={{0,16},{1,17},{2,18},{3,19},{4,20},{5,21},{6,22},{7,23},{8,24},{9,... | collective-permute-start | bytes 49160 | tf_op jit(solution)/shard_map/ppermute | solution.py:322
  7.3 2.8 %collective-permute-start.1 = (f32[16,512]{1,0:T(8,128)S(1)}, f32[16,512]{1,0:T(8,128)S(1)}, u32[]{:S(2)}, u32[]{:S(2)}) collective-permute-start(f32[16,512]{1,0:T(8,128)S(1)} %pad_maximum_fusion.1), channel_id=1, source_target_pairs={{0,8},{1,9},{2,10},{3,11},{4,12},{5,13},{6,14},{7,15},{8,0},{9,1},... | collective-permute-start | bytes 98312 | tf_op jit(solution)/shard_map/ppermute | solution.py:322
  10.1 5.1 %collective-permute-start.4 = (f32[32,512]{1,0:T(8,128)S(1)}, f32[32,512]{1,0:T(8,128)S(1)}, u32[]{:S(2)}, u32[]{:S(2)}) collective-permute-start(f32[32,512]{1,0:T(8,128)S(1)} %pad_maximum_fusion), channel_id=1, source_target_pairs={{0,6},{1,7},{2,4},{3,5},{4,2},{5,3},{6,0},{7,1},{8,14},{9,15},{10,... | collective-permute-start | bytes 196616 | tf_op jit(solution)/shard_map/ppermute | solution.py:322
  12.2 3.1 %collective-permute-start.3 = (f32[32,512]{1,0:T(8,128)S(1)}, f32[32,512]{1,0:T(8,128)S(1)}, u32[]{:S(2)}, u32[]{:S(2)}) collective-permute-start(f32[32,512]{1,0:T(8,128)S(1)} %pad_maximum_fusion), channel_id=1, source_target_pairs={{0,4},{1,5},{2,6},{3,7},{4,0},{5,1},{6,2},{7,3},{8,12},{9,13},{10,... | collective-permute-start | bytes 196616 | tf_op jit(solution)/shard_map/ppermute | solution.py:322
  12.5 3.1 %collective-permute-start.2 = (f32[32,512]{1,0:T(8,128)S(1)}, f32[32,512]{1,0:T(8,128)S(1)}, u32[]{:S(2)}, u32[]{:S(2)}) collective-permute-start(f32[32,512]{1,0:T(8,128)S(1)} %pad_maximum_fusion), channel_id=1, source_target_pairs={{0,2},{1,3},{2,0},{3,1},{4,6},{5,7},{6,4},{7,5},{8,10},{9,11},{10,... | collective-permute-start | bytes 196616 | tf_op jit(solution)/shard_map/ppermute | solution.py:322
  15.6 6.3 %collective-permute-start.5 = (f32[128,512]{1,0:T(8,128)S(1)}, f32[128,512]{1,0:T(8,128)S(1)}, u32[]{:S(2)}, u32[]{:S(2)}) collective-permute-start(f32[128,512]{1,0:T(8,128)S(1)} %constant_dynamic-update-slice_fusion.gathered_ref), channel_id=1, source_target_pairs={{0,1},{1,0},{2,3},{3,2},{4,5},{5,4},{6,7},{7,6},{8,9},{9,8},{10,11... | collective-permute-start | bytes 786440 | tf_op jit(solution)/shard_map/ppermute | solution.py:322

commit v7 on v6

--- a/solution.py
+++ b/solution.py
@@ -212,7 +212,7 @@
 
 def update_kernel(
     members, bins, hx_ref, gathered_ref, spread_ref, resp_ref, obs_ref, weight_ref, x_ref,
-    field_ref, finals_ref, left, anom, out, sems,
+    field_ref, finals_ref, left, anom, out, own, sems,
 ):
     sensors = weight_ref.shape[1]
     turn(gathered_ref, left)
@@ -223,8 +223,6 @@
         center = sublane_mean(hx)
         anom[0:members, cut] = hx - center
         anom[members:, cut] = jnp.broadcast_to(center, (anom.shape[0] - members, step))
-    cut = slice(sensors, sensors + 128)
-    picked = hx_ref[:, cut] + observe(members, bins, left, spread_ref, resp_ref, cut)
     rhi, rlo = split(anom[...])
     whi, wlo = split(
         jnp.concatenate([anom[0:members, :] * weight_ref[t : t + 1, :] for t in range(2)], axis=0)
@@ -275,7 +273,11 @@
         for b in group:
             copies.append(pltpu.make_async_copy(out.at[b], field_ref.at[:, b, :], sems.at[b]))
             copies[-1].start()
-    finals_ref[...] = mm(total[:, 0:members], picked).T[0 : finals_ref.shape[0], :]
+    cut = slice(sensors, sensors + 128)
+    picked = hx_ref[:, cut] + observe(members, bins, left, spread_ref, resp_ref, cut)
+    own[...] = mm(total[:, 0:members], picked).T[0 : own.shape[0], :]
+    copies.append(pltpu.make_async_copy(own, finals_ref, sems.at[bins]))
+    copies[-1].start()
     for copy in copies:
         copy.wait()
 
@@ -429,12 +431,13 @@
             jax.ShapeDtypeStruct((batches * share, members), F32),
         ],
         in_specs=[VMEM_SPEC] * 7,
-        out_specs=[HBM_SPEC, VMEM_SPEC],
+        out_specs=[HBM_SPEC, HBM_SPEC],
         scratch_shapes=[
             left,
             pltpu.VMEM((members + 16, sensors), F32),
             pltpu.VMEM((bins, members, cells), F32),
-            pltpu.SemaphoreType.DMA((bins,)),
+            pltpu.VMEM((batches * share, members), F32),
+            pltpu.SemaphoreType.DMA((bins + 1,)),
         ],
         compiler_params=large,
         name="update",

time: 30.3 us -> 29.9 us (0.987)
  Pallas kernels: 16 us -> 15.6 us
    pallas_call x1, Pallas kernels: 8.25 us -> 7.85 us  [shards(): pl.pallas_call(functools.partial(update_kernel, members, bins), out_shape...]
where the time goes in v7:
time: 29.9 us; the launch traced here: 29.8 us
  Pallas kernels  15.6 us (52%)
  starting transfers between devices  12 us (40%)
  waiting for transfers between devices  1.27 us (4%)
  between operations  0.78 us (3%)
    ppermute x6, starting transfers between devices, exchange(): return lax.ppermute(value, AXES, [(i, i ^ mask) for i in range(devices)])  12 us
    pallas_call x1, Pallas kernels, shards(): pl.pallas_call(functools.partial(update_kernel, members, bins), out_shape...  7.85 us
    pallas_call x1, Pallas kernels, shards(): pl.pallas_call(means_kernel, out_shape=jax.ShapeDtypeStruct((nb, rows), F...  2.21 us
    pallas_call x1, Pallas kernels, halves_of(): pl.pallas_call(halves_kernel, out_shape=jax.ShapeDtypeStruct((bins, 3 * m...  1.78 us
    pallas_call x1, Pallas kernels, shards(): pl.pallas_call(functools.partial(partial_kernel, members, bins), out_shap...  1.46 us
    pallas_call x2, Pallas kernels, spread_of(): pl.pallas_call(functools.partial(spread_kernel, bits, nb, first), out_sha...  1.29 us
    ppermute x6, waiting for transfers between devices, exchange(): return lax.ppermute(value, AXES, [(i, i ^ mask) for i in range(devices)])  1.27 us
    pallas_call x1, Pallas kernels, obs_of(): pl.pallas_call(obs_kernel, out_shape=jax.ShapeDtypeStruct((2, sensors, 2...  0.63 us
  transfers between devices with their start and end apart: 6, of which 3 were waited for; matrix products, arithmetic and copies ran while one was open for 0% of the time, Pallas kernels for 19%

profile of v7, /device:TPU:1, one launch (start us, length us, event | category | flops | bytes accessed | tf_op | source)
XLA Modules:
  0.0 29.8 jit_solution(695460267179258994)
XLA Ops:
  0.6 0.0 copy-start.4
  0.6 0.0 copy-start.3
  0.7 0.0 copy-start.2
  0.7 0.0 copy-start.5
  0.7 0.0 copy-start.1
  0.7 2.2 %means.1 = f32[8,512]{1,0:T(8,128)S(1)} custom-call(f32[64,8,1024]{2,1,0:T(8,128)} %x_ref.2, f32[1,1024]{1,0:T(1,128)} %bitcast.17), custom_call_target="tpu_custom_call" | custom-call | tf_op jit(solution)/shard_map/means/pallas_call | solution.py:328
  2.9 0.0 copy-start
  2.9 3.2 %collective-permute-start = (f32[8,512]{1,0:T(8,128)S(1)}, f32[8,512]{1,0:T(8,128)S(1)}, u32[]{:S(2)}, u32[]{:S(2)}) collective-permute-start(f32[8,512]{1,0:T(8,128)S(1)} %means.1), channel_id=1, source_target_pairs={{0,16},{1,17},{2,18},{3,19},{4,20},{5,21},{6,22},{7,23},{8,24},{9,... | collective-permute-start | bytes 49160 | tf_op jit(solution)/shard_map/ppermute | solution.py:324
  6.1 0.0 copy-done.4
  6.1 0.0 copy-done.3
  6.1 0.0 copy-done.2
  6.1 0.0 copy-done.5
  6.1 0.0 copy-done.1
  6.1 0.4 %roles.1 = (f32[2,2048]{1,0:T(2,128)S(1)}, s32[4,2176]{1,0:T(4,128)S(1)}, f32[4,2176]{1,0:T(4,128)S(1)}, f32[8,2176]{1,0:T(8,128)S(1)}) custom-call(s32[1]{0:T(128)} %bitcast.4.me_ref, s32[16,128]{1,0:T(8,128)S(1)} %bitcast.15, f32[16,128]{1,0:T(8,128)S(1)} %bitcast.16, s32[4,2048]{1,0:T(4,128)S(1)} %bitcast.13, f32[4,2048]{1,0:T(4,128)S(1)} %bitcast.14, ...), custom_call_target="tpu_custom_call" | custom-call | bytes 1800000 | tf_op jit(solution)/shard_map/roles/pallas_call | solution.py:343
  6.6 0.6 %spread.2.spread_ref = bf16[384,2176]{1,0:T(8,128)(2,1)S(1)} custom-call(s32[1]{0:T(128)} %bitcast.4.me_ref, s32[4,2176]{1,0:T(4,128)S(1)} %get-tuple-element.48.blocks_ref, f32[4,2176]{1,0:T(4,128)S(1)} %get-tuple-element.49.weight_ref), custom_call_target="tpu_custom_call" | custom-call | bytes 3000000 | tf_op jit(solution)/shard_map/spread/pallas_call | solution.py:313
  7.2 0.0 collective-permute-done
  7.3 1.3 %collective-permute-start.1 = (f32[16,512]{1,0:T(8,128)S(1)}, f32[16,512]{1,0:T(8,128)S(1)}, u32[]{:S(2)}, u32[]{:S(2)}) collective-permute-start(f32[16,512]{1,0:T(8,128)S(1)} %pad_maximum_fusion.1), channel_id=1, source_target_pairs={{0,8},{1,9},{2,10},{3,11},{4,12},{5,13},{6,14},{7,15},{8,0},{9,1},... | collective-permute-start | bytes 98312 | tf_op jit(solution)/shard_map/ppermute | solution.py:324
  8.6 0.6 %spread.3.spread_ref = bf16[384,2176]{1,0:T(8,128)(2,1)S(1)} custom-call(s32[1]{0:T(128)} %bitcast.4.me_ref, s32[4,2176]{1,0:T(4,128)S(1)} %get-tuple-element.48.blocks_ref, f32[4,2176]{1,0:T(4,128)S(1)} %get-tuple-element.49.weight_ref), custom_call_target="tpu_custom_call" | custom-call | bytes 3000000 | tf_op jit(solution)/shard_map/spread/pallas_call | solution.py:313
  9.3 0.8 %collective-permute-done.1 = f32[16,512]{1,0:T(8,128)S(1)} collective-permute-done((f32[16,512]{1,0:T(8,128)S(1)}, f32[16,512]{1,0:T(8,128)S(1)}, u32[]{:S(2)}, u32[]{:S(2)}) %collective-permute-start.1) | collective-permute-done | bytes 32800 | tf_op jit(solution)/shard_map/ppermute | solution.py:324
  10.1 2.2 %collective-permute-start.4 = (f32[32,512]{1,0:T(8,128)S(1)}, f32[32,512]{1,0:T(8,128)S(1)}, u32[]{:S(2)}, u32[]{:S(2)}) collective-permute-start(f32[32,512]{1,0:T(8,128)S(1)} %pad_maximum_fusion), channel_id=1, source_target_pairs={{0,6},{1,7},{2,4},{3,5},{4,2},{5,3},{6,0},{7,1},{8,14},{9,15},{10,... | collective-permute-start | bytes 196616 | tf_op jit(solution)/shard_map/ppermute | solution.py:324
  12.2 0.2 collective-permute-start.3
  12.5 0.3 collective-permute-start.2
  12.7 0.0 copy-done
  12.7 0.6 %observed.1.obs_ref = bf16[2,2048,128]{2,1,0:T(8,128)(2,1)S(1)} custom-call(f32[64,2048]{1,0:T(8,128)S(1)} %bitcast.11), custom_call_target="tpu_custom_call" | custom-call | bytes 1200000 | tf_op jit(solution)/shard_map/observed/pallas_call | solution.py:359
  13.4 1.8 %halves.1.x_ref = bf16[8,192,1024]{2,1,0:T(8,128)(2,1)S(1)} custom-call(f32[64,8,1024]{2,1,0:T(8,128)} %x_ref.2), custom_call_target="tpu_custom_call" | custom-call | bytes 4500000 | tf_op jit(solution)/shard_map/halves/pallas_call | solution.py:370
  15.2 0.0 collective-permute-done.4
  15.2 0.2 collective-permute-done.3
  15.4 0.2 collective-permute-done.2
  15.6 4.8 %collective-permute-start.5 = (f32[128,512]{1,0:T(8,128)S(1)}, f32[128,512]{1,0:T(8,128)S(1)}, u32[]{:S(2)}, u32[]{:S(2)}) collective-permute-start(f32[128,512]{1,0:T(8,128)S(1)} %constant_dynamic-update-slice_fusion.gathered_ref), channel_id=1, source_target_pairs={{0,1},{1,0},{2,3},{3,2},{4,5},{5,4},{6,7},{7,6},{8,9},{9,8},{10,11... | collective-permute-start | bytes 786440 | tf_op jit(solution)/shard_map/ppermute | solution.py:324
  20.4 1.5 %partial.1.hx_ref = f32[64,2176]{1,0:T(8,128)S(1)} custom-call(f32[128,512]{1,0:T(8,128)S(1)} %constant_dynamic-update-slice_fusion.gathered_ref, bf16[384,2176]{1,0:T(8,128)(2,1)S(1)} %spread.2.spread_ref, f32[8,2176]{1,0:T(8,128)S(1)} %get-tuple-element.65.resp_ref), custom_call_target="tpu_custom_call" | custom-call | bytes 3600000 | tf_op jit(solution)/shard_map/partial/pallas_call | solution.py:416
  21.9 0.0 collective-permute-done.5.gathered_ref
  21.9 7.9 %update.1 = (f32[64,8,1024]{2,1,0:T(8,128)}, f32[64,64]{1,0:T(8,128)}) custom-call(f32[64,2176]{1,0:T(8,128)S(1)} %partial.1.hx_ref, f32[128,512]{1,0:T(8,128)S(1)} %collective-permute-done.5.gathered_ref, bf16[384,2176]{1,0:T(8,128)(2,1)S(1)} %spread.3.spread_ref, f32[8,2176]{1,0:T(8,128)S(1)} %get-tuple-element.65.resp_ref, ...), custom_call_target="tpu_custom_call" | custom-call | tf_op jit(solution)/shard_map/update/pallas_call | solution.py:427
  (6 shorter events, 0.0 us)
Async XLA Ops:
  0.6 5.5 %copy-start.4 = (s32[2048]{0:T(1024)S(1)}, s32[2048]{0:T(1024)}, u32[]{:S(2)}) copy-start(s32[2048]{0:T(1024)} %param.15) | copy-start | bytes 24580
  0.6 5.5 %copy-start.3 = (f32[2048,4]{0,1:T(4,128)S(1)}, f32[2048,4]{0,1:T(4,128)}, u32[]{:S(2)}) copy-start(f32[2048,4]{0,1:T(4,128)} %param.11) | copy-start | bytes 98308
  0.7 5.5 %copy-start.2 = (s32[2048,4]{0,1:T(4,128)S(1)}, s32[2048,4]{0,1:T(4,128)}, u32[]{:S(2)}) copy-start(s32[2048,4]{0,1:T(4,128)} %param.10) | copy-start | bytes 98308
  0.7 5.5 %copy-start.5 = (f32[2048]{0:T(1024)S(1)}, f32[2048]{0:T(1024)}, u32[]{:S(2)}) copy-start(f32[2048]{0:T(1024)} %param.14) | copy-start | bytes 24580
  0.7 5.5 %copy-start.1 = (f32[2048,8]{0,1:T(8,128)S(1)}, f32[2048,8]{0,1:T(8,128)}, u32[]{:S(2)}) copy-start(f32[2048,8]{0,1:T(8,128)} %param.12) | copy-start | bytes 196612
  2.9 9.8 %copy-start = (f32[2048,64]{0,1:T(8,128)S(1)}, f32[2048,64]{0,1:T(8,128)}, u32[]{:S(2)}) copy-start(f32[2048,64]{0,1:T(8,128)} %param.13) | copy-start | bytes 1572868
  2.9 4.3 %collective-permute-start = (f32[8,512]{1,0:T(8,128)S(1)}, f32[8,512]{1,0:T(8,128)S(1)}, u32[]{:S(2)}, u32[]{:S(2)}) collective-permute-start(f32[8,512]{1,0:T(8,128)S(1)} %means.1), channel_id=1, source_target_pairs={{0,16},{1,17},{2,18},{3,19},{4,20},{5,21},{6,22},{7,23},{8,24},{9,... | collective-permute-start | bytes 49160 | tf_op jit(solution)/shard_map/ppermute | solution.py:324
  7.3 2.8 %collective-permute-start.1 = (f32[16,512]{1,0:T(8,128)S(1)}, f32[16,512]{1,0:T(8,128)S(1)}, u32[]{:S(2)}, u32[]{:S(2)}) collective-permute-start(f32[16,512]{1,0:T(8,128)S(1)} %pad_maximum_fusion.1), channel_id=1, source_target_pairs={{0,8},{1,9},{2,10},{3,11},{4,12},{5,13},{6,14},{7,15},{8,0},{9,1},... | collective-permute-start | bytes 98312 | tf_op jit(solution)/shard_map/ppermute | solution.py:324
  10.1 5.1 %collective-permute-start.4 = (f32[32,512]{1,0:T(8,128)S(1)}, f32[32,512]{1,0:T(8,128)S(1)}, u32[]{:S(2)}, u32[]{:S(2)}) collective-permute-start(f32[32,512]{1,0:T(8,128)S(1)} %pad_maximum_fusion), channel_id=1, source_target_pairs={{0,6},{1,7},{2,4},{3,5},{4,2},{5,3},{6,0},{7,1},{8,14},{9,15},{10,... | collective-permute-start | bytes 196616 | tf_op jit(solution)/shard_map/ppermute | solution.py:324
  12.2 3.1 %collective-permute-start.3 = (f32[32,512]{1,0:T(8,128)S(1)}, f32[32,512]{1,0:T(8,128)S(1)}, u32[]{:S(2)}, u32[]{:S(2)}) collective-permute-start(f32[32,512]{1,0:T(8,128)S(1)} %pad_maximum_fusion), channel_id=1, source_target_pairs={{0,4},{1,5},{2,6},{3,7},{4,0},{5,1},{6,2},{7,3},{8,12},{9,13},{10,... | collective-permute-start | bytes 196616 | tf_op jit(solution)/shard_map/ppermute | solution.py:324
  12.5 3.1 %collective-permute-start.2 = (f32[32,512]{1,0:T(8,128)S(1)}, f32[32,512]{1,0:T(8,128)S(1)}, u32[]{:S(2)}, u32[]{:S(2)}) collective-permute-start(f32[32,512]{1,0:T(8,128)S(1)} %pad_maximum_fusion), channel_id=1, source_target_pairs={{0,2},{1,3},{2,0},{3,1},{4,6},{5,7},{6,4},{7,5},{8,10},{9,11},{10,... | collective-permute-start | bytes 196616 | tf_op jit(solution)/shard_map/ppermute | solution.py:324
  15.6 6.3 %collective-permute-start.5 = (f32[128,512]{1,0:T(8,128)S(1)}, f32[128,512]{1,0:T(8,128)S(1)}, u32[]{:S(2)}, u32[]{:S(2)}) collective-permute-start(f32[128,512]{1,0:T(8,128)S(1)} %constant_dynamic-update-slice_fusion.gathered_ref), channel_id=1, source_target_pairs={{0,1},{1,0},{2,3},{3,2},{4,5},{5,4},{6,7},{7,6},{8,9},{9,8},{10,11... | collective-permute-start | bytes 786440 | tf_op jit(solution)/shard_map/ppermute | solution.py:324

commit v8 on v7

--- a/solution.py
+++ b/solution.py
@@ -25,7 +25,13 @@
 
 
 def mm(a, b):
-    return jnp.dot(a, b, precision=lax.Precision.HIGHEST, preferred_element_type=F32)
+    ahi, alo = split(a)
+    bhi, blo = split(b)
+    return (
+        jnp.dot(ahi, bhi, preferred_element_type=F32)
+        + jnp.dot(ahi, blo, preferred_element_type=F32)
+        + jnp.dot(alo, bhi, preferred_element_type=F32)
+    )
 
 
 def sublane_mean(x):
@@ -222,7 +228,7 @@
         hx = hx_ref[:, cut] + observe(members, bins, left, spread_ref, resp_ref, cut)
         center = sublane_mean(hx)
         anom[0:members, cut] = hx - center
-        anom[members:, cut] = jnp.broadcast_to(center, (anom.shape[0] - members, step))
+        anom[members:, cut] = jnp.broadcast_to(center, (members, step))
     rhi, rlo = split(anom[...])
     whi, wlo = split(
         jnp.concatenate([anom[0:members, :] * weight_ref[t : t + 1, :] for t in range(2)], axis=0)
@@ -238,10 +244,7 @@
         + jnp.dot(whi, obs_ref[1], preferred_element_type=F32)
     )
     lane = lax.broadcasted_iota(jnp.int32, (2 * members, 2 * members), 1)
-    wide_sums = jnp.concatenate(
-        [sums, jnp.zeros((2 * members, 2 * members - sums.shape[1]), F32)], axis=1
-    )
-    base = jnp.where(lane < members, wide_sums, pulls - sums[:, members : members + 1])
+    base = jnp.where(lane < members, sums, pulls - sums)
     lane = lane[0:members]
     right = lane >= members
     row = lax.broadcasted_iota(jnp.int32, lane.shape, 0)
@@ -434,7 +437,7 @@
         out_specs=[HBM_SPEC, HBM_SPEC],
         scratch_shapes=[
             left,
-            pltpu.VMEM((members + 16, sensors), F32),
+            pltpu.VMEM((2 * members, sensors), F32),
             pltpu.VMEM((bins, members, cells), F32),
             pltpu.VMEM((batches * share, members), F32),
             pltpu.SemaphoreType.DMA((bins + 1,)),

time: 29.9 us -> 29.4 us (0.983)
  Pallas kernels: 15.6 us -> 15.1 us
    pallas_call x1, Pallas kernels: 7.85 us -> 7.31 us  [shards(): pl.pallas_call(functools.partial(update_kernel, members, bins), out_shape...]
where the time goes in v8:
time: 29.4 us; the launch traced here: 29.2 us
  Pallas kernels  15.1 us (51%)
  starting transfers between devices  12 us (41%)
  waiting for transfers between devices  1.27 us (4%)
  between operations  0.78 us (3%)
    ppermute x6, starting transfers between devices, exchange(): return lax.ppermute(value, AXES, [(i, i ^ mask) for i in range(devices)])  12 us
    pallas_call x1, Pallas kernels, shards(): pl.pallas_call(functools.partial(update_kernel, members, bins), out_shape...  7.31 us
    pallas_call x1, Pallas kernels, shards(): pl.pallas_call(means_kernel, out_shape=jax.ShapeDtypeStruct((nb, rows), F...  2.21 us
    pallas_call x1, Pallas kernels, halves_of(): pl.pallas_call(halves_kernel, out_shape=jax.ShapeDtypeStruct((bins, 3 * m...  1.78 us
    pallas_call x1, Pallas kernels, shards(): pl.pallas_call(functools.partial(partial_kernel, members, bins), out_shap...  1.46 us
    pallas_call x2, Pallas kernels, spread_of(): pl.pallas_call(functools.partial(spread_kernel, bits, nb, first), out_sha...  1.29 us
    ppermute x6, waiting for transfers between devices, exchange(): return lax.ppermute(value, AXES, [(i, i ^ mask) for i in range(devices)])  1.27 us
    pallas_call x1, Pallas kernels, obs_of(): pl.pallas_call(obs_kernel, out_shape=jax.ShapeDtypeStruct((2, sensors, 2...  0.63 us
  transfers between devices with their start and end apart: 6, of which 3 were waited for; matrix products, arithmetic and copies ran while one was open for 0% of the time, Pallas kernels for 19%

profile of v8, /device:TPU:1, one launch (start us, length us, event | category | flops | bytes accessed | tf_op | source)
XLA Modules:
  0.0 29.2 jit_solution(10047264365614871911)
XLA Ops:
  0.6 0.0 copy-start.4
  0.6 0.0 copy-start.3
  0.7 0.0 copy-start.2
  0.7 0.0 copy-start.5
  0.7 0.0 copy-start.1
  0.7 2.2 %means.1 = f32[8,512]{1,0:T(8,128)S(1)} custom-call(f32[64,8,1024]{2,1,0:T(8,128)} %x_ref.2, f32[1,1024]{1,0:T(1,128)} %bitcast.17), custom_call_target="tpu_custom_call" | custom-call | tf_op jit(solution)/shard_map/means/pallas_call | solution.py:331
  2.9 0.0 copy-start
  2.9 3.2 %collective-permute-start = (f32[8,512]{1,0:T(8,128)S(1)}, f32[8,512]{1,0:T(8,128)S(1)}, u32[]{:S(2)}, u32[]{:S(2)}) collective-permute-start(f32[8,512]{1,0:T(8,128)S(1)} %means.1), channel_id=1, source_target_pairs={{0,16},{1,17},{2,18},{3,19},{4,20},{5,21},{6,22},{7,23},{8,24},{9,... | collective-permute-start | bytes 49160 | tf_op jit(solution)/shard_map/ppermute | solution.py:327
  6.1 0.0 copy-done.4
  6.1 0.0 copy-done.3
  6.1 0.0 copy-done.2
  6.1 0.0 copy-done.5
  6.1 0.0 copy-done.1
  6.1 0.4 %roles.1 = (f32[2,2048]{1,0:T(2,128)S(1)}, s32[4,2176]{1,0:T(4,128)S(1)}, f32[4,2176]{1,0:T(4,128)S(1)}, f32[8,2176]{1,0:T(8,128)S(1)}) custom-call(s32[1]{0:T(128)} %bitcast.4.me_ref, s32[16,128]{1,0:T(8,128)S(1)} %bitcast.15, f32[16,128]{1,0:T(8,128)S(1)} %bitcast.16, s32[4,2048]{1,0:T(4,128)S(1)} %bitcast.13, f32[4,2048]{1,0:T(4,128)S(1)} %bitcast.14, ...), custom_call_target="tpu_custom_call" | custom-call | bytes 1800000 | tf_op jit(solution)/shard_map/roles/pallas_call | solution.py:346
  6.6 0.6 %spread.2.spread_ref = bf16[384,2176]{1,0:T(8,128)(2,1)S(1)} custom-call(s32[1]{0:T(128)} %bitcast.4.me_ref, s32[4,2176]{1,0:T(4,128)S(1)} %get-tuple-element.48.blocks_ref, f32[4,2176]{1,0:T(4,128)S(1)} %get-tuple-element.49.weight_ref), custom_call_target="tpu_custom_call" | custom-call | bytes 3000000 | tf_op jit(solution)/shard_map/spread/pallas_call | solution.py:316
  7.2 0.0 collective-permute-done
  7.3 1.3 %collective-permute-start.1 = (f32[16,512]{1,0:T(8,128)S(1)}, f32[16,512]{1,0:T(8,128)S(1)}, u32[]{:S(2)}, u32[]{:S(2)}) collective-permute-start(f32[16,512]{1,0:T(8,128)S(1)} %pad_maximum_fusion.1), channel_id=1, source_target_pairs={{0,8},{1,9},{2,10},{3,11},{4,12},{5,13},{6,14},{7,15},{8,0},{9,1},... | collective-permute-start | bytes 98312 | tf_op jit(solution)/shard_map/ppermute | solution.py:327
  8.6 0.6 %spread.3.spread_ref = bf16[384,2176]{1,0:T(8,128)(2,1)S(1)} custom-call(s32[1]{0:T(128)} %bitcast.4.me_ref, s32[4,2176]{1,0:T(4,128)S(1)} %get-tuple-element.48.blocks_ref, f32[4,2176]{1,0:T(4,128)S(1)} %get-tuple-element.49.weight_ref), custom_call_target="tpu_custom_call" | custom-call | bytes 3000000 | tf_op jit(solution)/shard_map/spread/pallas_call | solution.py:316
  9.3 0.8 %collective-permute-done.1 = f32[16,512]{1,0:T(8,128)S(1)} collective-permute-done((f32[16,512]{1,0:T(8,128)S(1)}, f32[16,512]{1,0:T(8,128)S(1)}, u32[]{:S(2)}, u32[]{:S(2)}) %collective-permute-start.1) | collective-permute-done | bytes 32800 | tf_op jit(solution)/shard_map/ppermute | solution.py:327
  10.1 2.2 %collective-permute-start.4 = (f32[32,512]{1,0:T(8,128)S(1)}, f32[32,512]{1,0:T(8,128)S(1)}, u32[]{:S(2)}, u32[]{:S(2)}) collective-permute-start(f32[32,512]{1,0:T(8,128)S(1)} %pad_maximum_fusion), channel_id=1, source_target_pairs={{0,6},{1,7},{2,4},{3,5},{4,2},{5,3},{6,0},{7,1},{8,14},{9,15},{10,... | collective-permute-start | bytes 196616 | tf_op jit(solution)/shard_map/ppermute | solution.py:327
  12.2 0.2 collective-permute-start.3
  12.5 0.3 collective-permute-start.2
  12.7 0.0 copy-done
  12.7 0.6 %observed.1.obs_ref = bf16[2,2048,128]{2,1,0:T(8,128)(2,1)S(1)} custom-call(f32[64,2048]{1,0:T(8,128)S(1)} %bitcast.11), custom_call_target="tpu_custom_call" | custom-call | bytes 1200000 | tf_op jit(solution)/shard_map/observed/pallas_call | solution.py:362
  13.4 1.8 %halves.1.x_ref = bf16[8,192,1024]{2,1,0:T(8,128)(2,1)S(1)} custom-call(f32[64,8,1024]{2,1,0:T(8,128)} %x_ref.2), custom_call_target="tpu_custom_call" | custom-call | bytes 4500000 | tf_op jit(solution)/shard_map/halves/pallas_call | solution.py:373
  15.2 0.0 collective-permute-done.4
  15.2 0.2 collective-permute-done.3
  15.4 0.2 collective-permute-done.2
  15.6 4.8 %collective-permute-start.5 = (f32[128,512]{1,0:T(8,128)S(1)}, f32[128,512]{1,0:T(8,128)S(1)}, u32[]{:S(2)}, u32[]{:S(2)}) collective-permute-start(f32[128,512]{1,0:T(8,128)S(1)} %constant_dynamic-update-slice_fusion.gathered_ref), channel_id=1, source_target_pairs={{0,1},{1,0},{2,3},{3,2},{4,5},{5,4},{6,7},{7,6},{8,9},{9,8},{10,11... | collective-permute-start | bytes 786440 | tf_op jit(solution)/shard_map/ppermute | solution.py:327
  20.4 1.5 %partial.1.hx_ref = f32[64,2176]{1,0:T(8,128)S(1)} custom-call(f32[128,512]{1,0:T(8,128)S(1)} %constant_dynamic-update-slice_fusion.gathered_ref, bf16[384,2176]{1,0:T(8,128)(2,1)S(1)} %spread.2.spread_ref, f32[8,2176]{1,0:T(8,128)S(1)} %get-tuple-element.65.resp_ref), custom_call_target="tpu_custom_call" | custom-call | bytes 3600000 | tf_op jit(solution)/shard_map/partial/pallas_call | solution.py:419
  21.9 0.0 collective-permute-done.5.gathered_ref
  21.9 7.3 %update.1 = (f32[64,8,1024]{2,1,0:T(8,128)}, f32[64,64]{1,0:T(8,128)}) custom-call(f32[64,2176]{1,0:T(8,128)S(1)} %partial.1.hx_ref, f32[128,512]{1,0:T(8,128)S(1)} %collective-permute-done.5.gathered_ref, bf16[384,2176]{1,0:T(8,128)(2,1)S(1)} %spread.3.spread_ref, f32[8,2176]{1,0:T(8,128)S(1)} %get-tuple-element.65.resp_ref, ...), custom_call_target="tpu_custom_call" | custom-call | tf_op jit(solution)/shard_map/update/pallas_call | solution.py:430
  (6 shorter events, 0.0 us)
Async XLA Ops:
  0.6 5.5 %copy-start.4 = (s32[2048]{0:T(1024)S(1)}, s32[2048]{0:T(1024)}, u32[]{:S(2)}) copy-start(s32[2048]{0:T(1024)} %param.15) | copy-start | bytes 24580
  0.6 5.5 %copy-start.3 = (f32[2048,4]{0,1:T(4,128)S(1)}, f32[2048,4]{0,1:T(4,128)}, u32[]{:S(2)}) copy-start(f32[2048,4]{0,1:T(4,128)} %param.11) | copy-start | bytes 98308
  0.7 5.5 %copy-start.2 = (s32[2048,4]{0,1:T(4,128)S(1)}, s32[2048,4]{0,1:T(4,128)}, u32[]{:S(2)}) copy-start(s32[2048,4]{0,1:T(4,128)} %param.10) | copy-start | bytes 98308
  0.7 5.5 %copy-start.5 = (f32[2048]{0:T(1024)S(1)}, f32[2048]{0:T(1024)}, u32[]{:S(2)}) copy-start(f32[2048]{0:T(1024)} %param.14) | copy-start | bytes 24580
  0.7 5.5 %copy-start.1 = (f32[2048,8]{0,1:T(8,128)S(1)}, f32[2048,8]{0,1:T(8,128)}, u32[]{:S(2)}) copy-start(f32[2048,8]{0,1:T(8,128)} %param.12) | copy-start | bytes 196612
  2.9 9.8 %copy-start = (f32[2048,64]{0,1:T(8,128)S(1)}, f32[2048,64]{0,1:T(8,128)}, u32[]{:S(2)}) copy-start(f32[2048,64]{0,1:T(8,128)} %param.13) | copy-start | bytes 1572868
  2.9 4.3 %collective-permute-start = (f32[8,512]{1,0:T(8,128)S(1)}, f32[8,512]{1,0:T(8,128)S(1)}, u32[]{:S(2)}, u32[]{:S(2)}) collective-permute-start(f32[8,512]{1,0:T(8,128)S(1)} %means.1), channel_id=1, source_target_pairs={{0,16},{1,17},{2,18},{3,19},{4,20},{5,21},{6,22},{7,23},{8,24},{9,... | collective-permute-start | bytes 49160 | tf_op jit(solution)/shard_map/ppermute | solution.py:327
  7.3 2.8 %collective-permute-start.1 = (f32[16,512]{1,0:T(8,128)S(1)}, f32[16,512]{1,0:T(8,128)S(1)}, u32[]{:S(2)}, u32[]{:S(2)}) collective-permute-start(f32[16,512]{1,0:T(8,128)S(1)} %pad_maximum_fusion.1), channel_id=1, source_target_pairs={{0,8},{1,9},{2,10},{3,11},{4,12},{5,13},{6,14},{7,15},{8,0},{9,1},... | collective-permute-start | bytes 98312 | tf_op jit(solution)/shard_map/ppermute | solution.py:327
  10.1 5.1 %collective-permute-start.4 = (f32[32,512]{1,0:T(8,128)S(1)}, f32[32,512]{1,0:T(8,128)S(1)}, u32[]{:S(2)}, u32[]{:S(2)}) collective-permute-start(f32[32,512]{1,0:T(8,128)S(1)} %pad_maximum_fusion), channel_id=1, source_target_pairs={{0,6},{1,7},{2,4},{3,5},{4,2},{5,3},{6,0},{7,1},{8,14},{9,15},{10,... | collective-permute-start | bytes 196616 | tf_op jit(solution)/shard_map/ppermute | solution.py:327
  12.2 3.1 %collective-permute-start.3 = (f32[32,512]{1,0:T(8,128)S(1)}, f32[32,512]{1,0:T(8,128)S(1)}, u32[]{:S(2)}, u32[]{:S(2)}) collective-permute-start(f32[32,512]{1,0:T(8,128)S(1)} %pad_maximum_fusion), channel_id=1, source_target_pairs={{0,4},{1,5},{2,6},{3,7},{4,0},{5,1},{6,2},{7,3},{8,12},{9,13},{10,... | collective-permute-start | bytes 196616 | tf_op jit(solution)/shard_map/ppermute | solution.py:327
  12.5 3.1 %collective-permute-start.2 = (f32[32,512]{1,0:T(8,128)S(1)}, f32[32,512]{1,0:T(8,128)S(1)}, u32[]{:S(2)}, u32[]{:S(2)}) collective-permute-start(f32[32,512]{1,0:T(8,128)S(1)} %pad_maximum_fusion), channel_id=1, source_target_pairs={{0,2},{1,3},{2,0},{3,1},{4,6},{5,7},{6,4},{7,5},{8,10},{9,11},{10,... | collective-permute-start | bytes 196616 | tf_op jit(solution)/shard_map/ppermute | solution.py:327
  15.6 6.3 %collective-permute-start.5 = (f32[128,512]{1,0:T(8,128)S(1)}, f32[128,512]{1,0:T(8,128)S(1)}, u32[]{:S(2)}, u32[]{:S(2)}) collective-permute-start(f32[128,512]{1,0:T(8,128)S(1)} %constant_dynamic-update-slice_fusion.gathered_ref), channel_id=1, source_target_pairs={{0,1},{1,0},{2,3},{3,2},{4,5},{5,4},{6,7},{7,6},{8,9},{9,8},{10,11... | collective-permute-start | bytes 786440 | tf_op jit(solution)/shard_map/ppermute | solution.py:327

commit v9 on v8

--- a/solution.py
+++ b/solution.py
@@ -269,8 +269,7 @@
     thi, tlo = split(total)
     lhs = jnp.concatenate([thi, tlo[:, 0:members]], axis=1)
     copies = []
-    for first_bin in range(0, bins, bins // 2):
-        group = range(first_bin, first_bin + bins // 2)
+    for group in (range(0, bins // 4), range(bins // 4, bins)):
         for b in group:
             out[b] = jnp.dot(lhs, x_ref[b], preferred_element_type=F32)
         for b in group:

time: 29.4 us -> 29.4 us (level)
  no operation moved by 1% of the time
where the time goes in v9:
time: 29.4 us; the launch traced here: 29.2 us
  Pallas kernels  15.1 us (51%)
  starting transfers between devices  12 us (41%)
  waiting for transfers between devices  1.27 us (4%)
  between operations  0.78 us (3%)
    ppermute x6, starting transfers between devices, exchange(): return lax.ppermute(value, AXES, [(i, i ^ mask) for i in range(devices)])  12 us
    pallas_call x1, Pallas kernels, shards(): pl.pallas_call(functools.partial(update_kernel, members, bins), out_shape...  7.32 us
    pallas_call x1, Pallas kernels, shards(): pl.pallas_call(means_kernel, out_shape=jax.ShapeDtypeStruct((nb, rows), F...  2.21 us
    pallas_call x1, Pallas kernels, halves_of(): pl.pallas_call(halves_kernel, out_shape=jax.ShapeDtypeStruct((bins, 3 * m...  1.78 us
    pallas_call x1, Pallas kernels, shards(): pl.pallas_call(functools.partial(partial_kernel, members, bins), out_shap...  1.46 us
    pallas_call x2, Pallas kernels, spread_of(): pl.pallas_call(functools.partial(spread_kernel, bits, nb, first), out_sha...  1.29 us
    ppermute x6, waiting for transfers between devices, exchange(): return lax.ppermute(value, AXES, [(i, i ^ mask) for i in range(devices)])  1.27 us
    pallas_call x1, Pallas kernels, obs_of(): pl.pallas_call(obs_kernel, out_shape=jax.ShapeDtypeStruct((2, sensors, 2...  0.63 us
  transfers between devices with their start and end apart: 6, of which 3 were waited for; matrix products, arithmetic and copies ran while one was open for 0% of the time, Pallas kernels for 19%

profile of v9, /device:TPU:1, one launch (start us, length us, event | category | flops | bytes accessed | tf_op | source)
XLA Modules:
  0.0 29.2 jit_solution(13197242770708668368)
XLA Ops:
  0.6 0.0 copy-start.4
  0.6 0.0 copy-start.3
  0.7 0.0 copy-start.2
  0.7 0.0 copy-start.5
  0.7 0.0 copy-start.1
  0.7 2.2 %means.1 = f32[8,512]{1,0:T(8,128)S(1)} custom-call(f32[64,8,1024]{2,1,0:T(8,128)} %x_ref.2, f32[1,1024]{1,0:T(1,128)} %bitcast.17), custom_call_target="tpu_custom_call" | custom-call | tf_op jit(solution)/shard_map/means/pallas_call | solution.py:330
  2.9 0.0 copy-start
  2.9 3.2 %collective-permute-start = (f32[8,512]{1,0:T(8,128)S(1)}, f32[8,512]{1,0:T(8,128)S(1)}, u32[]{:S(2)}, u32[]{:S(2)}) collective-permute-start(f32[8,512]{1,0:T(8,128)S(1)} %means.1), channel_id=1, source_target_pairs={{0,16},{1,17},{2,18},{3,19},{4,20},{5,21},{6,22},{7,23},{8,24},{9,... | collective-permute-start | bytes 49160 | tf_op jit(solution)/shard_map/ppermute | solution.py:326
  6.1 0.0 copy-done.4
  6.1 0.0 copy-done.3
  6.1 0.0 copy-done.2
  6.1 0.0 copy-done.5
  6.1 0.0 copy-done.1
  6.1 0.4 %roles.1 = (f32[2,2048]{1,0:T(2,128)S(1)}, s32[4,2176]{1,0:T(4,128)S(1)}, f32[4,2176]{1,0:T(4,128)S(1)}, f32[8,2176]{1,0:T(8,128)S(1)}) custom-call(s32[1]{0:T(128)} %bitcast.4.me_ref, s32[16,128]{1,0:T(8,128)S(1)} %bitcast.15, f32[16,128]{1,0:T(8,128)S(1)} %bitcast.16, s32[4,2048]{1,0:T(4,128)S(1)} %bitcast.13, f32[4,2048]{1,0:T(4,128)S(1)} %bitcast.14, ...), custom_call_target="tpu_custom_call" | custom-call | bytes 1800000 | tf_op jit(solution)/shard_map/roles/pallas_call | solution.py:345
  6.6 0.6 %spread.2.spread_ref = bf16[384,2176]{1,0:T(8,128)(2,1)S(1)} custom-call(s32[1]{0:T(128)} %bitcast.4.me_ref, s32[4,2176]{1,0:T(4,128)S(1)} %get-tuple-element.48.blocks_ref, f32[4,2176]{1,0:T(4,128)S(1)} %get-tuple-element.49.weight_ref), custom_call_target="tpu_custom_call" | custom-call | bytes 3000000 | tf_op jit(solution)/shard_map/spread/pallas_call | solution.py:315
  7.2 0.0 collective-permute-done
  7.3 1.3 %collective-permute-start.1 = (f32[16,512]{1,0:T(8,128)S(1)}, f32[16,512]{1,0:T(8,128)S(1)}, u32[]{:S(2)}, u32[]{:S(2)}) collective-permute-start(f32[16,512]{1,0:T(8,128)S(1)} %pad_maximum_fusion.1), channel_id=1, source_target_pairs={{0,8},{1,9},{2,10},{3,11},{4,12},{5,13},{6,14},{7,15},{8,0},{9,1},... | collective-permute-start | bytes 98312 | tf_op jit(solution)/shard_map/ppermute | solution.py:326
  8.6 0.6 %spread.3.spread_ref = bf16[384,2176]{1,0:T(8,128)(2,1)S(1)} custom-call(s32[1]{0:T(128)} %bitcast.4.me_ref, s32[4,2176]{1,0:T(4,128)S(1)} %get-tuple-element.48.blocks_ref, f32[4,2176]{1,0:T(4,128)S(1)} %get-tuple-element.49.weight_ref), custom_call_target="tpu_custom_call" | custom-call | bytes 3000000 | tf_op jit(solution)/shard_map/spread/pallas_call | solution.py:315
  9.3 0.8 %collective-permute-done.1 = f32[16,512]{1,0:T(8,128)S(1)} collective-permute-done((f32[16,512]{1,0:T(8,128)S(1)}, f32[16,512]{1,0:T(8,128)S(1)}, u32[]{:S(2)}, u32[]{:S(2)}) %collective-permute-start.1) | collective-permute-done | bytes 32800 | tf_op jit(solution)/shard_map/ppermute | solution.py:326
  10.1 2.2 %collective-permute-start.4 = (f32[32,512]{1,0:T(8,128)S(1)}, f32[32,512]{1,0:T(8,128)S(1)}, u32[]{:S(2)}, u32[]{:S(2)}) collective-permute-start(f32[32,512]{1,0:T(8,128)S(1)} %pad_maximum_fusion), channel_id=1, source_target_pairs={{0,6},{1,7},{2,4},{3,5},{4,2},{5,3},{6,0},{7,1},{8,14},{9,15},{10,... | collective-permute-start | bytes 196616 | tf_op jit(solution)/shard_map/ppermute | solution.py:326
  12.2 0.2 collective-permute-start.3
  12.5 0.3 collective-permute-start.2
  12.7 0.0 copy-done
  12.7 0.6 %observed.1.obs_ref = bf16[2,2048,128]{2,1,0:T(8,128)(2,1)S(1)} custom-call(f32[64,2048]{1,0:T(8,128)S(1)} %bitcast.11), custom_call_target="tpu_custom_call" | custom-call | bytes 1200000 | tf_op jit(solution)/shard_map/observed/pallas_call | solution.py:361
  13.4 1.8 %halves.1.x_ref = bf16[8,192,1024]{2,1,0:T(8,128)(2,1)S(1)} custom-call(f32[64,8,1024]{2,1,0:T(8,128)} %x_ref.2), custom_call_target="tpu_custom_call" | custom-call | bytes 4500000 | tf_op jit(solution)/shard_map/halves/pallas_call | solution.py:372
  15.2 0.0 collective-permute-done.4
  15.2 0.2 collective-permute-done.3
  15.4 0.2 collective-permute-done.2
  15.6 4.8 %collective-permute-start.5 = (f32[128,512]{1,0:T(8,128)S(1)}, f32[128,512]{1,0:T(8,128)S(1)}, u32[]{:S(2)}, u32[]{:S(2)}) collective-permute-start(f32[128,512]{1,0:T(8,128)S(1)} %constant_dynamic-update-slice_fusion.gathered_ref), channel_id=1, source_target_pairs={{0,1},{1,0},{2,3},{3,2},{4,5},{5,4},{6,7},{7,6},{8,9},{9,8},{10,11... | collective-permute-start | bytes 786440 | tf_op jit(solution)/shard_map/ppermute | solution.py:326
  20.4 1.5 %partial.1.hx_ref = f32[64,2176]{1,0:T(8,128)S(1)} custom-call(f32[128,512]{1,0:T(8,128)S(1)} %constant_dynamic-update-slice_fusion.gathered_ref, bf16[384,2176]{1,0:T(8,128)(2,1)S(1)} %spread.2.spread_ref, f32[8,2176]{1,0:T(8,128)S(1)} %get-tuple-element.65.resp_ref), custom_call_target="tpu_custom_call" | custom-call | bytes 3600000 | tf_op jit(solution)/shard_map/partial/pallas_call | solution.py:418
  21.9 0.0 collective-permute-done.5.gathered_ref
  21.9 7.3 %update.1 = (f32[64,8,1024]{2,1,0:T(8,128)}, f32[64,64]{1,0:T(8,128)}) custom-call(f32[64,2176]{1,0:T(8,128)S(1)} %partial.1.hx_ref, f32[128,512]{1,0:T(8,128)S(1)} %collective-permute-done.5.gathered_ref, bf16[384,2176]{1,0:T(8,128)(2,1)S(1)} %spread.3.spread_ref, f32[8,2176]{1,0:T(8,128)S(1)} %get-tuple-element.65.resp_ref, ...), custom_call_target="tpu_custom_call" | custom-call | tf_op jit(solution)/shard_map/update/pallas_call | solution.py:429
  (6 shorter events, 0.0 us)
Async XLA Ops:
  0.6 5.5 %copy-start.4 = (s32[2048]{0:T(1024)S(1)}, s32[2048]{0:T(1024)}, u32[]{:S(2)}) copy-start(s32[2048]{0:T(1024)} %param.15) | copy-start | bytes 24580
  0.6 5.5 %copy-start.3 = (f32[2048,4]{0,1:T(4,128)S(1)}, f32[2048,4]{0,1:T(4,128)}, u32[]{:S(2)}) copy-start(f32[2048,4]{0,1:T(4,128)} %param.11) | copy-start | bytes 98308
  0.7 5.5 %copy-start.2 = (s32[2048,4]{0,1:T(4,128)S(1)}, s32[2048,4]{0,1:T(4,128)}, u32[]{:S(2)}) copy-start(s32[2048,4]{0,1:T(4,128)} %param.10) | copy-start | bytes 98308
  0.7 5.5 %copy-start.5 = (f32[2048]{0:T(1024)S(1)}, f32[2048]{0:T(1024)}, u32[]{:S(2)}) copy-start(f32[2048]{0:T(1024)} %param.14) | copy-start | bytes 24580
  0.7 5.5 %copy-start.1 = (f32[2048,8]{0,1:T(8,128)S(1)}, f32[2048,8]{0,1:T(8,128)}, u32[]{:S(2)}) copy-start(f32[2048,8]{0,1:T(8,128)} %param.12) | copy-start | bytes 196612
  2.9 9.8 %copy-start = (f32[2048,64]{0,1:T(8,128)S(1)}, f32[2048,64]{0,1:T(8,128)}, u32[]{:S(2)}) copy-start(f32[2048,64]{0,1:T(8,128)} %param.13) | copy-start | bytes 1572868
  2.9 4.3 %collective-permute-start = (f32[8,512]{1,0:T(8,128)S(1)}, f32[8,512]{1,0:T(8,128)S(1)}, u32[]{:S(2)}, u32[]{:S(2)}) collective-permute-start(f32[8,512]{1,0:T(8,128)S(1)} %means.1), channel_id=1, source_target_pairs={{0,16},{1,17},{2,18},{3,19},{4,20},{5,21},{6,22},{7,23},{8,24},{9,... | collective-permute-start | bytes 49160 | tf_op jit(solution)/shard_map/ppermute | solution.py:326
  7.3 2.8 %collective-permute-start.1 = (f32[16,512]{1,0:T(8,128)S(1)}, f32[16,512]{1,0:T(8,128)S(1)}, u32[]{:S(2)}, u32[]{:S(2)}) collective-permute-start(f32[16,512]{1,0:T(8,128)S(1)} %pad_maximum_fusion.1), channel_id=1, source_target_pairs={{0,8},{1,9},{2,10},{3,11},{4,12},{5,13},{6,14},{7,15},{8,0},{9,1},... | collective-permute-start | bytes 98312 | tf_op jit(solution)/shard_map/ppermute | solution.py:326
  10.1 5.1 %collective-permute-start.4 = (f32[32,512]{1,0:T(8,128)S(1)}, f32[32,512]{1,0:T(8,128)S(1)}, u32[]{:S(2)}, u32[]{:S(2)}) collective-permute-start(f32[32,512]{1,0:T(8,128)S(1)} %pad_maximum_fusion), channel_id=1, source_target_pairs={{0,6},{1,7},{2,4},{3,5},{4,2},{5,3},{6,0},{7,1},{8,14},{9,15},{10,... | collective-permute-start | bytes 196616 | tf_op jit(solution)/shard_map/ppermute | solution.py:326
  12.2 3.1 %collective-permute-start.3 = (f32[32,512]{1,0:T(8,128)S(1)}, f32[32,512]{1,0:T(8,128)S(1)}, u32[]{:S(2)}, u32[]{:S(2)}) collective-permute-start(f32[32,512]{1,0:T(8,128)S(1)} %pad_maximum_fusion), channel_id=1, source_target_pairs={{0,4},{1,5},{2,6},{3,7},{4,0},{5,1},{6,2},{7,3},{8,12},{9,13},{10,... | collective-permute-start | bytes 196616 | tf_op jit(solution)/shard_map/ppermute | solution.py:326
  12.5 3.1 %collective-permute-start.2 = (f32[32,512]{1,0:T(8,128)S(1)}, f32[32,512]{1,0:T(8,128)S(1)}, u32[]{:S(2)}, u32[]{:S(2)}) collective-permute-start(f32[32,512]{1,0:T(8,128)S(1)} %pad_maximum_fusion), channel_id=1, source_target_pairs={{0,2},{1,3},{2,0},{3,1},{4,6},{5,7},{6,4},{7,5},{8,10},{9,11},{10,... | collective-permute-start | bytes 196616 | tf_op jit(solution)/shard_map/ppermute | solution.py:326
  15.6 6.3 %collective-permute-start.5 = (f32[128,512]{1,0:T(8,128)S(1)}, f32[128,512]{1,0:T(8,128)S(1)}, u32[]{:S(2)}, u32[]{:S(2)}) collective-permute-start(f32[128,512]{1,0:T(8,128)S(1)} %constant_dynamic-update-slice_fusion.gathered_ref), channel_id=1, source_target_pairs={{0,1},{1,0},{2,3},{3,2},{4,5},{5,4},{6,7},{7,6},{8,9},{9,8},{10,11... | collective-permute-start | bytes 786440 | tf_op jit(solution)/shard_map/ppermute | solution.py:326
